TPU v7x, 32 devices: a whole 2x2x4 slice. The times are simulated.
32 devices in a mesh: sector: 16 (over z, x, core), radial: 2 (over y).
Axes of the slice: x: 2, y: 2, z: 4, core: 2. Of those that a mesh axis runs over, the one named last changes fastest.
Arguments:
- loads: bfloat16 [32, 1536, 256], P('sector', 'radial'), may hold values from -6 to 6
- state: bfloat16 [32, 1536, 256], P('sector', 'radial'), may hold values from -0.375 to 0.375
- factors: bfloat16 [16, 2, 1536, 1024], P('sector', None, 'radial')
- assign: int32 [16], replicated, may hold values from 0 to 15, each once
- iface: int32 [2, 2, 128], P('radial'), may hold values from 0 to 767, as said below
Outputs:
- sensitivity: float32 [32, 1536], P('sector', 'radial')
Inputs may be any that keep to these rules, and one draw needn't show every extreme that they name: `assign`: each slot holds a different harmonic; the value 0 stands for the slot that holds harmonics 0 and 16, any other value h for harmonic h. `iface`: within one cycle the 256 listed positions are all different.
All inputs are finite; a program needn't handle non-finite values.
Results may differ from a plain program's by a relative error of at most 0.013.
Values may be sent and summed in bfloat16 or wider, within the bound.
No kernel may reach another device: no remote copies, remote signals or barrier semaphores. Data moves between devices by JAX's collectives and lax.ppermute only.
A program may use at most 128 MiB of HBM per device.

v0:
```python
import math

import jax
import jax.numpy as jnp
from jax import lax
from jax.sharding import PartitionSpec as P


def padded(block, sides, width):
    for axis, dim in sides:
        count = lax.axis_size(axis)
        forward = [(i, i + 1) for i in range(count - 1)]
        backward = [(target, source) for source, target in forward]
        low = lax.ppermute(
            lax.slice_in_dim(block, block.shape[dim] - width, None, axis=dim), axis, forward
        )
        high = lax.ppermute(lax.slice_in_dim(block, 0, width, axis=dim), axis, backward)
        block = jnp.concatenate([low, block, high], axis=dim)
    return block


def forward_table(assign, sectors):
    position = jnp.arange(sectors, dtype=jnp.int32)
    phases = assign[:, None] * position[None, :] % sectors
    angles = phases.astype(jnp.float32) * (2.0 * math.pi / sectors)
    paired = (assign == 0)[:, None]
    alternate = (1 - 2 * (position % 2)).astype(jnp.float32)[None, :]
    real_rows = jnp.cos(angles)
    imag_rows = jnp.where(paired, alternate, -jnp.sin(angles))
    stacked = jnp.stack([real_rows, imag_rows], axis=1)
    return stacked.reshape(2 * assign.shape[0], sectors).astype(jnp.bfloat16)


def inverse_table(assign, sectors):
    position = jnp.arange(sectors, dtype=jnp.int32)
    phases = assign[:, None] * position[None, :] % sectors
    angles = phases.astype(jnp.float32) * (2.0 * math.pi / sectors)
    paired = (assign == 0)[:, None]
    alternate = (1 - 2 * (position % 2)).astype(jnp.float32)[None, :]
    real_cols = jnp.where(paired, 1.0, 2.0) * jnp.cos(angles) / sectors
    imag_cols = jnp.where(paired, alternate, -2.0 * jnp.sin(angles)) / sectors
    stacked = jnp.stack([real_cols, imag_cols], axis=1)
    return jnp.transpose(stacked.reshape(2 * assign.shape[0], sectors)).astype(jnp.bfloat16)


def transposed(weight, operand):
    return lax.dot_general(
        weight, operand, (((0,), (0,)), ((), ())), preferred_element_type=jnp.float32
    )


def solve_slot(spectrum, weight_real, weight_imag, paired):
    real_real = jnp.dot(weight_real, spectrum[0], preferred_element_type=jnp.float32)
    imag_imag = jnp.dot(weight_imag, spectrum[1], preferred_element_type=jnp.float32)
    imag_real = jnp.dot(weight_imag, spectrum[0], preferred_element_type=jnp.float32)
    real_imag = jnp.dot(weight_real, spectrum[1], preferred_element_type=jnp.float32)
    middle_real = jnp.where(paired, real_real, real_real - imag_imag)
    middle_imag = jnp.where(paired, imag_imag, imag_real + real_imag)
    middle = jnp.stack([middle_real, middle_imag]).astype(jnp.bfloat16)
    back_real = transposed(weight_real, middle[0])
    back_imag = transposed(weight_imag, middle[1])
    cross_real = transposed(weight_real, middle[1])
    cross_imag = transposed(weight_imag, middle[0])
    final_real = jnp.where(paired, back_real, back_real + back_imag)
    final_imag = jnp.where(paired, back_imag, cross_real - cross_imag)
    return jnp.stack([final_real, final_imag])


def per_device(loads, state, factors, assign, iface):
    inner_face = iface[0, 0]
    outer_face = iface[0, 1]
    face_width = inner_face.shape[0]
    face_rows = jnp.concatenate([loads[:, inner_face, :], loads[:, outer_face, :]], axis=1)
    extended = padded(face_rows, (("radial", 1),), face_width)
    from_below = extended[:, :face_width, :].astype(jnp.float32)
    from_above = extended[:, 3 * face_width :, :].astype(jnp.float32)
    assembled = loads.astype(jnp.float32).at[:, inner_face, :].add(from_below)
    assembled = assembled.at[:, outer_face, :].add(from_above).astype(jnp.bfloat16)
    sectors = 2 * assign.shape[0]
    forward = forward_table(assign, sectors)
    inverse = inverse_table(assign, sectors)
    paired = assign[lax.axis_index("sector")] == 0
    weight_real = factors[0, 0]
    weight_imag = factors[0, 1]
    cycle_width = weight_real.shape[0]
    pieces = lax.all_to_all(assembled, "sector", split_axis=2, concat_axis=0, tiled=True)
    flat = pieces.reshape(pieces.shape[0], -1)
    product = jnp.dot(forward, flat, preferred_element_type=jnp.float32)
    spectrum = product.astype(jnp.bfloat16).reshape(pieces.shape)
    harmonic = lax.all_to_all(spectrum, "sector", split_axis=0, concat_axis=2, tiled=True)
    spectrum_rims = jnp.concatenate(
        [harmonic[:, outer_face, :], harmonic[:, inner_face, :]], axis=1
    )
    rimmed = padded(spectrum_rims, (("radial", 1),), face_width)
    below_rows = rimmed[:, :face_width, :]
    above_rows = rimmed[:, 3 * face_width :, :]
    widened = jnp.concatenate([harmonic, above_rows, below_rows], axis=1)
    back = solve_slot(widened, weight_real, weight_imag, paired)
    to_upper = back[:, cycle_width : cycle_width + face_width, :]
    to_lower = back[:, cycle_width + face_width :, :]
    outgoing = jnp.concatenate([to_lower, to_upper], axis=1)
    returned = padded(outgoing.astype(jnp.bfloat16), (("radial", 1),), face_width).astype(
        outgoing.dtype
    )
    got_lower = returned[:, :face_width, :]
    got_upper = returned[:, 3 * face_width :, :]
    total = back[:, :cycle_width, :].at[:, outer_face, :].add(got_lower)
    solved = total.at[:, inner_face, :].add(got_upper).astype(jnp.bfloat16)
    pieces = lax.all_to_all(solved, "sector", split_axis=2, concat_axis=0, tiled=True)
    flat = pieces.reshape(pieces.shape[0], -1)
    product = jnp.dot(inverse, flat, preferred_element_type=jnp.float32)
    physical = product.astype(jnp.bfloat16).reshape(pieces.shape)
    adjoint = lax.all_to_all(physical, "sector", split_axis=0, concat_axis=2, tiled=True)
    return jnp.einsum("sdr,sdr->sd", adjoint, state, preferred_element_type=jnp.float32)


def solution(mesh):
    return jax.shard_map(
        per_device,
        mesh=mesh,
        in_specs=(
            P("sector", "radial", None),
            P("sector", "radial", None),
            P("sector", None, "radial", None),
            P(),
            P("radial", None, None),
        ),
        out_specs=P("sector", "radial"),
        check_vma=False,
    )
```

profile of v0, /device:TPU:0, one launch (start us, length us, event | category | flops | bytes accessed | tf_op | source)
XLA Modules:
  0.0 228.6 jit_solution(15137418273525457393)
XLA Ops:
  0.8 2.4 %gather_fusion = bf16[128,2,256]{2,0,1:T(8,128)(2,1)S(1)} fusion(bf16[2,768,256]{2,1,0:T(8,128)(2,1)} %param.5, s32[1024]{0:T(1024)S(1)} %get-tuple-element.17), kind=kCustom, calls=%fused_computation | custom fusion | bytes 262656 | tf_op jit(solution)/shard_map/gather | solution.py:73
  3.2 4.9 %collective-permute-start = (bf16[2,128,256]{2,1,0:T(8,128)(2,1)S(1)}, bf16[2,128,256]{2,1,0:T(8,128)(2,1)S(1)}, u32[]{:S(2)}, u32[]{:S(2)}) collective-permute-start(bf16[2,128,256]{2,1,0:T(8,128)(2,1)S(1)} %bitcast.151), channel_id=1, source_target_pairs={{0,1},{2,3},{4,5},{6,7},{8,9},{10,11},{12,13},{14,15},{16,17},{18,... | collective-permute-start | bytes 393224 | tf_op jit(solution)/shard_map/ppermute | solution.py:14
  11.5 4.5 %collective-permute-done.1 = bf16[2,128,256]{2,1,0:T(8,128)(2,1)S(1)} collective-permute-done((bf16[2,128,256]{2,1,0:T(8,128)(2,1)S(1)}, bf16[2,128,256]{2,1,0:T(8,128)(2,1)S(1)}, u32[]{:S(2)}, u32[]{:S(2)}) %collective-permute-start.1) | collective-permute-done | bytes 131104 | tf_op jit(solution)/shard_map/ppermute | solution.py:17
  16.2 5.2 %scatter_fusion = f32[2,768,256]{2,0,1:T(2,128)S(1)} fusion(f32[2,768,256]{2,0,1:T(2,128)S(1)} %copy.94, s32[128]{0:T(128)S(1)} %get-tuple-element.10, f32[128,2,256]{2,1,0:T(2,128)S(1)} %copy.95), kind=kCustom, calls=%fused_computation.4 | custom fusion | flops 65536 | bytes 786944 | tf_op jit(solution)/shard_map/scatter-add | solution.py:77
  21.4 5.2 %scatter_fusion.1 = f32[2,768,256]{2,0,1:T(2,128)S(1)} fusion(f32[2,768,256]{2,0,1:T(2,128)S(1)} %scatter_fusion, s32[128]{0:T(128)S(1)} %get-tuple-element.9, f32[128,2,256]{2,1,0:T(2,128)S(1)} %copy.96), kind=kCustom, calls=%fused_computation.5 | custom fusion | flops 65536 | bytes 786944 | tf_op jit(solution)/shard_map/scatter-add | solution.py:78
  27.1 2.3 %copy.97 = bf16[2,768,256]{1,0,2:T(2,128)(2,1)} copy(bf16[2,768,256]{2,0,1:T(2,128)(2,1)S(1)} %convert_element_type.81) | data formatting | bytes 1572864 | tf_op jit(solution)/shard_map/convert_element_type | solution.py:78
  29.5 5.9 %all-to-all-start = ((bf16[2,768,256]{1,0,2:T(2,128)(2,1)}), bf16[2,768,256]{1,0,2:T(2,128)(2,1)S(1)}, u32[]{:S(2)}, u32[]{:S(2)}) async-start(bf16[2,768,256]{1,0,2:T(2,128)(2,1)} %copy.97), calls=%async_computation | async-start | bytes 1572864 | tf_op jit(solution)/shard_map/all_to_all | solution.py:86
  36.2 17.9 %all-to-all-done = bf16[2,768,256]{1,0,2:T(2,128)(2,1)S(1)} async-done(((bf16[2,768,256]{1,0,2:T(2,128)(2,1)}), bf16[2,768,256]{1,0,2:T(2,128)(2,1)S(1)}, u32[]{:S(2)}, u32[]{:S(2)}) %all-to-all-start) | async-done | bytes 786464 | tf_op jit(solution)/shard_map/all_to_all | solution.py:86
  54.2 4.5 %copy.99 = bf16[16,2,768,16]{3,2,1,0:T(8,128)(2,1)} copy(bf16[16,2,768,16]{2,3,0,1:T(8,128)(2,1)S(1)} %bitcast.146) | data formatting | bytes 1572864 | tf_op jit(solution)/shard_map/all_to_all | solution.py:86
  58.7 12.3 %reshape.335 = bf16[32,12288]{1,0:T(8,128)(2,1)S(1)} reshape(bf16[16,2,768,16]{3,2,1,0:T(8,128)(2,1)} %copy.99) | data formatting | bytes 1572864 | tf_op jit(solution)/shard_map/reshape | solution.py:87
  72.3 2.9 %copy.100 = bf16[32,12288]{0,1:T(8,128)(2,1)S(1)} copy(bf16[32,12288]{1,0:T(8,128)(2,1)} %convolution_convert_fusion.1) | data formatting | bytes 1572864 | tf_op jit(solution)/shard_map/convert_element_type | solution.py:89
  75.1 3.9 %copy.101 = bf16[32,768,16]{1,2,0:T(8,128)(2,1)} copy(bf16[32,768,16]{0,2,1:T(8,128)(2,1)S(1)} %bitcast.142) | data formatting | bytes 1572864 | tf_op jit(solution)/shard_map/reshape | solution.py:89
  79.1 25.7 %all_to_all.66 = bf16[32,768,16]{1,2,0:T(8,128)(2,1)S(1)} all-to-all(bf16[32,768,16]{1,2,0:T(8,128)(2,1)} %copy.101), channel_id=1, replica_groups=mesh['sector'=16,'radial'=2] {'sector'}, dimensions={0} | all-to-all | bytes 1572864 | tf_op jit(solution)/shard_map/all_to_all | solution.py:90
  113.0 5.2 %collective-permute-start.3 = (bf16[2,128,256]{2,0,1:T(2,128)(2,1)S(1)}, bf16[2,128,256]{2,0,1:T(2,128)(2,1)S(1)}, u32[]{:S(2)}, u32[]{:S(2)}) collective-permute-start(bf16[2,128,256]{2,0,1:T(2,128)(2,1)S(1)} %bitcast.152), channel_id=1, source_target_pairs={{0,1},{2,3},{4,5},{6,7},{8,9},{10,11},{12,13},{14,15},{16,17},{18,... | collective-permute-start | bytes 393224 | tf_op jit(solution)/shard_map/ppermute | solution.py:14
  128.2 4.4 %collective-permute-start.4 = (bf16[2,128,256]{1,2,0:T(8,128)(2,1)S(1)}, bf16[2,128,256]{1,2,0:T(8,128)(2,1)S(1)}, u32[]{:S(2)}, u32[]{:S(2)}) collective-permute-start(bf16[2,128,256]{1,2,0:T(8,128)(2,1)S(1)} %get-tuple-element.5), channel_id=1, source_target_pairs={{0,1},{2,3},{4,5},{6,7},{8,9},{10,11},{12,13},{14,15},{16,17},{18,... | collective-permute-start | bytes 393224 | tf_op jit(solution)/shard_map/ppermute | solution.py:14
  135.3 4.4 %collective-permute-done.5 = bf16[2,128,256]{1,2,0:T(8,128)(2,1)} collective-permute-done((bf16[2,128,256]{1,2,0:T(8,128)(2,1)S(1)}, bf16[2,128,256]{1,2,0:T(8,128)(2,1)}, u32[]{:S(2)}, u32[]{:S(2)}) %collective-permute-start.5) | collective-permute-done | bytes 131104 | tf_op jit(solution)/shard_map/ppermute | solution.py:17
  140.9 5.2 %scatter_fusion.2 = f32[2,768,256]{2,0,1:T(2,128)S(1)} fusion(f32[2,768,256]{2,0,1:T(2,128)S(1)} %copy.107, s32[128]{0:T(128)S(1)} %get-tuple-element.9, f32[128,2,256]{2,1,0:T(2,128)S(1)} %copy.108), kind=kCustom, calls=%fused_computation.6 | custom fusion | flops 65536 | bytes 786944 | tf_op jit(solution)/shard_map/scatter-add | solution.py:107
  146.0 5.2 %scatter_fusion.3 = f32[2,768,256]{2,0,1:T(2,128)S(1)} fusion(f32[2,768,256]{2,0,1:T(2,128)S(1)} %scatter_fusion.2, s32[128]{0:T(128)S(1)} %get-tuple-element.10, f32[128,2,256]{2,1,0:T(2,128)S(1)} %copy.109), kind=kCustom, calls=%fused_computation.7 | custom fusion | flops 65536 | bytes 786944 | tf_op jit(solution)/shard_map/scatter-add | solution.py:108
  153.2 23.5 %all_to_all.67 = bf16[2,768,256]{1,0,2:T(2,128)(2,1)S(1)} all-to-all(bf16[2,768,256]{1,0,2:T(2,128)(2,1)S(1)} %copy.110), channel_id=1, replica_groups=mesh['sector'=16,'radial'=2] {'sector'}, dimensions={2} | all-to-all | bytes 1572864 | tf_op jit(solution)/shard_map/all_to_all | solution.py:109
  176.8 4.5 %copy.112 = bf16[16,2,768,16]{3,2,1,0:T(8,128)(2,1)} copy(bf16[16,2,768,16]{2,3,0,1:T(8,128)(2,1)S(1)} %bitcast.147) | data formatting | bytes 1572864 | tf_op jit(solution)/shard_map/all_to_all | solution.py:109
  181.3 12.3 %reshape.337 = bf16[32,12288]{1,0:T(8,128)(2,1)S(1)} reshape(bf16[16,2,768,16]{3,2,1,0:T(8,128)(2,1)} %copy.112) | data formatting | bytes 1572864 | tf_op jit(solution)/shard_map/reshape | solution.py:110
  194.9 2.9 %copy.113 = bf16[32,12288]{0,1:T(8,128)(2,1)S(1)} copy(bf16[32,12288]{1,0:T(8,128)(2,1)} %convolution_convert_fusion) | data formatting | bytes 1572864 | tf_op jit(solution)/shard_map/convert_element_type | solution.py:112
  197.8 3.9 %copy.114 = bf16[32,768,16]{1,2,0:T(8,128)(2,1)} copy(bf16[32,768,16]{0,2,1:T(8,128)(2,1)S(1)} %bitcast.143) | data formatting | bytes 1572864 | tf_op jit(solution)/shard_map/reshape | solution.py:112
  201.7 24.2 %all_to_all.68 = bf16[32,768,16]{1,2,0:T(8,128)(2,1)S(1)} all-to-all(bf16[32,768,16]{1,2,0:T(8,128)(2,1)} %copy.114), channel_id=1, replica_groups=mesh['sector'=16,'radial'=2] {'sector'}, dimensions={0} | all-to-all | bytes 1572864 | tf_op jit(solution)/shard_map/all_to_all | solution.py:113
  (63 shorter events, 34.3 us)
Async XLA Ops:
  0.0 8.0 %copy-start.1 = (bf16[2,768,256]{2,1,0:T(8,128)(2,1)S(1)}, bf16[2,768,256]{2,1,0:T(8,128)(2,1)}, u32[]{:S(2)}) copy-start(bf16[2,768,256]{2,1,0:T(8,128)(2,1)} %param.5) | copy-start | bytes 2359300
  3.2 8.1 %collective-permute-start = (bf16[2,128,256]{2,1,0:T(8,128)(2,1)S(1)}, bf16[2,128,256]{2,1,0:T(8,128)(2,1)S(1)}, u32[]{:S(2)}, u32[]{:S(2)}) collective-permute-start(bf16[2,128,256]{2,1,0:T(8,128)(2,1)S(1)} %bitcast.151), channel_id=1, source_target_pairs={{0,1},{2,3},{4,5},{6,7},{8,9},{10,11},{12,13},{14,15},{16,17},{18,... | collective-permute-start | bytes 393224 | tf_op jit(solution)/shard_map/ppermute | solution.py:14
  9.1 6.9 %collective-permute-start.1 = (bf16[2,128,256]{2,1,0:T(8,128)(2,1)S(1)}, bf16[2,128,256]{2,1,0:T(8,128)(2,1)S(1)}, u32[]{:S(2)}, u32[]{:S(2)}) collective-permute-start(bf16[2,128,256]{2,1,0:T(8,128)(2,1)S(1)} %bitcast.150), channel_id=1, source_target_pairs={{1,0},{3,2},{5,4},{7,6},{9,8},{11,10},{13,12},{15,14},{17,16},{19,... | collective-permute-start | bytes 393224 | tf_op jit(solution)/shard_map/ppermute | solution.py:17
  27.1 8.3 %copy-start.3 = (s32[16]{0:T(128)S(1)}, s32[16]{0:T(128)}, u32[]{:S(2)}) copy-start(s32[16]{0:T(128)} %param.8) | copy-start | bytes 196
  29.5 24.6 %all-to-all-start = ((bf16[2,768,256]{1,0,2:T(2,128)(2,1)}), bf16[2,768,256]{1,0,2:T(2,128)(2,1)S(1)}, u32[]{:S(2)}, u32[]{:S(2)}) async-start(bf16[2,768,256]{1,0,2:T(2,128)(2,1)} %copy.97), calls=%async_computation | async-start | bytes 1572864 | tf_op jit(solution)/shard_map/all_to_all | solution.py:86
  104.9 0.9 copy-start.2
  107.6 15.5 %copy-start = (bf16[1,2,768,1024]{3,2,1,0:T(8,128)(2,1)S(1)}, bf16[1,2,768,1024]{3,2,1,0:T(8,128)(2,1)}, u32[]{:S(2)}) copy-start(bf16[1,2,768,1024]{3,2,1,0:T(8,128)(2,1)} %param.7) | copy-start | bytes 9437188
  111.7 8.4 %collective-permute-start.2 = (bf16[2,128,256]{2,0,1:T(2,128)(2,1)S(1)}, bf16[2,128,256]{2,0,1:T(2,128)(2,1)}, u32[]{:S(2)}, u32[]{:S(2)}) collective-permute-start(bf16[2,128,256]{2,0,1:T(2,128)(2,1)S(1)} %bitcast.153), channel_id=1, source_target_pairs={{1,0},{3,2},{5,4},{7,6},{9,8},{11,10},{13,12},{15,14},{17,16},{19,... | collective-permute-start | bytes 393224 | tf_op jit(solution)/shard_map/ppermute | solution.py:17
  113.0 8.6 %collective-permute-start.3 = (bf16[2,128,256]{2,0,1:T(2,128)(2,1)S(1)}, bf16[2,128,256]{2,0,1:T(2,128)(2,1)S(1)}, u32[]{:S(2)}, u32[]{:S(2)}) collective-permute-start(bf16[2,128,256]{2,0,1:T(2,128)(2,1)S(1)} %bitcast.152), channel_id=1, source_target_pairs={{0,1},{2,3},{4,5},{6,7},{8,9},{10,11},{12,13},{14,15},{16,17},{18,... | collective-permute-start | bytes 393224 | tf_op jit(solution)/shard_map/ppermute | solution.py:14
  128.2 7.0 %collective-permute-start.4 = (bf16[2,128,256]{1,2,0:T(8,128)(2,1)S(1)}, bf16[2,128,256]{1,2,0:T(8,128)(2,1)S(1)}, u32[]{:S(2)}, u32[]{:S(2)}) collective-permute-start(bf16[2,128,256]{1,2,0:T(8,128)(2,1)S(1)} %get-tuple-element.5), channel_id=1, source_target_pairs={{0,1},{2,3},{4,5},{6,7},{8,9},{10,11},{12,13},{14,15},{16,17},{18,... | collective-permute-start | bytes 393224 | tf_op jit(solution)/shard_map/ppermute | solution.py:14
  132.7 7.0 %collective-permute-start.5 = (bf16[2,128,256]{1,2,0:T(8,128)(2,1)S(1)}, bf16[2,128,256]{1,2,0:T(8,128)(2,1)}, u32[]{:S(2)}, u32[]{:S(2)}) collective-permute-start(bf16[2,128,256]{1,2,0:T(8,128)(2,1)S(1)} %get-tuple-element.6), channel_id=1, source_target_pairs={{1,0},{3,2},{5,4},{7,6},{9,8},{11,10},{13,12},{15,14},{17,16},{19,... | collective-permute-start | bytes 393224 | tf_op jit(solution)/shard_map/ppermute | solution.py:17
where the time goes:
time: 230 us; the launch traced here: 229 us
  blocking collectives  73.4 us (32%)
  local copies, waits for them, and re-layouts  66.9 us (29%)
  other arithmetic  27.9 us (12%)
  waiting for transfers between devices  27.5 us (12%)
  starting transfers between devices  24.3 us (11%)
  matrix products  7.43 us (3%)
    all_to_all x1, blocking collectives, per_device(): lax.all_to_all(spectrum, 'sector', split_axis=0, concat_axis=2, tiled=True)  25.7 us
    reshape x2, local copies, waits for them, and re-layouts, per_device(): flat = pieces.reshape(pieces.shape[0], -1)  24.7 us
    all_to_all x1, blocking collectives, per_device(): lax.all_to_all(physical, 'sector', split_axis=0, concat_axis=2, tiled=True)  24.2 us
    all_to_all x1, blocking collectives, per_device(): lax.all_to_all(solved, 'sector', split_axis=2, concat_axis=0, tiled=True)  23.5 us
    all_to_all x1, waiting for transfers between devices, per_device(): lax.all_to_all(assembled, 'sector', split_axis=2, concat_axis=0, tiled=True)  17.9 us
    ppermute x3, starting transfers between devices, padded(): lax.ppermute(lax.slice_in_dim(block, block.shape[dim] - width, None, axis...  14.5 us
    ppermute x3, waiting for transfers between devices, padded(): lax.ppermute(lax.slice_in_dim(block, 0, width, axis=dim), axis, backward)  8.86 us
    all_to_all x1, starting transfers between devices, per_device(): lax.all_to_all(assembled, 'sector', split_axis=2, concat_axis=0, tiled=True)  5.91 us
  transfers between devices with their start and end apart: 7, of which 5 were waited for; matrix products, arithmetic and copies ran while one was open for 3% of the time, Pallas kernels for 0%

commit v1 on v0

v1 whole, which is shorter than its diff:
```python
import math

import jax
import jax.numpy as jnp
from jax import lax
from jax.experimental import pallas as pl
from jax.experimental.pallas import tpu as pltpu
from jax.sharding import PartitionSpec as P

F32 = jnp.float32
BF16 = jnp.bfloat16
VMEM = pl.BlockSpec(memory_space=pltpu.VMEM)
SMEM = pl.BlockSpec(memory_space=pltpu.SMEM)
PARAMS = pltpu.CompilerParams(vmem_limit_bytes=48 * 1024 * 1024)
TILE = 16


def tables(assign, sectors):
    position = jnp.arange(sectors, dtype=jnp.int32)
    phases = assign[:, None] * position[None, :] % sectors
    angles = phases.astype(F32) * (2.0 * math.pi / sectors)
    paired = (assign == 0)[:, None]
    alternate = (1 - 2 * (position % 2)).astype(F32)[None, :]
    cos, sin = jnp.cos(angles), jnp.sin(angles)
    forward = jnp.stack([cos, jnp.where(paired, alternate, -sin)], axis=1)
    inverse = jnp.stack(
        [jnp.where(paired, 1.0, 2.0) * cos / sectors, jnp.where(paired, alternate, -2.0 * sin) / sectors],
        axis=1,
    )
    forward = forward.reshape(2 * assign.shape[0], sectors).astype(BF16)
    inverse = jnp.transpose(inverse.reshape(2 * assign.shape[0], sectors)).astype(BF16)
    return forward, inverse


def widen(table):
    eye = jnp.eye(TILE, dtype=BF16)
    side = table.shape[0] * TILE
    return (table[:, None, :, None] * eye[None, :, None, :]).reshape(side, side)


def dot(a, b):
    return jnp.dot(a, b, preferred_element_type=F32)


def transform_kernel(table_ref, x_ref, out_ref):
    count, rows, width = x_ref.shape
    for start in range(0, rows, TILE):
        tile = x_ref[:, start : start + TILE, :].reshape(count * TILE, width)
        out_ref[:, start : start + TILE, :] = (
            dot(table_ref[...], tile).astype(BF16).reshape(count, TILE, width)
        )


def transform(forward, pieces):
    rows = pieces.shape[1]
    if rows % TILE:
        return jnp.einsum("ks,sdr->kdr", forward, pieces, preferred_element_type=F32).astype(BF16)
    return pl.pallas_call(
        transform_kernel,
        out_shape=jax.ShapeDtypeStruct(pieces.shape, BF16),
        in_specs=[VMEM, VMEM],
        out_specs=VMEM,
        compiler_params=PARAMS,
        name="transform",
    )(widen(forward), pieces)


def respond_kernel(table_ref, x_ref, state_ref, out_ref):
    count, rows, width = x_ref.shape
    ones = jnp.ones((8, width), BF16)
    for index, start in enumerate(range(0, rows, TILE)):
        tile = x_ref[:, start : start + TILE, :].reshape(count * TILE, width)
        adjoint = dot(table_ref[...], tile).astype(BF16).astype(F32)
        state = state_ref[:, start : start + TILE, :].reshape(count * TILE, width).astype(F32)
        product = adjoint * state
        high = product.astype(BF16)
        low = (product - high.astype(F32)).astype(BF16)
        contract = (((1,), (1,)), ((), ()))
        total = lax.dot_general(ones, high, contract, preferred_element_type=F32)
        total = total + lax.dot_general(ones, low, contract, preferred_element_type=F32)
        out_ref[index : index + 1, :] = total[:1]


def respond(inverse, pieces, state):
    count, rows, _ = pieces.shape
    if rows % TILE:
        adjoint = jnp.einsum("sk,kdr->sdr", inverse, pieces, preferred_element_type=F32).astype(BF16)
        return jnp.sum(adjoint.astype(F32) * state.astype(F32), axis=-1)
    sums = pl.pallas_call(
        respond_kernel,
        out_shape=jax.ShapeDtypeStruct((rows // TILE, count * TILE), F32),
        in_specs=[VMEM, VMEM, VMEM],
        out_specs=VMEM,
        compiler_params=PARAMS,
        name="respond",
    )(widen(inverse), pieces, state)
    return sums.reshape(rows // TILE, count, TILE).transpose(1, 0, 2).reshape(count, rows)


def rows_of(x_ref, part):
    chunks, _, rows, width = x_ref.shape
    return x_ref[:, part].reshape(chunks * rows, width)


def faces_kernel(index_ref, x_ref, out_ref):
    count = index_ref.shape[0]
    cycle = x_ref.shape[0] * x_ref.shape[2]
    pick = index_ref[...] == lax.broadcasted_iota(jnp.int32, (count, cycle), 1)
    pick = jnp.where(pick, 1.0, 0.0).astype(BF16)
    for part in range(2):
        out_ref[part] = dot(pick, rows_of(x_ref, part)).astype(BF16)


def prepare_kernel(index_ref, weight_ref, out_ref):
    cycle = weight_ref.shape[1]
    count = index_ref.shape[1]
    pick = lax.broadcasted_iota(jnp.int32, (cycle, count), 0) == index_ref[...]
    pick = jnp.where(pick, 1.0, 0.0).astype(BF16)
    for part in range(2):
        out_ref[part] = dot(weight_ref[part, :, :cycle], pick).astype(BF16)


def right_sides(real, imag, paired):
    zero = jnp.zeros_like(imag)
    turned = jnp.where(paired, zero, imag)
    upper = jnp.concatenate([real, turned], axis=1)
    lower = jnp.concatenate([-turned, jnp.where(paired, imag, real)], axis=1)
    return upper, lower


def own_kernel(paired_ref, weight_ref, x_ref, out_ref):
    cycle = weight_ref.shape[1]
    upper, lower = right_sides(rows_of(x_ref, 0), rows_of(x_ref, 1), paired_ref[0] != 0)
    out_ref[...] = dot(weight_ref[0, :, :cycle], upper) + dot(weight_ref[1, :, :cycle], lower)


def back_sides(real, imag, paired):
    zero = jnp.zeros_like(imag)
    turned = jnp.where(paired, zero, imag)
    upper = jnp.concatenate([real, turned], axis=1)
    lower = jnp.concatenate([turned, jnp.where(paired, imag, -real)], axis=1)
    return upper, lower


def middle_kernel(paired_ref, own_ref, edge_ref, back_ref, near_ref, middle_ref, out_ref):
    paired = paired_ref[0] != 0
    width = near_ref.shape[2]
    upper, lower = right_sides(near_ref[0], near_ref[1], paired)
    middle = own_ref[...] + dot(edge_ref[0], upper) + dot(edge_ref[1], lower)
    middle = middle.astype(BF16)
    middle_ref[...] = middle
    upper, lower = back_sides(middle[:, :width], middle[:, width:], paired)
    out_ref[...] = (dot(back_ref[0], upper) + dot(back_ref[1], lower)).astype(BF16)


def back_kernel(paired_ref, turned_ref, middle_ref, out_ref):
    paired = paired_ref[0] != 0
    cycle = middle_ref.shape[0]
    width = middle_ref.shape[1] // 2
    upper, lower = back_sides(middle_ref[:, :width], middle_ref[:, width:], paired)
    out_ref[...] = dot(turned_ref[0, :cycle], upper) + dot(turned_ref[1, :cycle], lower)


def finish_kernel(index_ref, back_ref, got_ref, out_ref):
    chunks, _, rows, width = out_ref.shape
    cycle = back_ref.shape[0]
    count = index_ref.shape[1]
    pick = lax.broadcasted_iota(jnp.int32, (cycle, count), 0) == index_ref[...]
    pick = jnp.where(pick, 1.0, 0.0).astype(BF16)
    total = (back_ref[...] + dot(pick, got_ref[...])).astype(BF16)
    for part in range(2):
        out_ref[:, part] = total[:, part * width : (part + 1) * width].reshape(chunks, rows, width)


def call(kernel, outs, specs, name, *operands):
    return pl.pallas_call(
        kernel,
        out_shape=outs,
        in_specs=specs,
        out_specs=jax.tree.map(lambda _: VMEM, outs),
        compiler_params=PARAMS,
        name=name,
    )(*operands)


def per_device(loads, state, factors, assign, iface):
    local, cycle, width = loads.shape
    inner, outer = iface[0, 0], iface[0, 1]
    face = inner.shape[0]
    devices = lax.axis_size("sector")
    cycles = lax.axis_size("radial")
    here = lax.axis_index("radial")
    sectors = local * devices
    rows = cycle // devices
    aligned = rows % TILE == 0
    weight = factors[0]
    forward, inverse = tables(assign, sectors)
    paired = (assign[lax.axis_index("sector")] == 0).astype(jnp.int32).reshape(1)
    shape = jax.ShapeDtypeStruct

    def exchange(pieces):
        return lax.all_to_all(pieces, "sector", split_axis=0, concat_axis=0, tiled=True)

    def by_chunk(block):
        return block.reshape(local, devices, rows, width).transpose(1, 0, 2, 3)

    def step(block, shift):
        pairs = [(i, i + shift) for i in range(cycles) if 0 <= i + shift < cycles]
        return lax.ppermute(block, "radial", pairs)

    above = weight[:, :, cycle : cycle + face]
    below = weight[:, :, cycle + face :]
    if cycles == 2:
        low = here == 0
        toward = jnp.where(low, outer, inner)
        away = jnp.where(low, inner, outer)
        sent = jnp.concatenate([toward, away])
        gathered = toward
        scattered = away
        outward = jnp.where(low, above, below)
    else:
        sent = jnp.concatenate([inner, outer])
        gathered = jnp.concatenate([inner, outer])
        scattered = jnp.concatenate([outer, inner])
        outward = jnp.concatenate([above, below], axis=2)

    gains = call(
        prepare_kernel, shape((2, cycle, gathered.shape[0]), BF16), [VMEM, VMEM], "prepare",
        gathered.reshape(1, -1), weight,
    )
    edge = jnp.concatenate([gains, outward], axis=2)
    turned = jnp.swapaxes(weight, 1, 2)
    outward_turned = jnp.swapaxes(outward, 1, 2)

    pieces = exchange(by_chunk(loads)).reshape(sectors, rows, width)
    spectrum = transform(forward, pieces)
    harmonic = exchange(spectrum.reshape(devices, 2, rows, width))

    harmonic, state = lax.optimization_barrier((harmonic, state))
    state = exchange(by_chunk(state)).reshape(sectors, rows, width)

    if not aligned:
        harmonic = harmonic.transpose(1, 0, 2, 3).reshape(1, 2, cycle, width)
    faces = call(
        faces_kernel, shape((2, 2 * face, width), BF16), [VMEM, VMEM], "faces",
        sent.reshape(-1, 1), harmonic,
    )
    own = call(
        own_kernel, shape((cycle, 2 * width), F32), [SMEM, VMEM, VMEM], "own", paired, weight, harmonic
    )
    if cycles == 2:
        near = lax.ppermute(faces, "radial", [(0, 1), (1, 0)])
    else:
        lower = step(faces, 1)
        upper = step(faces, -1)
        beyond_above = step(faces[:, :face], -2)
        beyond_below = step(faces[:, face:], 2)
        far_above = (upper[:, face:].astype(F32) + beyond_above.astype(F32)).astype(BF16)
        far_below = (lower[:, :face].astype(F32) + beyond_below.astype(F32)).astype(BF16)
        near = jnp.concatenate([lower[:, face:], upper[:, :face], far_above, far_below], axis=1)
    middle, leaving = call(
        middle_kernel,
        (shape((cycle, 2 * width), BF16), shape((outward.shape[2], 2 * width), BF16)),
        [SMEM, VMEM, VMEM, VMEM, VMEM], "middle",
        paired, own, edge, outward_turned, near,
    )
    if cycles == 2:
        got = lax.ppermute(leaving, "radial", [(0, 1), (1, 0)])
    else:
        got = jnp.concatenate([step(leaving[:face], 1), step(leaving[face:], -1)], axis=0)
    back = call(
        back_kernel, shape((cycle, 2 * width), F32), [SMEM, VMEM, VMEM], "back", paired, turned, middle
    )
    solved = call(
        finish_kernel, shape((devices, 2, rows, width) if aligned else (1, 2, cycle, width), BF16),
        [VMEM, VMEM, VMEM], "finish", scattered.reshape(1, -1), back, got,
    )
    if not aligned:
        solved = solved.reshape(2, devices, rows, width).transpose(1, 0, 2, 3)
    pieces = exchange(solved).reshape(sectors, rows, width)
    found = respond(inverse, pieces, state).reshape(devices, local, rows)
    return exchange(found).transpose(1, 0, 2).reshape(local, cycle)


def solution(mesh):
    return jax.shard_map(
        per_device,
        mesh=mesh,
        in_specs=(
            P("sector", "radial", None),
            P("sector", "radial", None),
            P("sector", None, "radial", None),
            P(),
            P("radial", None, None),
        ),
        out_specs=P("sector", "radial"),
        check_vma=False,
    )
```

time: 230 us -> 131 us (0.57)
  blocking collectives: 73.4 us -> 37.6 us
  local copies, waits for them, and re-layouts: 66.9 us -> 33.7 us
  other arithmetic: 27.9 us -> 8.74 us
  Pallas kernels: 0 us -> 9.68 us
  matrix products: 7.43 us -> 0 us
  waiting for transfers between devices: 27.5 us -> 20.5 us
  starting transfers between devices: 24.3 us -> 19.2 us
    all_to_all x3 -> x2, blocking collectives: 73.4 us -> 37.6 us  [exchange(): lax.all_to_all(pieces, 'sector', split_axis=0, concat_axis=0, tiled=True)]
    reshape x4 -> x5, local copies, waits for them, and re-layouts: 32.5 us -> 5.29 us  [the longest x2 4.35 us: by_chunk(): return block.reshape(local, devices, rows, width).transpose(1, 0, 2, 3)]
    scatter-add x4 -> x0, other arithmetic: 20.6 us -> none  [the longest x1 5.16 us: per_device(): assembled = loads.astype(jnp.float32).at[:, inner_face, :].add(from_below)]
    ppermute x6 -> x2, starting transfers between devices: 18.4 us -> 2.12 us  [the longest x1 1.52 us: per_device(): near = lax.ppermute(faces, 'radial', [(0, 1), (1, 0)])]
    mul x0 -> x2, local copies, waits for them, and re-layouts: none -> 16.2 us  [widen(): return (table[:, None, :, None] * eye[None, :, None, :]).reshape(side, side)]
    all_to_all x1 -> x3, starting transfers between devices: 5.91 us -> 17 us  [exchange(): lax.all_to_all(pieces, 'sector', split_axis=0, concat_axis=0, tiled=True)]
    all_to_all x7 -> x0, local copies, waits for them, and re-layouts: 11.1 us -> none  [the longest x2 4.59 us: per_device(): lax.all_to_all(assembled, 'sector', split_axis=2, concat_axis=0, tiled=True)]
    convert_element_type x7 -> x1, local copies, waits for them, and re-layouts: 10.7 us -> 0.08 us  [tables(): jnp.transpose(inverse.reshape(2 * assign.shape[0], sectors)).astype(BF16)]
  transfers between devices with their start and end apart: 7 -> 5, of which waited for: 5 -> 3; matrix products, arithmetic and copies ran while one was open for 3% -> 24% of each run, Pallas kernels for 0% -> 5%
where the time goes in v1:
time: 131 us; the launch traced here: 130 us
  blocking collectives  37.6 us (29%)
  local copies, waits for them, and re-layouts  33.7 us (26%)
  waiting for transfers between devices  20.5 us (16%)
  starting transfers between devices  19.2 us (15%)
  Pallas kernels  9.68 us (7%)
  other arithmetic  8.74 us (7%)
    all_to_all x2, blocking collectives, exchange(): lax.all_to_all(pieces, 'sector', split_axis=0, concat_axis=0, tiled=True)  37.6 us
    all_to_all x3, starting transfers between devices, exchange(): lax.all_to_all(pieces, 'sector', split_axis=0, concat_axis=0, tiled=True)  17 us
    all_to_all x3, waiting for transfers between devices, exchange(): lax.all_to_all(pieces, 'sector', split_axis=0, concat_axis=0, tiled=True)  16.7 us
    mul x2, local copies, waits for them, and re-layouts, widen(): return (table[:, None, :, None] * eye[None, :, None, :]).reshape(side, side)  16.2 us
    unnamed x21, local copies, waits for them, and re-layouts  8.14 us
    pallas_call x6, Pallas kernels, call(): pl.pallas_call(kernel, out_shape=outs, in_specs=specs, out_specs=jax.tree...  6.78 us
    reshape x2, local copies, waits for them, and re-layouts, by_chunk(): return block.reshape(local, devices, rows, width).transpose(1, 0, 2, 3)  4.35 us
    ppermute x1, waiting for transfers between devices, per_device(): got = lax.ppermute(leaving, 'radial', [(0, 1), (1, 0)])  3.87 us
  transfers between devices with their start and end apart: 5, of which 3 were waited for; matrix products, arithmetic and copies ran while one was open for 24% of the time, Pallas kernels for 5%

profile of v1, /device:TPU:0, one launch (start us, length us, event | category | flops | bytes accessed | tf_op | source)
XLA Modules:
  0.0 130.2 jit_solution(15093411535323102652)
XLA Ops:
  0.0 2.2 %copy.39 = bf16[2,16,48,256]{3,2,0,1:T(8,128)(2,1)} copy(bf16[2,16,48,256]{3,2,1,0:T(8,128)(2,1)} %bitcast.46) | data formatting | bytes 1572864 | tf_op jit(solution)/shard_map/reshape | solution.py:205
  2.2 7.4 %all-to-all-start = ((bf16[16,2,48,256]{3,2,1,0:T(8,128)(2,1)}), bf16[16,2,48,256]{3,2,1,0:T(8,128)(2,1)S(1)}, u32[]{:S(2)}, u32[]{:S(2)}) async-start(bf16[16,2,48,256]{3,2,1,0:T(8,128)(2,1)} %bitcast.32), calls=%async_computation | async-start | bytes 1572864 | tf_op jit(solution)/shard_map/all_to_all | solution.py:202
  10.5 3.6 %broadcast_multiply_fusion = (bf16[32,16,32,16]{3,2,1,0:T(8,128)(2,1)}, bf16[32,16,32,16]{3,2,1,0:T(8,128)(2,1)}) fusion(bf16[32,32]{1,0:T(8,128)(2,1)S(1)} %bitcast.51, bf16[16,16]{1,0:T(8,128)(2,1)S(1)} %fusion.4, bf16[32,32]{1,0:T(8,128)(2,1)S(1)} %copy.24), kind=kLoop, calls=%fused_computation | loop fusion | flops 524288 | bytes 1053184 | tf_op jit(solution)/shard_map/mul | solution.py:38
  14.1 8.4 %mul.145.table_ref = bf16[512,512]{1,0:T(8,128)(2,1)} reshape(bf16[32,16,32,16]{3,2,1,0:T(8,128)(2,1)} %get-tuple-element.13) | data formatting | bytes 1048576 | tf_op jit(solution)/shard_map/mul | solution.py:38
  22.5 5.8 %all-to-all-done = bf16[16,2,48,256]{3,2,1,0:T(8,128)(2,1)S(1)} async-done(((bf16[16,2,48,256]{3,2,1,0:T(8,128)(2,1)}), bf16[16,2,48,256]{3,2,1,0:T(8,128)(2,1)S(1)}, u32[]{:S(2)}, u32[]{:S(2)}) %all-to-all-start) | async-done | bytes 786464 | tf_op jit(solution)/shard_map/all_to_all | solution.py:202
  31.9 25.8 %all_to_all.25.x_ref = bf16[16,2,48,256]{3,2,1,0:T(8,128)(2,1)} all-to-all(bf16[16,2,48,256]{3,2,1,0:T(8,128)(2,1)S(1)} %bitcast.40), channel_id=1, replica_groups=mesh['sector'=16,'radial'=2] {'sector'}, dimensions={0} | all-to-all | bytes 1572864 | tf_op jit(solution)/shard_map/all_to_all | solution.py:202
  57.7 2.2 %copy.38 = bf16[2,16,48,256]{3,2,0,1:T(8,128)(2,1)} copy(bf16[2,16,48,256]{3,2,1,0:T(8,128)(2,1)} %bitcast.47) | data formatting | bytes 1572864 | tf_op jit(solution)/shard_map/reshape | solution.py:205
  59.9 4.3 %all-to-all-start.3 = ((bf16[16,2,48,256]{3,2,1,0:T(8,128)(2,1)}), bf16[16,2,48,256]{3,2,1,0:T(8,128)(2,1)}, u32[]{:S(2)}, u32[]{:S(2)}) async-start(bf16[16,2,48,256]{3,2,1,0:T(8,128)(2,1)} %bitcast.45), calls=%async_computation.3 | async-start | bytes 1572864 | tf_op jit(solution)/shard_map/all_to_all | solution.py:202
  64.2 2.8 %copy.25 = bf16[1,2,768,1024]{2,3,1,0:T(8,128)(2,1)} copy(bf16[1,2,768,1024]{3,2,1,0:T(8,128)(2,1)S(1)} %copy-done) | data formatting | bytes 6291456 | tf_op args[2]
  68.9 1.2 slice_select_fusion
  71.2 1.1 faces.1
  72.3 1.5 %collective-permute-start = (bf16[2,256,256]{2,1,0:T(8,128)(2,1)}, bf16[2,256,256]{2,1,0:T(8,128)(2,1)S(1)}, u32[]{:S(2)}, u32[]{:S(2)}) collective-permute-start(bf16[2,256,256]{2,1,0:T(8,128)(2,1)} %faces.1), channel_id=1, source_target_pairs={{0,1},{1,0},{2,3},{3,2},{4,5},{5,4},{6,7},{7,6},{8,9},{9,8},{10,11... | collective-permute-start | bytes 786440 | tf_op jit(solution)/shard_map/ppermute | solution.py:252
  73.8 1.9 %pad_maximum_fusion = bf16[2,768,256]{1,2,0:T(8,128)(2,1)} fusion(bf16[2,768,128]{1,2,0:T(8,128)(2,1)S(1)} %slice_select_fusion, bf16[2,768,128]{1,2,0:T(8,128)(2,1)} %copy.29), kind=kLoop, calls=%fused_computation.2 | loop fusion | flops 1572864 | bytes 1572864 | tf_op jit(solution)/shard_map/concatenate | solution.py:231
  77.0 2.3 %copy.31.edge_ref = bf16[2,768,256]{2,1,0:T(8,128)(2,1)} copy(bf16[2,768,256]{1,2,0:T(8,128)(2,1)} %pad_maximum_fusion) | data formatting | bytes 1572864 | tf_op jit(solution)/shard_map/concatenate | solution.py:231
  79.3 1.2 fusion.11.back_ref
  81.7 1.4 %own.1.own_ref = f32[768,512]{1,0:T(8,128)S(1)} custom-call(s32[1]{0:T(128)S(6)} %convert_element_type.65.paired_ref, bf16[2,768,1024]{2,1,0:T(8,128)(2,1)S(1)} %bitcast.34, bf16[16,2,48,256]{3,2,1,0:T(8,128)(2,1)S(1)} %copy-done.3), custom_call_target="tpu_custom_call" | custom-call | tf_op jit(solution)/shard_map/own/pallas_call | solution.py:176
  84.6 1.4 %back.1.back_ref = f32[768,512]{1,0:T(8,128)S(1)} custom-call(s32[1]{0:T(128)S(6)} %convert_element_type.65.paired_ref, bf16[2,1024,768]{2,1,0:T(8,128)(2,1)S(1)} %bitcast.37, bf16[768,512]{1,0:T(8,128)(2,1)S(1)} %get-tuple-element.10.middle_ref), custom_call_target="tpu_custom_call" | custom-call | tf_op jit(solution)/shard_map/back/pallas_call | solution.py:176
  86.0 3.9 %collective-permute-done.1.got_ref = bf16[128,512]{1,0:T(8,128)(2,1)S(1)} collective-permute-done((bf16[128,512]{1,0:T(8,128)(2,1)S(1)}, bf16[128,512]{1,0:T(8,128)(2,1)S(1)}, u32[]{:S(2)}, u32[]{:S(2)}) %collective-permute-start.1) | collective-permute-done | bytes 131104 | tf_op jit(solution)/shard_map/ppermute | solution.py:268
  89.8 1.2 finish.1
  91.1 5.4 %all-to-all-start.2 = ((bf16[16,2,48,256]{3,2,1,0:T(8,128)(2,1)}), bf16[16,2,48,256]{3,2,1,0:T(8,128)(2,1)S(1)}, u32[]{:S(2)}, u32[]{:S(2)}) async-start(bf16[16,2,48,256]{3,2,1,0:T(8,128)(2,1)} %finish.1), calls=%async_computation.2 | async-start | bytes 1572864 | tf_op jit(solution)/shard_map/all_to_all | solution.py:202
  96.5 7.8 %mul.142.table_ref = bf16[512,512]{1,0:T(8,128)(2,1)S(1)} reshape(bf16[32,16,32,16]{3,2,1,0:T(8,128)(2,1)} %get-tuple-element.14) | data formatting | bytes 1048576 | tf_op jit(solution)/shard_map/mul | solution.py:38
  104.3 10.9 %all-to-all-done.2 = bf16[16,2,48,256]{3,2,1,0:T(8,128)(2,1)S(1)} async-done(((bf16[16,2,48,256]{3,2,1,0:T(8,128)(2,1)}), bf16[16,2,48,256]{3,2,1,0:T(8,128)(2,1)S(1)}, u32[]{:S(2)}, u32[]{:S(2)}) %all-to-all-start.2) | async-done | bytes 786464 | tf_op jit(solution)/shard_map/all_to_all | solution.py:202
  115.2 2.3 %respond.1 = f32[3,512]{1,0:T(4,128)S(1)} custom-call(bf16[512,512]{1,0:T(8,128)(2,1)S(1)} %mul.142.table_ref, bf16[32,48,256]{2,1,0:T(8,128)(2,1)S(1)} %bitcast.39, bf16[32,48,256]{2,1,0:T(8,128)(2,1)} %bitcast.19.state_ref), custom_call_target="tpu_custom_call" | custom-call | tf_op jit(solution)/shard_map/respond/pallas_call | solution.py:89
  117.8 11.8 %all_to_all.26 = f32[16,2,48]{2,1,0:T(2,128)S(1)} all-to-all(f32[16,2,48]{2,1,0:T(2,128)S(1)} %reshape_reshape.3), channel_id=1, replica_groups=mesh['sector'=16,'radial'=2] {'sector'}, dimensions={0} | all-to-all | bytes 12288 | tf_op jit(solution)/shard_map/all_to_all | solution.py:202
  (44 shorter events, 11.6 us)
Async XLA Ops:
  0.0 9.6 %copy-start.8 = (s32[16]{0:T(128)S(1)}, s32[16]{0:T(128)}, u32[]{:S(2)}) copy-start(s32[16]{0:T(128)} %param.8) | copy-start | bytes 196
  2.2 26.1 %all-to-all-start = ((bf16[16,2,48,256]{3,2,1,0:T(8,128)(2,1)}), bf16[16,2,48,256]{3,2,1,0:T(8,128)(2,1)S(1)}, u32[]{:S(2)}, u32[]{:S(2)}) async-start(bf16[16,2,48,256]{3,2,1,0:T(8,128)(2,1)} %bitcast.32), calls=%async_computation | async-start | bytes 1572864 | tf_op jit(solution)/shard_map/all_to_all | solution.py:202
  28.3 0.9 copy-start.4
  29.2 1.1 copy-start.5
  30.3 1.0 copy-start.7
  31.3 32.8 %copy-start = (bf16[1,2,768,1024]{3,2,1,0:T(8,128)(2,1)S(1)}, bf16[1,2,768,1024]{3,2,1,0:T(8,128)(2,1)}, u32[]{:S(2)}) copy-start(bf16[1,2,768,1024]{3,2,1,0:T(8,128)(2,1)} %param.7) | copy-start | bytes 9437188
  59.9 31.2 %all-to-all-start.3 = ((bf16[16,2,48,256]{3,2,1,0:T(8,128)(2,1)}), bf16[16,2,48,256]{3,2,1,0:T(8,128)(2,1)}, u32[]{:S(2)}, u32[]{:S(2)}) async-start(bf16[16,2,48,256]{3,2,1,0:T(8,128)(2,1)} %bitcast.45), calls=%async_computation.3 | async-start | bytes 1572864 | tf_op jit(solution)/shard_map/all_to_all | solution.py:202
  64.2 2.8 %copy-start.9 = (s32[1,2,128]{2,1,0:T(2,128)S(1)}, s32[1,2,128]{2,1,0:T(2,128)}, u32[]{:S(2)}) copy-start(s32[1,2,128]{2,1,0:T(2,128)} %param.9) | copy-start | bytes 3076
  70.0 1.1 copy-start.2
  72.3 10.8 %collective-permute-start = (bf16[2,256,256]{2,1,0:T(8,128)(2,1)}, bf16[2,256,256]{2,1,0:T(8,128)(2,1)S(1)}, u32[]{:S(2)}, u32[]{:S(2)}) collective-permute-start(bf16[2,256,256]{2,1,0:T(8,128)(2,1)} %faces.1), channel_id=1, source_target_pairs={{0,1},{1,0},{2,3},{3,2},{4,5},{5,4},{6,7},{7,6},{8,9},{9,8},{10,11... | collective-permute-start | bytes 786440 | tf_op jit(solution)/shard_map/ppermute | solution.py:252
  79.3 3.8 %copy-start.6 = (bf16[2,768,256]{2,1,0:T(8,128)(2,1)S(1)}, bf16[2,768,256]{2,1,0:T(8,128)(2,1)}, u32[]{:S(2)}) copy-start(bf16[2,768,256]{2,1,0:T(8,128)(2,1)} %copy.31.edge_ref) | copy-start | bytes 2359300
  80.6 1.1 copy-start.3
  81.7 2.9 %copy-start.1 = (bf16[1,2,768,1024]{2,3,1,0:T(8,128)(2,1)S(1)}, bf16[1,2,768,1024]{2,3,1,0:T(8,128)(2,1)}, u32[]{:S(2)}) copy-start(bf16[1,2,768,1024]{2,3,1,0:T(8,128)(2,1)} %copy.25) | copy-start | bytes 9437188
  84.0 5.9 %collective-permute-start.1 = (bf16[128,512]{1,0:T(8,128)(2,1)S(1)}, bf16[128,512]{1,0:T(8,128)(2,1)S(1)}, u32[]{:S(2)}, u32[]{:S(2)}) collective-permute-start(bf16[128,512]{1,0:T(8,128)(2,1)S(1)} %get-tuple-element.11), channel_id=1, source_target_pairs={{0,1},{1,0},{2,3},{3,2},{4,5},{5,4},{6,7},{7,6},{8,9},{9,8},{10,11... | collective-permute-start | bytes 393224 | tf_op jit(solution)/shard_map/ppermute | solution.py:268
  91.1 24.1 %all-to-all-start.2 = ((bf16[16,2,48,256]{3,2,1,0:T(8,128)(2,1)}), bf16[16,2,48,256]{3,2,1,0:T(8,128)(2,1)S(1)}, u32[]{:S(2)}, u32[]{:S(2)}) async-start(bf16[16,2,48,256]{3,2,1,0:T(8,128)(2,1)} %finish.1), calls=%async_computation.2 | async-start | bytes 1572864 | tf_op jit(solution)/shard_map/all_to_all | solution.py:202

commit v2 on v1

--- a/solution.py
+++ b/solution.py
@@ -11,7 +11,7 @@
 BF16 = jnp.bfloat16
 VMEM = pl.BlockSpec(memory_space=pltpu.VMEM)
 SMEM = pl.BlockSpec(memory_space=pltpu.SMEM)
-PARAMS = pltpu.CompilerParams(vmem_limit_bytes=48 * 1024 * 1024)
+ANY = pl.BlockSpec(memory_space=pl.ANY)
 TILE = 16
 
 
@@ -32,12 +32,6 @@
     return forward, inverse
 
 
-def widen(table):
-    eye = jnp.eye(TILE, dtype=BF16)
-    side = table.shape[0] * TILE
-    return (table[:, None, :, None] * eye[None, :, None, :]).reshape(side, side)
-
-
 def dot(a, b):
     return jnp.dot(a, b, preferred_element_type=F32)
 
@@ -51,23 +45,21 @@
         )
 
 
-def transform(forward, pieces):
+def transform(table, pieces):
     rows = pieces.shape[1]
     if rows % TILE:
-        return jnp.einsum("ks,sdr->kdr", forward, pieces, preferred_element_type=F32).astype(BF16)
-    return pl.pallas_call(
-        transform_kernel,
-        out_shape=jax.ShapeDtypeStruct(pieces.shape, BF16),
-        in_specs=[VMEM, VMEM],
-        out_specs=VMEM,
-        compiler_params=PARAMS,
-        name="transform",
-    )(widen(forward), pieces)
+        return jnp.einsum("ks,sdr->kdr", table, pieces, preferred_element_type=F32).astype(BF16)
+    return call(
+        transform_kernel, jax.ShapeDtypeStruct(pieces.shape, BF16), [VMEM, VMEM], "transform", 8, table, pieces
+    )
 
 
 def respond_kernel(table_ref, x_ref, state_ref, out_ref):
     count, rows, width = x_ref.shape
-    ones = jnp.ones((8, width), BF16)
+    lanes = 128
+    ones = jnp.ones((width, lanes), BF16)
+    place = lax.broadcasted_iota(jnp.int32, (count * TILE, lanes), 0) % lanes
+    diagonal = place == lax.broadcasted_iota(jnp.int32, (count * TILE, lanes), 1)
     for index, start in enumerate(range(0, rows, TILE)):
         tile = x_ref[:, start : start + TILE, :].reshape(count * TILE, width)
         adjoint = dot(table_ref[...], tile).astype(BF16).astype(F32)
@@ -75,25 +67,19 @@
         product = adjoint * state
         high = product.astype(BF16)
         low = (product - high.astype(F32)).astype(BF16)
-        contract = (((1,), (1,)), ((), ()))
-        total = lax.dot_general(ones, high, contract, preferred_element_type=F32)
-        total = total + lax.dot_general(ones, low, contract, preferred_element_type=F32)
-        out_ref[index : index + 1, :] = total[:1]
-
-
-def respond(inverse, pieces, state):
+        total = jnp.where(diagonal, dot(high, ones) + dot(low, ones), 0.0)
+        out_ref[index] = jnp.sum(total.reshape(count * TILE // lanes, lanes, lanes), axis=1)
+
+
+def respond(table, pieces, state):
     count, rows, _ = pieces.shape
     if rows % TILE:
-        adjoint = jnp.einsum("sk,kdr->sdr", inverse, pieces, preferred_element_type=F32).astype(BF16)
+        adjoint = jnp.einsum("sk,kdr->sdr", table, pieces, preferred_element_type=F32).astype(BF16)
         return jnp.sum(adjoint.astype(F32) * state.astype(F32), axis=-1)
-    sums = pl.pallas_call(
-        respond_kernel,
-        out_shape=jax.ShapeDtypeStruct((rows // TILE, count * TILE), F32),
-        in_specs=[VMEM, VMEM, VMEM],
-        out_specs=VMEM,
-        compiler_params=PARAMS,
-        name="respond",
-    )(widen(inverse), pieces, state)
+    sums = call(
+        respond_kernel, jax.ShapeDtypeStruct((rows // TILE, count * TILE // 128, 128), F32),
+        [VMEM, VMEM, VMEM], "respond", 12, table, pieces, state,
+    )
     return sums.reshape(rows // TILE, count, TILE).transpose(1, 0, 2).reshape(count, rows)
 
 
@@ -111,13 +97,65 @@
         out_ref[part] = dot(pick, rows_of(x_ref, part)).astype(BF16)
 
 
-def prepare_kernel(index_ref, weight_ref, out_ref):
+def widen(table):
+    count = table.shape[0]
+    side = count * TILE
+    spread = lax.broadcasted_iota(jnp.int32, (side, count), 0) // TILE
+    spread = spread == lax.broadcasted_iota(jnp.int32, (side, count), 1)
+    spread = jnp.where(spread, 1.0, 0.0).astype(BF16)
+    tall = dot(spread, table).astype(BF16)
+    full = lax.dot_general(tall, spread, (((1,), (1,)), ((), ())), preferred_element_type=F32)
+    row = lax.broadcasted_iota(jnp.int32, (side, side), 0) % TILE
+    column = lax.broadcasted_iota(jnp.int32, (side, side), 1) % TILE
+    return jnp.where(row == column, full, 0.0).astype(BF16)
+
+
+def widen_kernel(forward_ref, inverse_ref, forward_out, inverse_out):
+    forward_out[...] = widen(forward_ref[...])
+    inverse_out[...] = widen(inverse_ref[...])
+
+
+def prepare_kernel(low_ref, index_ref, weight_ref, edge_ref, turned_ref, away_ref):
     cycle = weight_ref.shape[1]
     count = index_ref.shape[1]
+    leaving = away_ref.shape[1]
+    face = (weight_ref.shape[2] - cycle) // 2
     pick = lax.broadcasted_iota(jnp.int32, (cycle, count), 0) == index_ref[...]
     pick = jnp.where(pick, 1.0, 0.0).astype(BF16)
     for part in range(2):
-        out_ref[part] = dot(weight_ref[part, :, :cycle], pick).astype(BF16)
+        own = weight_ref[part, :, :cycle]
+        outward = weight_ref[part, :, cycle:]
+        if leaving == face:
+            outward = jnp.where(low_ref[0] != 0, outward[:, :face], outward[:, face:])
+        edge_ref[part, :, :count] = dot(own, pick).astype(BF16)
+        edge_ref[part, :, count:] = outward
+        turned_ref[part] = own.T
+        away_ref[part] = outward.T
+
+
+def chunk_kernel(x_ref, out_ref, sems):
+    local = x_ref.shape[0]
+    copies = [pltpu.make_async_copy(x_ref.at[i], out_ref.at[:, i], sems.at[i]) for i in range(local)]
+    for copy in copies:
+        copy.start()
+    for copy in copies:
+        copy.wait()
+
+
+def by_chunk(block, devices):
+    local, cycle, width = block.shape
+    rows = cycle // devices
+    split = block.reshape(local, devices, rows, width)
+    if rows % TILE:
+        return split.transpose(1, 0, 2, 3)
+    return pl.pallas_call(
+        chunk_kernel,
+        out_shape=jax.ShapeDtypeStruct((devices, local, rows, width), block.dtype),
+        in_specs=[ANY],
+        out_specs=ANY,
+        scratch_shapes=[pltpu.SemaphoreType.DMA((local,))],
+        name="chunk",
+    )(split)
 
 
 def right_sides(real, imag, paired):
@@ -155,10 +193,9 @@
 
 def back_kernel(paired_ref, turned_ref, middle_ref, out_ref):
     paired = paired_ref[0] != 0
-    cycle = middle_ref.shape[0]
     width = middle_ref.shape[1] // 2
     upper, lower = back_sides(middle_ref[:, :width], middle_ref[:, width:], paired)
-    out_ref[...] = dot(turned_ref[0, :cycle], upper) + dot(turned_ref[1, :cycle], lower)
+    out_ref[...] = dot(turned_ref[0], upper) + dot(turned_ref[1], lower)
 
 
 def finish_kernel(index_ref, back_ref, got_ref, out_ref):
@@ -172,13 +209,13 @@
         out_ref[:, part] = total[:, part * width : (part + 1) * width].reshape(chunks, rows, width)
 
 
-def call(kernel, outs, specs, name, *operands):
+def call(kernel, outs, specs, name, mebibytes, *operands):
     return pl.pallas_call(
         kernel,
         out_shape=outs,
         in_specs=specs,
         out_specs=jax.tree.map(lambda _: VMEM, outs),
-        compiler_params=PARAMS,
+        compiler_params=pltpu.CompilerParams(vmem_limit_bytes=mebibytes * 1024 * 1024),
         name=name,
     )(*operands)
 
@@ -201,52 +238,52 @@
     def exchange(pieces):
         return lax.all_to_all(pieces, "sector", split_axis=0, concat_axis=0, tiled=True)
 
-    def by_chunk(block):
-        return block.reshape(local, devices, rows, width).transpose(1, 0, 2, 3)
-
     def step(block, shift):
         pairs = [(i, i + shift) for i in range(cycles) if 0 <= i + shift < cycles]
         return lax.ppermute(block, "radial", pairs)
 
-    above = weight[:, :, cycle : cycle + face]
-    below = weight[:, :, cycle + face :]
     if cycles == 2:
-        low = here == 0
-        toward = jnp.where(low, outer, inner)
-        away = jnp.where(low, inner, outer)
+        toward = jnp.where(here == 0, outer, inner)
+        away = jnp.where(here == 0, inner, outer)
         sent = jnp.concatenate([toward, away])
-        gathered = toward
-        scattered = away
-        outward = jnp.where(low, above, below)
+        gathered, scattered = toward, away
     else:
-        sent = jnp.concatenate([inner, outer])
-        gathered = jnp.concatenate([inner, outer])
+        sent = gathered = jnp.concatenate([inner, outer])
         scattered = jnp.concatenate([outer, inner])
-        outward = jnp.concatenate([above, below], axis=2)
-
-    gains = call(
-        prepare_kernel, shape((2, cycle, gathered.shape[0]), BF16), [VMEM, VMEM], "prepare",
-        gathered.reshape(1, -1), weight,
-    )
-    edge = jnp.concatenate([gains, outward], axis=2)
-    turned = jnp.swapaxes(weight, 1, 2)
-    outward_turned = jnp.swapaxes(outward, 1, 2)
-
-    pieces = exchange(by_chunk(loads)).reshape(sectors, rows, width)
+    sent = sent.reshape(-1, 1)
+    scattered = scattered.reshape(1, -1)
+    edges = gathered.shape[0]
+
+    pieces = exchange(by_chunk(loads, devices)).reshape(sectors, rows, width)
+
+    edge, turned, outward = call(
+        prepare_kernel,
+        (shape((2, cycle, 2 * edges), BF16), shape((2, cycle, cycle), BF16), shape((2, edges, cycle), BF16)),
+        [SMEM, VMEM, VMEM], "prepare", 20,
+        (here == 0).astype(jnp.int32).reshape(1), gathered.reshape(1, -1), weight,
+    )
+    if aligned:
+        wide = shape((sectors * TILE, sectors * TILE), BF16)
+        forward, inverse = call(widen_kernel, (wide, wide), [VMEM, VMEM], "widen", 12, forward, inverse)
+    state = by_chunk(state, devices)
+    ready = (pieces, edge, turned, outward, forward, inverse, state, sent, scattered, paired)
+    pieces, edge, turned, outward, forward, inverse, state, sent, scattered, paired = (
+        lax.optimization_barrier(ready)
+    )
+
     spectrum = transform(forward, pieces)
     harmonic = exchange(spectrum.reshape(devices, 2, rows, width))
 
     harmonic, state = lax.optimization_barrier((harmonic, state))
-    state = exchange(by_chunk(state)).reshape(sectors, rows, width)
+    state = exchange(state).reshape(sectors, rows, width)
 
     if not aligned:
         harmonic = harmonic.transpose(1, 0, 2, 3).reshape(1, 2, cycle, width)
     faces = call(
-        faces_kernel, shape((2, 2 * face, width), BF16), [VMEM, VMEM], "faces",
-        sent.reshape(-1, 1), harmonic,
+        faces_kernel, shape((2, 2 * face, width), BF16), [VMEM, VMEM], "faces", 8, sent, harmonic,
     )
     own = call(
-        own_kernel, shape((cycle, 2 * width), F32), [SMEM, VMEM, VMEM], "own", paired, weight, harmonic
+        own_kernel, shape((cycle, 2 * width), F32), [SMEM, VMEM, VMEM], "own", 12, paired, weight, harmonic
     )
     if cycles == 2:
         near = lax.ppermute(faces, "radial", [(0, 1), (1, 0)])
@@ -260,20 +297,20 @@
         near = jnp.concatenate([lower[:, face:], upper[:, :face], far_above, far_below], axis=1)
     middle, leaving = call(
         middle_kernel,
-        (shape((cycle, 2 * width), BF16), shape((outward.shape[2], 2 * width), BF16)),
-        [SMEM, VMEM, VMEM, VMEM, VMEM], "middle",
-        paired, own, edge, outward_turned, near,
+        (shape((cycle, 2 * width), BF16), shape((edges, 2 * width), BF16)),
+        [SMEM, VMEM, VMEM, VMEM, VMEM], "middle", 12,
+        paired, own, edge, outward, near,
     )
     if cycles == 2:
         got = lax.ppermute(leaving, "radial", [(0, 1), (1, 0)])
     else:
         got = jnp.concatenate([step(leaving[:face], 1), step(leaving[face:], -1)], axis=0)
     back = call(
-        back_kernel, shape((cycle, 2 * width), F32), [SMEM, VMEM, VMEM], "back", paired, turned, middle
+        back_kernel, shape((cycle, 2 * width), F32), [SMEM, VMEM, VMEM], "back", 12, paired, turned, middle
     )
     solved = call(
         finish_kernel, shape((devices, 2, rows, width) if aligned else (1, 2, cycle, width), BF16),
-        [VMEM, VMEM, VMEM], "finish", scattered.reshape(1, -1), back, got,
+        [VMEM, VMEM, VMEM], "finish", 12, scattered, back, got,
     )
     if not aligned:
         solved = solved.reshape(2, devices, rows, width).transpose(1, 0, 2, 3)

time: 131 us -> 157 us (1.20)
  Pallas kernels: 9.68 us -> 59.9 us
  blocking collectives: 37.6 us -> 61.8 us
  local copies, waits for them, and re-layouts: 33.7 us -> 9.75 us
  waiting for transfers between devices: 20.5 us -> 8.69 us
  other arithmetic: 8.74 us -> 0.77 us
  starting transfers between devices: 19.2 us -> 14.9 us
    pallas_call x2, Pallas kernels: 2.9 us -> 49.9 us  [by_chunk(): pl.pallas_call(chunk_kernel, out_shape=jax.ShapeDtypeStruct((devices, loc...]
    all_to_all x2 -> x3, blocking collectives: 37.6 us -> 61.8 us  [exchange(): lax.all_to_all(pieces, 'sector', split_axis=0, concat_axis=0, tiled=True)]
    mul x2 -> x0, local copies, waits for them, and re-layouts: 16.2 us -> none  [widen(): return (table[:, None, :, None] * eye[None, :, None, :]).reshape(side, side)]
    all_to_all x3 -> x2, waiting for transfers between devices: 16.7 us -> 1.46 us  [exchange(): lax.all_to_all(pieces, 'sector', split_axis=0, concat_axis=0, tiled=True)]
    all_to_all x3 -> x2, starting transfers between devices: 17 us -> 11.7 us  [exchange(): lax.all_to_all(pieces, 'sector', split_axis=0, concat_axis=0, tiled=True)]
    ppermute x1, waiting for transfers between devices: 0.01 us -> 4.82 us  [per_device(): near = lax.ppermute(faces, 'radial', [(0, 1), (1, 0)])]
    reshape x3 -> x0, local copies, waits for them, and re-layouts: 4.49 us -> none  [the longest x2 4.35 us: by_chunk(): return block.reshape(local, devices, rows, width).transpose(1, 0, 2, 3)]
    mul x1 -> x0, other arithmetic: 3.64 us -> none  [widen(): return (table[:, None, :, None] * eye[None, :, None, :]).reshape(side, side)]
  transfers between devices with their start and end apart: 5 -> 4, of which waited for: 3 -> 3; matrix products, arithmetic and copies ran while one was open for 24% -> 1% of each run, Pallas kernels for 5% -> 20%
where the time goes in v2:
time: 157 us
  blocking collectives  61.8 us (39%)
  Pallas kernels  59.9 us (38%)
  starting transfers between devices  14.9 us (9%)
  local copies, waits for them, and re-layouts  9.75 us (6%)
  waiting for transfers between devices  8.69 us (6%)
    all_to_all x3, blocking collectives, exchange(): lax.all_to_all(pieces, 'sector', split_axis=0, concat_axis=0, tiled=True)  61.8 us
    pallas_call x2, Pallas kernels, by_chunk(): pl.pallas_call(chunk_kernel, out_shape=jax.ShapeDtypeStruct((devices, loc...  49.9 us
    all_to_all x2, starting transfers between devices, exchange(): lax.all_to_all(pieces, 'sector', split_axis=0, concat_axis=0, tiled=True)  11.7 us
    pallas_call x9, Pallas kernels, call(): pl.pallas_call(kernel, out_shape=outs, in_specs=specs, out_specs=jax.tree...  10 us
    unnamed x30, local copies, waits for them, and re-layouts  8.04 us
    ppermute x1, waiting for transfers between devices, per_device(): near = lax.ppermute(faces, 'radial', [(0, 1), (1, 0)])  4.82 us
  transfers between devices with their start and end apart: 4, of which 3 were waited for; matrix products, arithmetic and copies ran while one was open for 1% of the time, Pallas kernels for 20%

profile of v2, /device:TPU:0, one launch (start us, length us, event | category | flops | bytes accessed | tf_op | source)
XLA Modules:
  0.0 156.7 jit_solution(12175823162132688515)
XLA Ops:
  0.0 24.9 %chunk.2 = bf16[16,2,48,256]{3,2,1,0:T(8,128)(2,1)} custom-call(bf16[2,16,48,256]{3,2,1,0:T(8,128)(2,1)} %bitcast.28), custom_call_target="tpu_custom_call" | custom-call | tf_op jit(solution)/shard_map/chunk/pallas_call | solution.py:151
  25.0 7.4 %all-to-all-start = ((bf16[16,2,48,256]{3,2,1,0:T(8,128)(2,1)}), bf16[16,2,48,256]{3,2,1,0:T(8,128)(2,1)}, u32[]{:S(2)}, u32[]{:S(2)}) async-start(bf16[16,2,48,256]{3,2,1,0:T(8,128)(2,1)} %chunk.2), calls=%async_computation | async-start | bytes 1572864 | tf_op jit(solution)/shard_map/all_to_all | solution.py:239
  34.5 24.9 %chunk.3 = bf16[16,2,48,256]{3,2,1,0:T(8,128)(2,1)} custom-call(bf16[2,16,48,256]{3,2,1,0:T(8,128)(2,1)} %bitcast.29), custom_call_target="tpu_custom_call" | custom-call | tf_op jit(solution)/shard_map/chunk/pallas_call | solution.py:151
  61.0 0.8 copy-done.9
  61.8 0.9 prepare.1
  62.7 1.4 copy-done.3
  64.1 0.9 copy-done.5
  65.8 1.0 copy-done.10
  66.8 1.7 %transform.1 = bf16[32,48,256]{2,1,0:T(8,128)(2,1)S(1)} custom-call(bf16[512,512]{1,0:T(8,128)(2,1)S(1)} %copy-done.10, bf16[32,48,256]{2,1,0:T(8,128)(2,1)} %bitcast.1.x_ref), custom_call_target="tpu_custom_call" | custom-call | tf_op jit(solution)/shard_map/transform/pallas_call | solution.py:213
  68.5 26.1 %all_to_all.25.x_ref = bf16[16,2,48,256]{3,2,1,0:T(8,128)(2,1)} all-to-all(bf16[16,2,48,256]{3,2,1,0:T(8,128)(2,1)S(1)} %bitcast.21), channel_id=1, replica_groups=mesh['sector'=16,'radial'=2] {'sector'}, dimensions={0} | all-to-all | bytes 1572864 | tf_op jit(solution)/shard_map/all_to_all | solution.py:239
  94.7 4.3 %all-to-all-start.3 = ((bf16[16,2,48,256]{3,2,1,0:T(8,128)(2,1)}), bf16[16,2,48,256]{3,2,1,0:T(8,128)(2,1)}, u32[]{:S(2)}, u32[]{:S(2)}) async-start(bf16[16,2,48,256]{3,2,1,0:T(8,128)(2,1)} %chunk.3), calls=%async_computation.3 | async-start | bytes 1572864 | tf_op jit(solution)/shard_map/all_to_all | solution.py:239
  99.1 1.1 copy-done.1
  100.7 1.6 %collective-permute-start = (bf16[2,256,256]{2,1,0:T(8,128)(2,1)S(1)}, bf16[2,256,256]{2,1,0:T(8,128)(2,1)S(1)}, u32[]{:S(2)}, u32[]{:S(2)}) collective-permute-start(bf16[2,256,256]{2,1,0:T(8,128)(2,1)S(1)} %faces.1), channel_id=1, source_target_pairs={{0,1},{1,0},{2,3},{3,2},{4,5},{5,4},{6,7},{7,6},{8,9},{9,8},{10,11... | collective-permute-start | bytes 786440 | tf_op jit(solution)/shard_map/ppermute | solution.py:289
  102.2 1.1 copy-done.2
  103.4 1.4 own.1.own_ref
  104.8 4.8 %collective-permute-done.near_ref = bf16[2,256,256]{2,1,0:T(8,128)(2,1)S(1)} collective-permute-done((bf16[2,256,256]{2,1,0:T(8,128)(2,1)S(1)}, bf16[2,256,256]{2,1,0:T(8,128)(2,1)S(1)}, u32[]{:S(2)}, u32[]{:S(2)}) %collective-permute-start) | collective-permute-done | bytes 262176 | tf_op jit(solution)/shard_map/ppermute | solution.py:289
  109.6 0.9 middle.1
  110.5 1.6 %collective-permute-start.1 = (bf16[128,512]{1,0:T(8,128)(2,1)S(1)}, bf16[128,512]{1,0:T(8,128)(2,1)S(1)}, u32[]{:S(2)}, u32[]{:S(2)}) collective-permute-start(bf16[128,512]{1,0:T(8,128)(2,1)S(1)} %get-tuple-element.41), channel_id=1, source_target_pairs={{0,1},{1,0},{2,3},{3,2},{4,5},{5,4},{6,7},{7,6},{8,9},{9,8},{10,11... | collective-permute-start | bytes 393224 | tf_op jit(solution)/shard_map/ppermute | solution.py:305
  112.1 1.4 back.1.back_ref
  113.4 2.4 %collective-permute-done.1.got_ref = bf16[128,512]{1,0:T(8,128)(2,1)S(1)} collective-permute-done((bf16[128,512]{1,0:T(8,128)(2,1)S(1)}, bf16[128,512]{1,0:T(8,128)(2,1)S(1)}, u32[]{:S(2)}, u32[]{:S(2)}) %collective-permute-start.1) | collective-permute-done | bytes 131104 | tf_op jit(solution)/shard_map/ppermute | solution.py:305
  116.2 1.5 all-to-all-done.3
  117.7 25.5 %all_to_all.26 = bf16[16,2,48,256]{3,2,1,0:T(8,128)(2,1)S(1)} all-to-all(bf16[16,2,48,256]{3,2,1,0:T(8,128)(2,1)S(1)} %finish.1), channel_id=1, replica_groups=mesh['sector'=16,'radial'=2] {'sector'}, dimensions={0} | all-to-all | bytes 1572864 | tf_op jit(solution)/shard_map/all_to_all | solution.py:239
  143.1 2.4 %respond.1 = f32[3,4,128]{2,1,0:T(4,128)S(1)} custom-call(bf16[512,512]{1,0:T(8,128)(2,1)S(1)} %copy-done.8, bf16[32,48,256]{2,1,0:T(8,128)(2,1)S(1)} %bitcast.20, bf16[32,48,256]{2,1,0:T(8,128)(2,1)} %bitcast.15.state_ref), custom_call_target="tpu_custom_call" | custom-call | tf_op jit(solution)/shard_map/respond/pallas_call | solution.py:213
  145.8 10.2 %all_to_all.27 = f32[16,2,48]{2,1,0:T(2,128)S(1)} all-to-all(f32[16,2,48]{2,1,0:T(2,128)S(1)} %reshape_reshape.3), channel_id=1, replica_groups=mesh['sector'=16,'radial'=2] {'sector'}, dimensions={0} | all-to-all | bytes 12288 | tf_op jit(solution)/shard_map/all_to_all | solution.py:239
  (44 shorter events, 5.5 us)
Async XLA Ops:
  0.0 32.4 %copy-start.13 = (s32[16]{0:T(128)S(1)}, s32[16]{0:T(128)}, u32[]{:S(2)}) copy-start(s32[16]{0:T(128)} %param.8) | copy-start | bytes 196
  0.0 61.8 %copy-start.14 = (s32[1,2,128]{2,1,0:T(2,128)S(1)}, s32[1,2,128]{2,1,0:T(2,128)}, u32[]{:S(2)}) copy-start(s32[1,2,128]{2,1,0:T(2,128)} %param.9) | copy-start | bytes 3076
  0.0 61.8 %copy-start = (bf16[1,2,768,1024]{3,2,1,0:T(8,128)(2,1)S(1)}, bf16[1,2,768,1024]{3,2,1,0:T(8,128)(2,1)}, u32[]{:S(2)}) copy-start(bf16[1,2,768,1024]{3,2,1,0:T(8,128)(2,1)} %param.7) | copy-start | bytes 9437188
  25.0 40.8 %all-to-all-start = ((bf16[16,2,48,256]{3,2,1,0:T(8,128)(2,1)}), bf16[16,2,48,256]{3,2,1,0:T(8,128)(2,1)}, u32[]{:S(2)}, u32[]{:S(2)}) async-start(bf16[16,2,48,256]{3,2,1,0:T(8,128)(2,1)} %chunk.2), calls=%async_computation | async-start | bytes 1572864 | tf_op jit(solution)/shard_map/all_to_all | solution.py:239
  60.2 0.8 copy-start.7
  61.0 0.8 copy-start.9
  62.6 1.4 copy-start.3
  64.1 0.9 copy-start.5
  65.0 0.8 copy-start.11
  65.8 1.0 copy-start.10
  94.7 23.0 %all-to-all-start.3 = ((bf16[16,2,48,256]{3,2,1,0:T(8,128)(2,1)}), bf16[16,2,48,256]{3,2,1,0:T(8,128)(2,1)}, u32[]{:S(2)}, u32[]{:S(2)}) async-start(bf16[16,2,48,256]{3,2,1,0:T(8,128)(2,1)} %chunk.3), calls=%async_computation.3 | async-start | bytes 1572864 | tf_op jit(solution)/shard_map/all_to_all | solution.py:239
  99.1 1.1 copy-start.1
  100.7 8.9 %collective-permute-start = (bf16[2,256,256]{2,1,0:T(8,128)(2,1)S(1)}, bf16[2,256,256]{2,1,0:T(8,128)(2,1)S(1)}, u32[]{:S(2)}, u32[]{:S(2)}) collective-permute-start(bf16[2,256,256]{2,1,0:T(8,128)(2,1)S(1)} %faces.1), channel_id=1, source_target_pairs={{0,1},{1,0},{2,3},{3,2},{4,5},{5,4},{6,7},{7,6},{8,9},{9,8},{10,11... | collective-permute-start | bytes 786440 | tf_op jit(solution)/shard_map/ppermute | solution.py:289
  102.2 1.1 copy-start.2
  103.4 6.2 %copy-start.6 = (bf16[2,768,256]{2,1,0:T(8,128)(2,1)S(1)}, bf16[2,768,256]{2,1,0:T(8,128)(2,1)}, u32[]{:S(2)}) copy-start(bf16[2,768,256]{2,1,0:T(8,128)(2,1)} %copy-done.5) | copy-start | bytes 2359300
  103.4 6.2 %copy-start.12 = (bf16[2,128,768]{2,1,0:T(8,128)(2,1)S(1)}, bf16[2,128,768]{2,1,0:T(8,128)(2,1)}, u32[]{:S(2)}) copy-start(bf16[2,128,768]{2,1,0:T(8,128)(2,1)} %copy-done.11) | copy-start | bytes 1179652
  104.8 7.3 %copy-start.4 = (bf16[2,768,768]{2,1,0:T(8,128)(2,1)S(1)}, bf16[2,768,768]{2,1,0:T(8,128)(2,1)}, u32[]{:S(2)}) copy-start(bf16[2,768,768]{2,1,0:T(8,128)(2,1)} %copy-done.3) | copy-start | bytes 7077892
  110.5 5.4 %collective-permute-start.1 = (bf16[128,512]{1,0:T(8,128)(2,1)S(1)}, bf16[128,512]{1,0:T(8,128)(2,1)S(1)}, u32[]{:S(2)}, u32[]{:S(2)}) collective-permute-start(bf16[128,512]{1,0:T(8,128)(2,1)S(1)} %get-tuple-element.41), channel_id=1, source_target_pairs={{0,1},{1,0},{2,3},{3,2},{4,5},{5,4},{6,7},{7,6},{8,9},{9,8},{10,11... | collective-permute-start | bytes 393224 | tf_op jit(solution)/shard_map/ppermute | solution.py:305
  113.4 29.7 %copy-start.8 = (bf16[512,512]{1,0:T(8,128)(2,1)S(1)}, bf16[512,512]{1,0:T(8,128)(2,1)}, u32[]{:S(2)}) copy-start(bf16[512,512]{1,0:T(8,128)(2,1)} %copy-done.7) | copy-start | bytes 1572868

commit v3 on v2

--- a/solution.py
+++ b/solution.py
@@ -13,6 +13,7 @@
 SMEM = pl.BlockSpec(memory_space=pltpu.SMEM)
 ANY = pl.BlockSpec(memory_space=pl.ANY)
 TILE = 16
+TOKEN = jax.ShapeDtypeStruct((8, 128), jnp.float32)
 
 
 def tables(assign, sectors):
@@ -36,8 +37,9 @@
     return jnp.dot(a, b, preferred_element_type=F32)
 
 
-def transform_kernel(table_ref, x_ref, out_ref):
+def transform_kernel(table_ref, x_ref, out_ref, token_ref):
     count, rows, width = x_ref.shape
+    token_ref[...] = jnp.zeros_like(token_ref)
     for start in range(0, rows, TILE):
         tile = x_ref[:, start : start + TILE, :].reshape(count * TILE, width)
         out_ref[:, start : start + TILE, :] = (
@@ -48,14 +50,21 @@
 def transform(table, pieces):
     rows = pieces.shape[1]
     if rows % TILE:
-        return jnp.einsum("ks,sdr->kdr", table, pieces, preferred_element_type=F32).astype(BF16)
+        out = jnp.einsum("ks,sdr->kdr", table, pieces, preferred_element_type=F32).astype(BF16)
+        return out, jnp.zeros(TOKEN.shape, TOKEN.dtype)
     return call(
-        transform_kernel, jax.ShapeDtypeStruct(pieces.shape, BF16), [VMEM, VMEM], "transform", 8, table, pieces
-    )
-
-
-def respond_kernel(table_ref, x_ref, state_ref, out_ref):
+        transform_kernel, (jax.ShapeDtypeStruct(pieces.shape, BF16), TOKEN), [VMEM, VMEM], "transform", 8,
+        table, pieces,
+    )
+
+
+def respond_kernel(table_ref, x_ref, far_ref, out_ref, state_ref, sems):
     count, rows, width = x_ref.shape
+    copies = []
+    for index, start in enumerate(range(0, rows, TILE)):
+        span = slice(start, start + TILE)
+        copies.append(pltpu.make_async_copy(far_ref.at[:, span], state_ref.at[:, span], sems.at[index]))
+        copies[-1].start()
     lanes = 128
     ones = jnp.ones((width, lanes), BF16)
     place = lax.broadcasted_iota(jnp.int32, (count * TILE, lanes), 0) % lanes
@@ -63,6 +72,7 @@
     for index, start in enumerate(range(0, rows, TILE)):
         tile = x_ref[:, start : start + TILE, :].reshape(count * TILE, width)
         adjoint = dot(table_ref[...], tile).astype(BF16).astype(F32)
+        copies[index].wait()
         state = state_ref[:, start : start + TILE, :].reshape(count * TILE, width).astype(F32)
         product = adjoint * state
         high = product.astype(BF16)
@@ -78,7 +88,8 @@
         return jnp.sum(adjoint.astype(F32) * state.astype(F32), axis=-1)
     sums = call(
         respond_kernel, jax.ShapeDtypeStruct((rows // TILE, count * TILE // 128, 128), F32),
-        [VMEM, VMEM, VMEM], "respond", 12, table, pieces, state,
+        [VMEM, VMEM, ANY], "respond", 12, table, pieces, state,
+        scratch=(pltpu.VMEM(state.shape, BF16), pltpu.SemaphoreType.DMA((rows // TILE,))),
     )
     return sums.reshape(rows // TILE, count, TILE).transpose(1, 0, 2).reshape(count, rows)
 
@@ -88,7 +99,8 @@
     return x_ref[:, part].reshape(chunks * rows, width)
 
 
-def faces_kernel(index_ref, x_ref, out_ref):
+def faces_kernel(index_ref, x_ref, out_ref, token_ref):
+    token_ref[...] = jnp.zeros_like(token_ref)
     count = index_ref.shape[0]
     cycle = x_ref.shape[0] * x_ref.shape[2]
     pick = index_ref[...] == lax.broadcasted_iota(jnp.int32, (count, cycle), 1)
@@ -133,29 +145,29 @@
         away_ref[part] = outward.T
 
 
-def chunk_kernel(x_ref, out_ref, sems):
-    local = x_ref.shape[0]
-    copies = [pltpu.make_async_copy(x_ref.at[i], out_ref.at[:, i], sems.at[i]) for i in range(local)]
-    for copy in copies:
-        copy.start()
+def chunk_kernel(token_ref, x_ref, out_ref, sems):
+    local, devices = x_ref.shape[:2]
+    step = devices // sems.shape[1]
+    copies = []
+    for i in range(local):
+        for j in range(sems.shape[1]):
+            span = slice(j * step, (j + 1) * step)
+            copies.append(pltpu.make_async_copy(x_ref.at[i, span], out_ref.at[span, i], sems.at[i, j]))
+            copies[-1].start()
     for copy in copies:
         copy.wait()
 
 
-def by_chunk(block, devices):
+def by_chunk(block, devices, token):
     local, cycle, width = block.shape
     rows = cycle // devices
     split = block.reshape(local, devices, rows, width)
-    if rows % TILE:
+    if rows % TILE or devices % 4:
         return split.transpose(1, 0, 2, 3)
-    return pl.pallas_call(
-        chunk_kernel,
-        out_shape=jax.ShapeDtypeStruct((devices, local, rows, width), block.dtype),
-        in_specs=[ANY],
-        out_specs=ANY,
-        scratch_shapes=[pltpu.SemaphoreType.DMA((local,))],
-        name="chunk",
-    )(split)
+    return call(
+        chunk_kernel, jax.ShapeDtypeStruct((devices, local, rows, width), block.dtype), [ANY, ANY], "chunk", 8,
+        token, split, scratch=(pltpu.SemaphoreType.DMA((local, 4)),),
+    )
 
 
 def right_sides(real, imag, paired):
@@ -209,12 +221,13 @@
         out_ref[:, part] = total[:, part * width : (part + 1) * width].reshape(chunks, rows, width)
 
 
-def call(kernel, outs, specs, name, mebibytes, *operands):
+def call(kernel, outs, specs, name, mebibytes, *operands, scratch=()):
     return pl.pallas_call(
         kernel,
         out_shape=outs,
         in_specs=specs,
         out_specs=jax.tree.map(lambda _: VMEM, outs),
+        scratch_shapes=scratch,
         compiler_params=pltpu.CompilerParams(vmem_limit_bytes=mebibytes * 1024 * 1024),
         name=name,
     )(*operands)
@@ -254,7 +267,7 @@
     scattered = scattered.reshape(1, -1)
     edges = gathered.shape[0]
 
-    pieces = exchange(by_chunk(loads, devices)).reshape(sectors, rows, width)
+    pieces = exchange(by_chunk(loads, devices, jnp.zeros(TOKEN.shape, TOKEN.dtype))).reshape(sectors, rows, width)
 
     edge, turned, outward = call(
         prepare_kernel,
@@ -265,23 +278,17 @@
     if aligned:
         wide = shape((sectors * TILE, sectors * TILE), BF16)
         forward, inverse = call(widen_kernel, (wide, wide), [VMEM, VMEM], "widen", 12, forward, inverse)
-    state = by_chunk(state, devices)
-    ready = (pieces, edge, turned, outward, forward, inverse, state, sent, scattered, paired)
-    pieces, edge, turned, outward, forward, inverse, state, sent, scattered, paired = (
-        lax.optimization_barrier(ready)
-    )
-
-    spectrum = transform(forward, pieces)
+    spectrum, token = transform(forward, pieces)
     harmonic = exchange(spectrum.reshape(devices, 2, rows, width))
-
-    harmonic, state = lax.optimization_barrier((harmonic, state))
-    state = exchange(state).reshape(sectors, rows, width)
+    state = by_chunk(state, devices, token)
 
     if not aligned:
         harmonic = harmonic.transpose(1, 0, 2, 3).reshape(1, 2, cycle, width)
-    faces = call(
-        faces_kernel, shape((2, 2 * face, width), BF16), [VMEM, VMEM], "faces", 8, sent, harmonic,
-    )
+    faces, token = call(
+        faces_kernel, (shape((2, 2 * face, width), BF16), TOKEN), [VMEM, VMEM], "faces", 8, sent, harmonic
+    )
+    state, _ = lax.optimization_barrier((state, token))
+    state = exchange(state).reshape(sectors, rows, width)
     own = call(
         own_kernel, shape((cycle, 2 * width), F32), [SMEM, VMEM, VMEM], "own", 12, paired, weight, harmonic
     )

time: 157 us -> 118 us (0.75)
  Pallas kernels: 59.9 us -> 14.2 us
  waiting for transfers between devices: 8.69 us -> 38.5 us
  blocking collectives: 61.8 us -> 35.7 us
  starting transfers between devices: 14.9 us -> 21.6 us
  local copies, waits for them, and re-layouts: 9.75 us -> 5.86 us
    pallas_call x2 -> x0, Pallas kernels: 49.9 us -> none  [by_chunk(): pl.pallas_call(chunk_kernel, out_shape=jax.ShapeDtypeStruct((devices, loc...]
    all_to_all x2 -> x3, waiting for transfers between devices: 1.46 us -> 33.7 us  [exchange(): lax.all_to_all(pieces, 'sector', split_axis=0, concat_axis=0, tiled=True)]
    all_to_all x3 -> x2, blocking collectives: 61.8 us -> 35.7 us  [exchange(): lax.all_to_all(pieces, 'sector', split_axis=0, concat_axis=0, tiled=True)]
    all_to_all x2 -> x3, starting transfers between devices: 11.7 us -> 18.5 us  [exchange(): lax.all_to_all(pieces, 'sector', split_axis=0, concat_axis=0, tiled=True)]
    pallas_call x9 -> x11, Pallas kernels: 10 us -> 14.2 us  [call(): pl.pallas_call(kernel, out_shape=outs, in_specs=specs, out_specs=jax.tree...]
    unnamed x30 -> x16, local copies, waits for them, and re-layouts: 8.04 us -> 4.15 us
    ppermute x1, waiting for transfers between devices: 4.82 us -> 2.63 us  [per_device(): near = lax.ppermute(faces, 'radial', [(0, 1), (1, 0)])]
  transfers between devices with their start and end apart: 4 -> 5, of which waited for: 3 -> 5; matrix products, arithmetic and copies ran while one was open for 1% -> 1% of each run, Pallas kernels for 20% -> 8%
where the time goes in v3:
time: 118 us
  waiting for transfers between devices  38.5 us (33%)
  blocking collectives  35.7 us (30%)
  starting transfers between devices  21.6 us (18%)
  Pallas kernels  14.2 us (12%)
  local copies, waits for them, and re-layouts  5.86 us (5%)
    all_to_all x2, blocking collectives, exchange(): lax.all_to_all(pieces, 'sector', split_axis=0, concat_axis=0, tiled=True)  35.7 us
    all_to_all x3, waiting for transfers between devices, exchange(): lax.all_to_all(pieces, 'sector', split_axis=0, concat_axis=0, tiled=True)  33.7 us
    all_to_all x3, starting transfers between devices, exchange(): lax.all_to_all(pieces, 'sector', split_axis=0, concat_axis=0, tiled=True)  18.5 us
    pallas_call x11, Pallas kernels, call(): pl.pallas_call(kernel, out_shape=outs, in_specs=specs, out_specs=jax.tree...  14.2 us
    unnamed x16, local copies, waits for them, and re-layouts  4.15 us
    ppermute x1, waiting for transfers between devices, per_device(): near = lax.ppermute(faces, 'radial', [(0, 1), (1, 0)])  2.63 us
  transfers between devices with their start and end apart: 5, of which 5 were waited for; matrix products, arithmetic and copies ran while one was open for 1% of the time, Pallas kernels for 8%

profile of v3, /device:TPU:0, one launch (start us, length us, event | category | flops | bytes accessed | tf_op | source)
XLA Modules:
  0.0 117.6 jit_solution(15165271866946259101)
XLA Ops:
  0.0 1.1 copy-done.2
  1.1 1.2 %chunk.2 = bf16[16,2,48,256]{3,2,1,0:T(8,128)(2,1)} custom-call(f32[8,128]{1,0:T(8,128)S(1)} %broadcast_in_dim.43.token_ref, bf16[2,16,48,256]{3,2,1,0:T(8,128)(2,1)S(1)} %bitcast.22), custom_call_target="tpu_custom_call" | custom-call | tf_op jit(solution)/shard_map/chunk/pallas_call | solution.py:225
  2.4 7.4 %all-to-all-start = ((bf16[16,2,48,256]{3,2,1,0:T(8,128)(2,1)}), bf16[16,2,48,256]{3,2,1,0:T(8,128)(2,1)S(1)}, u32[]{:S(2)}, u32[]{:S(2)}) async-start(bf16[16,2,48,256]{3,2,1,0:T(8,128)(2,1)} %chunk.2), calls=%async_computation | async-start | bytes 1572864 | tf_op jit(solution)/shard_map/all_to_all | solution.py:252
  11.3 0.8 copy-done.4
  12.1 16.3 %all-to-all-done = bf16[16,2,48,256]{3,2,1,0:T(8,128)(2,1)S(1)} async-done(((bf16[16,2,48,256]{3,2,1,0:T(8,128)(2,1)}), bf16[16,2,48,256]{3,2,1,0:T(8,128)(2,1)S(1)}, u32[]{:S(2)}, u32[]{:S(2)}) %all-to-all-start) | async-done | bytes 786464 | tf_op jit(solution)/shard_map/all_to_all | solution.py:252
  28.4 1.5 %transform.1 = (bf16[32,48,256]{2,1,0:T(8,128)(2,1)}, f32[8,128]{1,0:T(8,128)S(1)}) custom-call(bf16[512,512]{1,0:T(8,128)(2,1)S(1)} %get-tuple-element.17.table_ref, bf16[32,48,256]{2,1,0:T(8,128)(2,1)S(1)} %bitcast.20), custom_call_target="tpu_custom_call" | custom-call | tf_op jit(solution)/shard_map/transform/pallas_call | solution.py:225
  29.9 5.7 %all-to-all-start.1 = ((bf16[16,2,48,256]{3,2,1,0:T(8,128)(2,1)}), bf16[16,2,48,256]{3,2,1,0:T(8,128)(2,1)}, u32[]{:S(2)}, u32[]{:S(2)}) async-start(bf16[16,2,48,256]{3,2,1,0:T(8,128)(2,1)} %bitcast.9), calls=%async_computation.1 | async-start | bytes 1572864 | tf_op jit(solution)/shard_map/all_to_all | solution.py:252
  35.6 1.3 %copy-done.3 = bf16[2,768,256]{2,1,0:T(8,128)(2,1)S(1)} copy-done((bf16[2,768,256]{2,1,0:T(8,128)(2,1)S(1)}, bf16[2,768,256]{2,1,0:T(8,128)(2,1)}, u32[]{:S(2)}) %copy-start.3) | copy-done | bytes 786456
  37.2 0.9 copy-done.1
  38.1 16.2 %all-to-all-done.1.x_ref = bf16[16,2,48,256]{3,2,1,0:T(8,128)(2,1)} async-done(((bf16[16,2,48,256]{3,2,1,0:T(8,128)(2,1)}), bf16[16,2,48,256]{3,2,1,0:T(8,128)(2,1)}, u32[]{:S(2)}, u32[]{:S(2)}) %all-to-all-start.1) | async-done | bytes 786464 | tf_op jit(solution)/shard_map/all_to_all | solution.py:252
  54.3 5.5 %all-to-all-start.3 = ((bf16[16,2,48,256]{3,2,1,0:T(8,128)(2,1)}), bf16[16,2,48,256]{3,2,1,0:T(8,128)(2,1)}, u32[]{:S(2)}, u32[]{:S(2)}) async-start(bf16[16,2,48,256]{3,2,1,0:T(8,128)(2,1)} %copy-done.1), calls=%async_computation.3 | async-start | bytes 1572864 | tf_op jit(solution)/shard_map/all_to_all | solution.py:252
  60.1 2.3 %faces.1 = (bf16[2,256,256]{2,1,0:T(8,128)(2,1)}, f32[8,128]{1,0:T(8,128)}) custom-call(s32[256,1]{1,0:T(8,128)S(1)} %copy.11.index_ref, bf16[16,2,48,256]{3,2,1,0:T(8,128)(2,1)} %all-to-all-done.1.x_ref), custom_call_target="tpu_custom_call" | custom-call | tf_op jit(solution)/shard_map/faces/pallas_call | solution.py:225
  62.3 1.5 %collective-permute-start = (bf16[2,256,256]{2,1,0:T(8,128)(2,1)}, bf16[2,256,256]{2,1,0:T(8,128)(2,1)S(1)}, u32[]{:S(2)}, u32[]{:S(2)}) collective-permute-start(bf16[2,256,256]{2,1,0:T(8,128)(2,1)} %get-tuple-element.21), channel_id=1, source_target_pairs={{0,1},{1,0},{2,3},{3,2},{4,5},{5,4},{6,7},{7,6},{8,9},{9,8},{10,11... | collective-permute-start | bytes 786440 | tf_op jit(solution)/shard_map/ppermute | solution.py:296
  65.1 0.9 prepare.1
  65.9 2.5 %own.1.own_ref = f32[768,512]{1,0:T(8,128)S(1)} custom-call(s32[1]{0:T(128)S(6)} %convert_element_type.49.paired_ref, bf16[2,768,1024]{2,1,0:T(8,128)(2,1)S(1)} %bitcast.19, bf16[16,2,48,256]{3,2,1,0:T(8,128)(2,1)} %all-to-all-done.1.x_ref), custom_call_target="tpu_custom_call" | custom-call | tf_op jit(solution)/shard_map/own/pallas_call | solution.py:225
  68.5 2.6 %collective-permute-done.near_ref = bf16[2,256,256]{2,1,0:T(8,128)(2,1)S(1)} collective-permute-done((bf16[2,256,256]{2,1,0:T(8,128)(2,1)}, bf16[2,256,256]{2,1,0:T(8,128)(2,1)S(1)}, u32[]{:S(2)}, u32[]{:S(2)}) %collective-permute-start) | collective-permute-done | bytes 262176 | tf_op jit(solution)/shard_map/ppermute | solution.py:296
  71.1 0.9 middle.1
  72.0 1.6 %collective-permute-start.1 = (bf16[128,512]{1,0:T(8,128)(2,1)S(1)}, bf16[128,512]{1,0:T(8,128)(2,1)S(1)}, u32[]{:S(2)}, u32[]{:S(2)}) collective-permute-start(bf16[128,512]{1,0:T(8,128)(2,1)S(1)} %get-tuple-element.23), channel_id=1, source_target_pairs={{0,1},{1,0},{2,3},{3,2},{4,5},{5,4},{6,7},{7,6},{8,9},{9,8},{10,11... | collective-permute-start | bytes 393224 | tf_op jit(solution)/shard_map/ppermute | solution.py:312
  73.5 1.4 %back.1.back_ref = f32[768,512]{1,0:T(8,128)S(1)} custom-call(s32[1]{0:T(128)S(6)} %convert_element_type.49.paired_ref, bf16[2,768,768]{2,1,0:T(8,128)(2,1)S(1)} %get-tuple-element.16.turned_ref, bf16[768,512]{1,0:T(8,128)(2,1)S(1)} %get-tuple-element.22.middle_ref), custom_call_target="tpu_custom_call" | custom-call | tf_op jit(solution)/shard_map/back/pallas_call | solution.py:225
  74.9 2.1 %collective-permute-done.1.got_ref = bf16[128,512]{1,0:T(8,128)(2,1)S(1)} collective-permute-done((bf16[128,512]{1,0:T(8,128)(2,1)S(1)}, bf16[128,512]{1,0:T(8,128)(2,1)S(1)}, u32[]{:S(2)}, u32[]{:S(2)}) %collective-permute-start.1) | collective-permute-done | bytes 131104 | tf_op jit(solution)/shard_map/ppermute | solution.py:312
  77.4 1.2 %all-to-all-done.3 = bf16[16,2,48,256]{3,2,1,0:T(8,128)(2,1)} async-done(((bf16[16,2,48,256]{3,2,1,0:T(8,128)(2,1)}), bf16[16,2,48,256]{3,2,1,0:T(8,128)(2,1)}, u32[]{:S(2)}, u32[]{:S(2)}) %all-to-all-start.3) | async-done | bytes 786464 | tf_op jit(solution)/shard_map/all_to_all | solution.py:252
  78.6 25.5 %all_to_all.25 = bf16[16,2,48,256]{3,2,1,0:T(8,128)(2,1)S(1)} all-to-all(bf16[16,2,48,256]{3,2,1,0:T(8,128)(2,1)S(1)} %finish.1), channel_id=1, replica_groups=mesh['sector'=16,'radial'=2] {'sector'}, dimensions={0} | all-to-all | bytes 1572864 | tf_op jit(solution)/shard_map/all_to_all | solution.py:252
  104.2 2.3 %respond.1 = f32[3,4,128]{2,1,0:T(4,128)S(1)} custom-call(bf16[512,512]{1,0:T(8,128)(2,1)S(1)} %copy-done.5, bf16[32,48,256]{2,1,0:T(8,128)(2,1)S(1)} %bitcast.21, bf16[32,48,256]{2,1,0:T(8,128)(2,1)} %bitcast.15.far_ref), custom_call_target="tpu_custom_call" | custom-call | tf_op jit(solution)/shard_map/respond/pallas_call | solution.py:225
  106.7 10.2 %all_to_all.26 = f32[16,2,48]{2,1,0:T(2,128)S(1)} all-to-all(f32[16,2,48]{2,1,0:T(2,128)S(1)} %reshape_reshape.3), channel_id=1, replica_groups=mesh['sector'=16,'radial'=2] {'sector'}, dimensions={0} | all-to-all | bytes 12288 | tf_op jit(solution)/shard_map/all_to_all | solution.py:252
  (32 shorter events, 3.8 us)
Async XLA Ops:
  0.0 9.8 %copy-start.6 = (s32[16]{0:T(128)S(1)}, s32[16]{0:T(128)}, u32[]{:S(2)}) copy-start(s32[16]{0:T(128)} %param.8) | copy-start | bytes 196
  0.0 1.1 copy-start.2
  2.4 26.1 %all-to-all-start = ((bf16[16,2,48,256]{3,2,1,0:T(8,128)(2,1)}), bf16[16,2,48,256]{3,2,1,0:T(8,128)(2,1)S(1)}, u32[]{:S(2)}, u32[]{:S(2)}) async-start(bf16[16,2,48,256]{3,2,1,0:T(8,128)(2,1)} %chunk.2), calls=%async_computation | async-start | bytes 1572864 | tf_op jit(solution)/shard_map/all_to_all | solution.py:252
  11.3 0.8 copy-start.4
  29.9 30.0 %copy-start.7 = (s32[1,2,128]{2,1,0:T(2,128)S(1)}, s32[1,2,128]{2,1,0:T(2,128)}, u32[]{:S(2)}) copy-start(s32[1,2,128]{2,1,0:T(2,128)} %param.9) | copy-start | bytes 3076
  29.9 24.4 %all-to-all-start.1 = ((bf16[16,2,48,256]{3,2,1,0:T(8,128)(2,1)}), bf16[16,2,48,256]{3,2,1,0:T(8,128)(2,1)}, u32[]{:S(2)}, u32[]{:S(2)}) async-start(bf16[16,2,48,256]{3,2,1,0:T(8,128)(2,1)} %bitcast.9), calls=%async_computation.1 | async-start | bytes 1572864 | tf_op jit(solution)/shard_map/all_to_all | solution.py:252
  35.6 29.5 %copy-start = (bf16[1,2,768,1024]{3,2,1,0:T(8,128)(2,1)S(1)}, bf16[1,2,768,1024]{3,2,1,0:T(8,128)(2,1)}, u32[]{:S(2)}) copy-start(bf16[1,2,768,1024]{3,2,1,0:T(8,128)(2,1)} %param.7) | copy-start | bytes 9437188
  35.6 1.3 %copy-start.3 = (bf16[2,768,256]{2,1,0:T(8,128)(2,1)S(1)}, bf16[2,768,256]{2,1,0:T(8,128)(2,1)}, u32[]{:S(2)}) copy-start(bf16[2,768,256]{2,1,0:T(8,128)(2,1)} %param.6) | copy-start | bytes 2359300
  37.2 0.9 copy-start.1
  54.3 24.3 %all-to-all-start.3 = ((bf16[16,2,48,256]{3,2,1,0:T(8,128)(2,1)}), bf16[16,2,48,256]{3,2,1,0:T(8,128)(2,1)}, u32[]{:S(2)}, u32[]{:S(2)}) async-start(bf16[16,2,48,256]{3,2,1,0:T(8,128)(2,1)} %copy-done.1), calls=%async_computation.3 | async-start | bytes 1572864 | tf_op jit(solution)/shard_map/all_to_all | solution.py:252
  62.3 8.8 %collective-permute-start = (bf16[2,256,256]{2,1,0:T(8,128)(2,1)}, bf16[2,256,256]{2,1,0:T(8,128)(2,1)S(1)}, u32[]{:S(2)}, u32[]{:S(2)}) collective-permute-start(bf16[2,256,256]{2,1,0:T(8,128)(2,1)} %get-tuple-element.21), channel_id=1, source_target_pairs={{0,1},{1,0},{2,3},{3,2},{4,5},{5,4},{6,7},{7,6},{8,9},{9,8},{10,11... | collective-permute-start | bytes 786440 | tf_op jit(solution)/shard_map/ppermute | solution.py:296
  72.0 5.1 %collective-permute-start.1 = (bf16[128,512]{1,0:T(8,128)(2,1)S(1)}, bf16[128,512]{1,0:T(8,128)(2,1)S(1)}, u32[]{:S(2)}, u32[]{:S(2)}) collective-permute-start(bf16[128,512]{1,0:T(8,128)(2,1)S(1)} %get-tuple-element.23), channel_id=1, source_target_pairs={{0,1},{1,0},{2,3},{3,2},{4,5},{5,4},{6,7},{7,6},{8,9},{9,8},{10,11... | collective-permute-start | bytes 393224 | tf_op jit(solution)/shard_map/ppermute | solution.py:312
  74.9 29.2 %copy-start.5 = (bf16[512,512]{1,0:T(8,128)(2,1)S(1)}, bf16[512,512]{1,0:T(8,128)(2,1)}, u32[]{:S(2)}) copy-start(bf16[512,512]{1,0:T(8,128)(2,1)} %copy-done.4) | copy-start | bytes 1572868

commit v4 on v2

--- a/solution.py
+++ b/solution.py
@@ -12,6 +12,7 @@
 VMEM = pl.BlockSpec(memory_space=pltpu.VMEM)
 SMEM = pl.BlockSpec(memory_space=pltpu.SMEM)
 ANY = pl.BlockSpec(memory_space=pl.ANY)
+HBM = pl.BlockSpec(memory_space=pltpu.HBM)
 TILE = 16
 
 
@@ -36,38 +37,61 @@
     return jnp.dot(a, b, preferred_element_type=F32)
 
 
-def transform_kernel(table_ref, x_ref, out_ref):
+def tiles(rows):
+    return [slice(start, start + TILE) for start in range(0, rows, TILE)]
+
+
+def transform_kernel(table_ref, x_ref, *refs):
+    out_ref, held_ref, sems = refs[-3:]
     count, rows, width = x_ref.shape
-    for start in range(0, rows, TILE):
-        tile = x_ref[:, start : start + TILE, :].reshape(count * TILE, width)
-        out_ref[:, start : start + TILE, :] = (
-            dot(table_ref[...], tile).astype(BF16).reshape(count, TILE, width)
-        )
-
-
-def transform(table, pieces):
-    rows = pieces.shape[1]
+    copies = []
+    for index, span in enumerate(tiles(rows)):
+        tile = x_ref[:, span, :].reshape(count * TILE, width)
+        held_ref[index] = dot(table_ref[...], tile).astype(BF16).reshape(count, TILE, width)
+        for part in range(2):
+            half = slice(part * count // 2, (part + 1) * count // 2)
+            copies.append(
+                pltpu.make_async_copy(held_ref.at[index, half], out_ref.at[half, span], sems.at[index, part])
+            )
+            copies[-1].start()
+    for copy in copies:
+        copy.wait()
+
+
+def transform(table, pieces, after):
+    count, rows, width = pieces.shape
     if rows % TILE:
         return jnp.einsum("ks,sdr->kdr", table, pieces, preferred_element_type=F32).astype(BF16)
+    steps = rows // TILE
     return call(
-        transform_kernel, jax.ShapeDtypeStruct(pieces.shape, BF16), [VMEM, VMEM], "transform", 8, table, pieces
-    )
+        transform_kernel, jax.ShapeDtypeStruct(pieces.shape, BF16), [VMEM, VMEM] + [ANY] * len(after), "transform", 8,
+        table, pieces, *after, out_spaces=[pltpu.HBM],
+        scratch=(pltpu.VMEM((steps, count, TILE, width), BF16), pltpu.SemaphoreType.DMA((steps, 2))),
+    )
+
+
+def stage_kernel(x_ref, out_ref, sems):
+    step = x_ref.shape[0] // sems.shape[0]
+    copies = []
+    for j in range(sems.shape[0]):
+        span = slice(j * step, (j + 1) * step)
+        copies.append(pltpu.make_async_copy(x_ref.at[span], out_ref.at[span], sems.at[j]))
+        copies[-1].start()
+    for copy in copies:
+        copy.wait()
 
 
 def respond_kernel(table_ref, x_ref, state_ref, out_ref):
     count, rows, width = x_ref.shape
     lanes = 128
-    ones = jnp.ones((width, lanes), BF16)
     place = lax.broadcasted_iota(jnp.int32, (count * TILE, lanes), 0) % lanes
     diagonal = place == lax.broadcasted_iota(jnp.int32, (count * TILE, lanes), 1)
-    for index, start in enumerate(range(0, rows, TILE)):
-        tile = x_ref[:, start : start + TILE, :].reshape(count * TILE, width)
+    for index, span in enumerate(tiles(rows)):
+        tile = x_ref[:, span, :].reshape(count * TILE, width)
         adjoint = dot(table_ref[...], tile).astype(BF16).astype(F32)
-        state = state_ref[:, start : start + TILE, :].reshape(count * TILE, width).astype(F32)
-        product = adjoint * state
-        high = product.astype(BF16)
-        low = (product - high.astype(F32)).astype(BF16)
-        total = jnp.where(diagonal, dot(high, ones) + dot(low, ones), 0.0)
+        state = state_ref[:, span, :].reshape(count * TILE, width).astype(F32)
+        total = jnp.sum(adjoint * state, axis=1, keepdims=True)
+        total = jnp.where(diagonal, total, 0.0)
         out_ref[index] = jnp.sum(total.reshape(count * TILE // lanes, lanes, lanes), axis=1)
 
 
@@ -88,13 +112,34 @@
     return x_ref[:, part].reshape(chunks * rows, width)
 
 
-def faces_kernel(index_ref, x_ref, out_ref):
-    count = index_ref.shape[0]
-    cycle = x_ref.shape[0] * x_ref.shape[2]
-    pick = index_ref[...] == lax.broadcasted_iota(jnp.int32, (count, cycle), 1)
+def fetch(x_ref, held_ref, sems):
+    chunks, pieces = x_ref.shape[0], sems.shape[0]
+    step = chunks // pieces
+    copies = []
+    for j in range(pieces):
+        span = slice(j * step, (j + 1) * step)
+        copies.append(pltpu.make_async_copy(x_ref.at[span], held_ref.at[span], sems.at[j]))
+        copies[-1].start()
+    return copies
+
+
+def fetch_scratch(array):
+    return pltpu.VMEM(array.shape, array.dtype), pltpu.SemaphoreType.DMA((math.gcd(array.shape[0], 8),))
+
+
+def faces_kernel(index_ref, x_ref, out_ref, held_ref, sems):
+    copies = fetch(x_ref, held_ref, sems)
+    chunks, _, rows, width = x_ref.shape
+    count = index_ref.shape[1]
+    square = (count, count)
+    diagonal = lax.broadcasted_iota(jnp.int32, square, 0) == lax.broadcasted_iota(jnp.int32, square, 1)
+    column = jnp.sum(jnp.where(diagonal, index_ref[...].astype(F32), 0.0), axis=1, keepdims=True)
+    pick = column.astype(jnp.int32) == lax.broadcasted_iota(jnp.int32, (count, chunks * rows), 1)
     pick = jnp.where(pick, 1.0, 0.0).astype(BF16)
+    for copy in copies:
+        copy.wait()
     for part in range(2):
-        out_ref[part] = dot(pick, rows_of(x_ref, part)).astype(BF16)
+        out_ref[part] = dot(pick, rows_of(held_ref, part)).astype(BF16)
 
 
 def widen(table):
@@ -134,10 +179,15 @@
 
 
 def chunk_kernel(x_ref, out_ref, sems):
-    local = x_ref.shape[0]
-    copies = [pltpu.make_async_copy(x_ref.at[i], out_ref.at[:, i], sems.at[i]) for i in range(local)]
-    for copy in copies:
-        copy.start()
+    local, devices = x_ref.shape[:2]
+    count = sems.shape[0]
+    step = devices // count
+    copies = []
+    for j in range(count):
+        span = slice(j * step, (j + 1) * step)
+        for i in range(local):
+            copies.append(pltpu.make_async_copy(x_ref.at[i, span], out_ref.at[span, i], sems.at[j, i]))
+            copies[-1].start()
     for copy in copies:
         copy.wait()
 
@@ -146,16 +196,40 @@
     local, cycle, width = block.shape
     rows = cycle // devices
     split = block.reshape(local, devices, rows, width)
-    if rows % TILE:
+    if rows % TILE or devices % 4:
         return split.transpose(1, 0, 2, 3)
-    return pl.pallas_call(
-        chunk_kernel,
-        out_shape=jax.ShapeDtypeStruct((devices, local, rows, width), block.dtype),
-        in_specs=[ANY],
-        out_specs=ANY,
-        scratch_shapes=[pltpu.SemaphoreType.DMA((local,))],
-        name="chunk",
-    )(split)
+    out = jax.ShapeDtypeStruct((devices, local, rows, width), block.dtype)
+    return call(
+        chunk_kernel, out, [HBM], "chunk", 8, split,
+        scratch=(pltpu.SemaphoreType.DMA((4, local)),),
+    )
+
+
+GROUP = 4
+
+
+def near_kernel(me_ref, x_ref, *refs):
+    *outs, sems = refs
+    copies = []
+    for k in range(GROUP):
+        member = me_ref[0] ^ k
+        copies.append(pltpu.make_async_copy(x_ref.at[:, :, member], outs[k], sems.at[k]))
+        copies[-1].start()
+    for copy in copies:
+        copy.wait()
+
+
+def far_kernel(me_ref, *refs):
+    blocks, out_ref, sems = refs[:GROUP], refs[GROUP], refs[GROUP + 1]
+    local = blocks[0].shape[0]
+    copies = []
+    for j, block in enumerate(blocks):
+        member = me_ref[0] ^ j
+        for i in range(local):
+            copies.append(pltpu.make_async_copy(block.at[i], out_ref.at[:, member * local + i], sems.at[j, i]))
+            copies[-1].start()
+    for copy in copies:
+        copy.wait()
 
 
 def right_sides(real, imag, paired):
@@ -166,9 +240,11 @@
     return upper, lower
 
 
-def own_kernel(paired_ref, weight_ref, x_ref, out_ref):
+def own_kernel(paired_ref, weight_ref, x_ref, out_ref, held_ref, sems):
     cycle = weight_ref.shape[1]
-    upper, lower = right_sides(rows_of(x_ref, 0), rows_of(x_ref, 1), paired_ref[0] != 0)
+    for copy in fetch(x_ref, held_ref, sems):
+        copy.wait()
+    upper, lower = right_sides(rows_of(held_ref, 0), rows_of(held_ref, 1), paired_ref[0] != 0)
     out_ref[...] = dot(weight_ref[0, :, :cycle], upper) + dot(weight_ref[1, :, :cycle], lower)
 
 
@@ -209,15 +285,25 @@
         out_ref[:, part] = total[:, part * width : (part + 1) * width].reshape(chunks, rows, width)
 
 
-def call(kernel, outs, specs, name, mebibytes, *operands):
-    return pl.pallas_call(
+def placed(operand, spec):
+    space = spec.memory_space
+    return pltpu.with_memory_space_constraint(operand, space) if space in (pltpu.VMEM, pltpu.HBM) else operand
+
+
+def call(kernel, outs, specs, name, mebibytes, *operands, scratch=(), out_spaces=None):
+    single = not isinstance(outs, (list, tuple))
+    shapes = [outs] if single else list(outs)
+    spaces = out_spaces or [pltpu.VMEM] * len(shapes)
+    results = pl.pallas_call(
         kernel,
-        out_shape=outs,
+        out_shape=[space(out.shape, out.dtype) for out, space in zip(shapes, spaces)],
         in_specs=specs,
-        out_specs=jax.tree.map(lambda _: VMEM, outs),
+        out_specs=[pl.BlockSpec(memory_space=space) for space in spaces],
+        scratch_shapes=scratch,
         compiler_params=pltpu.CompilerParams(vmem_limit_bytes=mebibytes * 1024 * 1024),
         name=name,
-    )(*operands)
+    )(*(placed(operand, spec) for operand, spec in zip(operands, specs)))
+    return results[0] if single else list(results)
 
 
 def per_device(loads, state, factors, assign, iface):
@@ -250,7 +336,7 @@
     else:
         sent = gathered = jnp.concatenate([inner, outer])
         scattered = jnp.concatenate([outer, inner])
-    sent = sent.reshape(-1, 1)
+    sent = sent.reshape(1, -1)
     scattered = scattered.reshape(1, -1)
     edges = gathered.shape[0]
 
@@ -265,25 +351,52 @@
     if aligned:
         wide = shape((sectors * TILE, sectors * TILE), BF16)
         forward, inverse = call(widen_kernel, (wide, wide), [VMEM, VMEM], "widen", 12, forward, inverse)
-    state = by_chunk(state, devices)
-    ready = (pieces, edge, turned, outward, forward, inverse, state, sent, scattered, paired)
-    pieces, edge, turned, outward, forward, inverse, state, sent, scattered, paired = (
-        lax.optimization_barrier(ready)
-    )
-
-    spectrum = transform(forward, pieces)
+    groups = devices // GROUP
+    by_groups = aligned and devices == groups * GROUP and groups > 1
+    place = lax.axis_index("sector")
+    member = (place % GROUP).astype(jnp.int32).reshape(1)
+    group = (place // GROUP).astype(jnp.int32).reshape(1)
+    blocks = []
+    if by_groups:
+        block = shape((local, groups, rows, width), BF16)
+        blocks = call(
+            near_kernel, [block] * GROUP, [SMEM, HBM], "near", 8,
+            member, state.reshape(local, groups, GROUP, rows, width),
+            scratch=(pltpu.SemaphoreType.DMA((GROUP,)),),
+        )
+        blocks = [
+            lax.ppermute(block, "sector", [(i, i ^ k) for i in range(devices)]) if k else block
+            for k, block in enumerate(blocks)
+        ]
+
+    spectrum = transform(forward, pieces, blocks[1:])
+    if by_groups:
+        state = call(
+            far_kernel, shape((groups, GROUP * local, rows, width), BF16), [SMEM] + [ANY] * GROUP, "far", 8,
+            member, *blocks, scratch=(pltpu.SemaphoreType.DMA((GROUP, local)),),
+        )
     harmonic = exchange(spectrum.reshape(devices, 2, rows, width))
-
-    harmonic, state = lax.optimization_barrier((harmonic, state))
-    state = exchange(state).reshape(sectors, rows, width)
 
     if not aligned:
         harmonic = harmonic.transpose(1, 0, 2, 3).reshape(1, 2, cycle, width)
     faces = call(
-        faces_kernel, shape((2, 2 * face, width), BF16), [VMEM, VMEM], "faces", 8, sent, harmonic,
-    )
+        faces_kernel, shape((2, 2 * face, width), BF16), [VMEM, HBM], "faces", 8,
+        sent, harmonic, scratch=fetch_scratch(harmonic),
+    )
+    if by_groups:
+        members = [[GROUP * z + i for z in range(groups)] for i in range(GROUP)]
+        state = lax.all_to_all(
+            state, "sector", split_axis=0, concat_axis=0, tiled=True, axis_index_groups=members
+        ).reshape(sectors, rows, width)
+        state = call(
+            stage_kernel, shape(state.shape, BF16), [HBM], "stage", 8, state,
+            scratch=(pltpu.SemaphoreType.DMA((4,)),),
+        )
+    else:
+        state = exchange(by_chunk(state, devices)).reshape(sectors, rows, width)
     own = call(
-        own_kernel, shape((cycle, 2 * width), F32), [SMEM, VMEM, VMEM], "own", 12, paired, weight, harmonic
+        own_kernel, shape((cycle, 2 * width), F32), [SMEM, VMEM, HBM], "own", 12, paired, weight, harmonic,
+        scratch=fetch_scratch(harmonic),
     )
     if cycles == 2:
         near = lax.ppermute(faces, "radial", [(0, 1), (1, 0)])

time: 157 us -> 116 us (0.74)
  blocking collectives: 61.8 us -> 11.8 us
  waiting for transfers between devices: 8.69 us -> 52.7 us
  Pallas kernels: 59.9 us -> 17.2 us
  starting transfers between devices: 14.9 us -> 26.2 us
  local copies, waits for them, and re-layouts: 9.75 us -> 5.99 us
    all_to_all x3 -> x1, blocking collectives: 61.8 us -> 11.8 us  [exchange(): lax.all_to_all(pieces, 'sector', split_axis=0, concat_axis=0, tiled=True)]
    pallas_call x11 -> x13, Pallas kernels: 59.9 us -> 17.2 us  [call(): pl.pallas_call(kernel, out_shape=[space(out.shape, out.dtype) for out, sp...]
    all_to_all x2 -> x3, waiting for transfers between devices: 1.46 us -> 32.9 us  [exchange(): lax.all_to_all(pieces, 'sector', split_axis=0, concat_axis=0, tiled=True)]
    ppermute x0 -> x3, waiting for transfers between devices: none -> 13.1 us  [per_device(): lax.ppermute(block, 'sector', [(i, i ^ k) for i in range(devices)])]
    all_to_all x0 -> x1, starting transfers between devices: none -> 4.95 us  [per_device(): lax.all_to_all(state, 'sector', split_axis=0, concat_axis=0, tiled=True,...]
    all_to_all x2 -> x3, starting transfers between devices: 11.7 us -> 16 us  [exchange(): lax.all_to_all(pieces, 'sector', split_axis=0, concat_axis=0, tiled=True)]
    unnamed x30 -> x20, local copies, waits for them, and re-layouts: 8.04 us -> 4.42 us
    ppermute x1, waiting for transfers between devices: 4.82 us -> 1.66 us  [per_device(): near = lax.ppermute(faces, 'radial', [(0, 1), (1, 0)])]
  transfers between devices with their start and end apart: 4 -> 9, of which waited for: 3 -> 7; matrix products, arithmetic and copies ran while one was open for 1% -> 1% of each run, Pallas kernels for 20% -> 11%
where the time goes in v4:
time: 116 us
  waiting for transfers between devices  52.7 us (45%)
  starting transfers between devices  26.2 us (23%)
  Pallas kernels  17.2 us (15%)
  blocking collectives  11.8 us (10%)
  local copies, waits for them, and re-layouts  5.99 us (5%)
    all_to_all x3, waiting for transfers between devices, exchange(): lax.all_to_all(pieces, 'sector', split_axis=0, concat_axis=0, tiled=True)  32.9 us
    pallas_call x13, Pallas kernels, call(): pl.pallas_call(kernel, out_shape=[space(out.shape, out.dtype) for out, sp...  17.2 us
    all_to_all x3, starting transfers between devices, exchange(): lax.all_to_all(pieces, 'sector', split_axis=0, concat_axis=0, tiled=True)  16 us
    ppermute x3, waiting for transfers between devices, per_device(): lax.ppermute(block, 'sector', [(i, i ^ k) for i in range(devices)])  13.1 us
    all_to_all x1, blocking collectives, exchange(): lax.all_to_all(pieces, 'sector', split_axis=0, concat_axis=0, tiled=True)  11.8 us
    all_to_all x1, starting transfers between devices, per_device(): lax.all_to_all(state, 'sector', split_axis=0, concat_axis=0, tiled=True,...  4.95 us
    unnamed x20, local copies, waits for them, and re-layouts  4.42 us
    all_to_all x1, waiting for transfers between devices, per_device(): lax.all_to_all(state, 'sector', split_axis=0, concat_axis=0, tiled=True,...  3.01 us
  transfers between devices with their start and end apart: 9, of which 7 were waited for; matrix products, arithmetic and copies ran while one was open for 1% of the time, Pallas kernels for 11%

profile of v4, /device:TPU:0, one launch (start us, length us, event | category | flops | bytes accessed | tf_op | source)
XLA Modules:
  0.0 115.6 jit_solution(16329651626950483387)
XLA Ops:
  0.0 2.2 %chunk.1 = bf16[16,2,48,256]{3,2,1,0:T(8,128)(2,1)} custom-call(bf16[2,16,48,256]{3,2,1,0:T(8,128)(2,1)} %bitcast.31), custom_call_target="tpu_custom_call" | custom-call | tf_op jit(solution)/shard_map/chunk/pallas_call | solution.py:297
  2.2 7.4 %all-to-all-start = ((bf16[16,2,48,256]{3,2,1,0:T(8,128)(2,1)}), bf16[16,2,48,256]{3,2,1,0:T(8,128)(2,1)S(1)}, u32[]{:S(2)}, u32[]{:S(2)}) async-start(bf16[16,2,48,256]{3,2,1,0:T(8,128)(2,1)} %chunk.1), calls=%async_computation | async-start | bytes 1572864 | tf_op jit(solution)/shard_map/all_to_all | solution.py:325
  9.6 1.3 %near.1 = (bf16[2,4,48,256]{3,2,1,0:T(8,128)(2,1)S(1)}, bf16[2,4,48,256]{3,2,1,0:T(8,128)(2,1)S(1)}, bf16[2,4,48,256]{3,2,1,0:T(8,128)(2,1)S(1)}, bf16[2,4,48,256]{3,2,1,0:T(8,128)(2,1)S(1)}) custom-call(s32[1]{0:T(128)} %bitcast.9.me_ref, bf16[2,4,4,48,256]{4,3,2,1,0:T(8,128)(2,1)} %bitcast.32), custom_call_target="tpu_custom_call" | custom-call | tf_op jit(solution)/shard_map/near/pallas_call | solution.py:297
  11.9 1.7 %collective-permute-start.1 = (bf16[2,4,48,256]{3,2,1,0:T(8,128)(2,1)S(1)}, bf16[2,4,48,256]{3,2,1,0:T(8,128)(2,1)S(1)}, u32[]{:S(2)}, u32[]{:S(2)}) collective-permute-start(bf16[2,4,48,256]{3,2,1,0:T(8,128)(2,1)S(1)} %get-tuple-element.20), channel_id=1, source_target_pairs={{0,4},{2,6},{4,0},{6,2},{8,12},{10,14},{12,8},{14,10},{16,20},{18,... | collective-permute-start | bytes 589832 | tf_op jit(solution)/shard_map/ppermute | solution.py:368
  16.0 7.7 %collective-permute-done.1.refs_1_.refs_2_ = bf16[2,4,48,256]{3,2,1,0:T(8,128)(2,1)S(1)} collective-permute-done((bf16[2,4,48,256]{3,2,1,0:T(8,128)(2,1)S(1)}, bf16[2,4,48,256]{3,2,1,0:T(8,128)(2,1)S(1)}, u32[]{:S(2)}, u32[]{:S(2)}) %collective-permute-start.1) | collective-permute-done | bytes 196640 | tf_op jit(solution)/shard_map/ppermute | solution.py:368
  23.7 5.4 %collective-permute-done.2.refs_2_.refs_3_ = bf16[2,4,48,256]{3,2,1,0:T(8,128)(2,1)S(1)} collective-permute-done((bf16[2,4,48,256]{3,2,1,0:T(8,128)(2,1)S(1)}, bf16[2,4,48,256]{3,2,1,0:T(8,128)(2,1)S(1)}, u32[]{:S(2)}, u32[]{:S(2)}) %collective-permute-start.2) | collective-permute-done | bytes 196640 | tf_op jit(solution)/shard_map/ppermute | solution.py:368
  29.1 1.4 %transform.1 = bf16[32,48,256]{2,1,0:T(8,128)(2,1)} custom-call(bf16[512,512]{1,0:T(8,128)(2,1)S(1)} %get-tuple-element.18.table_ref, bf16[32,48,256]{2,1,0:T(8,128)(2,1)S(1)} %bitcast.22, bf16[2,4,48,256]{3,2,1,0:T(8,128)(2,1)S(1)} %collective-permute-done.refs_0_.refs_1_, bf16[2,4,48,256]{3,2,1,0:T(8,128)(2,1)S(1)} %collective-permute-done.1.refs_1_.refs_2_, ...), custom_call_target="tpu_custom_call" | custom-call | tf_op jit(solution)/shard_map/transform/pallas_call | solution.py:297
  30.5 4.7 %all-to-all-start.1 = ((bf16[16,2,48,256]{3,2,1,0:T(8,128)(2,1)}), bf16[16,2,48,256]{3,2,1,0:T(8,128)(2,1)}, u32[]{:S(2)}, u32[]{:S(2)}) async-start(bf16[16,2,48,256]{3,2,1,0:T(8,128)(2,1)} %bitcast.30), calls=%async_computation.1 | async-start | bytes 1572864 | tf_op jit(solution)/shard_map/all_to_all | solution.py:325
  35.3 1.1 copy-done.3
  38.6 15.5 %all-to-all-done.1.x_ref = bf16[16,2,48,256]{3,2,1,0:T(8,128)(2,1)} async-done(((bf16[16,2,48,256]{3,2,1,0:T(8,128)(2,1)}), bf16[16,2,48,256]{3,2,1,0:T(8,128)(2,1)}, u32[]{:S(2)}, u32[]{:S(2)}) %all-to-all-start.1) | async-done | bytes 786464 | tf_op jit(solution)/shard_map/all_to_all | solution.py:325
  54.1 4.9 %all-to-all-start.3 = ((bf16[4,8,48,256]{3,2,1,0:T(8,128)(2,1)}), bf16[4,8,48,256]{3,2,1,0:T(8,128)(2,1)}, u32[]{:S(2)}, u32[]{:S(2)}) async-start(bf16[4,8,48,256]{3,2,1,0:T(8,128)(2,1)} %copy-done.1), calls=%async_computation.3 | async-start | bytes 1572864 | tf_op jit(solution)/shard_map/all_to_all | solution.py:388
  59.0 2.4 %faces.1 = bf16[2,256,256]{2,1,0:T(8,128)(2,1)} custom-call(s32[1,256]{1,0:T(1,128)S(1)} %bitcast.29, bf16[16,2,48,256]{3,2,1,0:T(8,128)(2,1)} %all-to-all-done.1.x_ref), custom_call_target="tpu_custom_call" | custom-call | tf_op jit(solution)/shard_map/faces/pallas_call | solution.py:297
  61.4 1.6 %collective-permute-start.3 = (bf16[2,256,256]{2,1,0:T(8,128)(2,1)}, bf16[2,256,256]{2,1,0:T(8,128)(2,1)S(1)}, u32[]{:S(2)}, u32[]{:S(2)}) collective-permute-start(bf16[2,256,256]{2,1,0:T(8,128)(2,1)} %faces.1), channel_id=1, source_target_pairs={{0,1},{1,0},{2,3},{3,2},{4,5},{5,4},{6,7},{7,6},{8,9},{9,8},{10,11... | collective-permute-start | bytes 786440 | tf_op jit(solution)/shard_map/ppermute | solution.py:402
  65.1 2.7 %own.1.own_ref = f32[768,512]{1,0:T(8,128)S(1)} custom-call(s32[1]{0:T(128)S(6)} %convert_element_type.49.paired_ref, bf16[2,768,1024]{2,1,0:T(8,128)(2,1)S(1)} %bitcast.20, bf16[16,2,48,256]{3,2,1,0:T(8,128)(2,1)} %all-to-all-done.1.x_ref), custom_call_target="tpu_custom_call" | custom-call | tf_op jit(solution)/shard_map/own/pallas_call | solution.py:297
  67.8 1.7 %collective-permute-done.3.near_ref = bf16[2,256,256]{2,1,0:T(8,128)(2,1)S(1)} collective-permute-done((bf16[2,256,256]{2,1,0:T(8,128)(2,1)}, bf16[2,256,256]{2,1,0:T(8,128)(2,1)S(1)}, u32[]{:S(2)}, u32[]{:S(2)}) %collective-permute-start.3) | collective-permute-done | bytes 262176 | tf_op jit(solution)/shard_map/ppermute | solution.py:402
  70.3 1.6 %collective-permute-start.4 = (bf16[128,512]{1,0:T(8,128)(2,1)S(1)}, bf16[128,512]{1,0:T(8,128)(2,1)S(1)}, u32[]{:S(2)}, u32[]{:S(2)}) collective-permute-start(bf16[128,512]{1,0:T(8,128)(2,1)S(1)} %get-tuple-element.25), channel_id=1, source_target_pairs={{0,1},{1,0},{2,3},{3,2},{4,5},{5,4},{6,7},{7,6},{8,9},{9,8},{10,11... | collective-permute-start | bytes 393224 | tf_op jit(solution)/shard_map/ppermute | solution.py:418
  71.9 1.4 %back.1.back_ref = f32[768,512]{1,0:T(8,128)S(1)} custom-call(s32[1]{0:T(128)S(6)} %convert_element_type.49.paired_ref, bf16[2,768,768]{2,1,0:T(8,128)(2,1)S(1)} %get-tuple-element.17.turned_ref, bf16[768,512]{1,0:T(8,128)(2,1)S(1)} %get-tuple-element.24.middle_ref), custom_call_target="tpu_custom_call" | custom-call | tf_op jit(solution)/shard_map/back/pallas_call | solution.py:297
  73.2 2.1 %collective-permute-done.4.got_ref = bf16[128,512]{1,0:T(8,128)(2,1)S(1)} collective-permute-done((bf16[128,512]{1,0:T(8,128)(2,1)S(1)}, bf16[128,512]{1,0:T(8,128)(2,1)S(1)}, u32[]{:S(2)}, u32[]{:S(2)}) %collective-permute-start.4) | collective-permute-done | bytes 131104 | tf_op jit(solution)/shard_map/ppermute | solution.py:418
  75.3 1.2 %finish.1 = bf16[16,2,48,256]{3,2,1,0:T(8,128)(2,1)} custom-call(s32[1,128]{1,0:T(1,128)S(1)} %bitcast.28, f32[768,512]{1,0:T(8,128)S(1)} %back.1.back_ref, bf16[128,512]{1,0:T(8,128)(2,1)S(1)} %collective-permute-done.4.got_ref), custom_call_target="tpu_custom_call" | custom-call | tf_op jit(solution)/shard_map/finish/pallas_call | solution.py:297
  76.6 3.0 %all-to-all-done.3 = bf16[4,8,48,256]{3,2,1,0:T(8,128)(2,1)} async-done(((bf16[4,8,48,256]{3,2,1,0:T(8,128)(2,1)}), bf16[4,8,48,256]{3,2,1,0:T(8,128)(2,1)}, u32[]{:S(2)}, u32[]{:S(2)}) %all-to-all-start.3) | async-done | bytes 786464 | tf_op jit(solution)/shard_map/all_to_all | solution.py:388
  79.6 3.9 %all-to-all-start.2 = ((bf16[16,2,48,256]{3,2,1,0:T(8,128)(2,1)}), bf16[16,2,48,256]{3,2,1,0:T(8,128)(2,1)S(1)}, u32[]{:S(2)}, u32[]{:S(2)}) async-start(bf16[16,2,48,256]{3,2,1,0:T(8,128)(2,1)} %finish.1), calls=%async_computation.2 | async-start | bytes 1572864 | tf_op jit(solution)/shard_map/all_to_all | solution.py:325
  83.5 1.3 %stage.1.state_ref = bf16[32,48,256]{2,1,0:T(8,128)(2,1)S(1)} custom-call(bf16[32,48,256]{2,1,0:T(8,128)(2,1)} %bitcast.16.x_ref), custom_call_target="tpu_custom_call" | custom-call | tf_op jit(solution)/shard_map/stage/pallas_call | solution.py:297
  84.7 17.4 %all-to-all-done.2 = bf16[16,2,48,256]{3,2,1,0:T(8,128)(2,1)S(1)} async-done(((bf16[16,2,48,256]{3,2,1,0:T(8,128)(2,1)}), bf16[16,2,48,256]{3,2,1,0:T(8,128)(2,1)S(1)}, u32[]{:S(2)}, u32[]{:S(2)}) %all-to-all-start.2) | async-done | bytes 786464 | tf_op jit(solution)/shard_map/all_to_all | solution.py:325
  103.1 11.8 %all_to_all.25 = f32[16,2,48]{2,1,0:T(2,128)S(1)} all-to-all(f32[16,2,48]{2,1,0:T(2,128)S(1)} %reshape_reshape.3), channel_id=1, replica_groups=mesh['sector'=16,'radial'=2] {'sector'}, dimensions={0} | all-to-all | bytes 12288 | tf_op jit(solution)/shard_map/all_to_all | solution.py:325
  (43 shorter events, 9.5 us)
Async XLA Ops:
  0.0 13.6 %copy-start.8 = (s32[16]{0:T(128)S(1)}, s32[16]{0:T(128)}, u32[]{:S(2)}) copy-start(s32[16]{0:T(128)} %param.8) | copy-start | bytes 196
  2.2 26.9 %all-to-all-start = ((bf16[16,2,48,256]{3,2,1,0:T(8,128)(2,1)}), bf16[16,2,48,256]{3,2,1,0:T(8,128)(2,1)S(1)}, u32[]{:S(2)}, u32[]{:S(2)}) async-start(bf16[16,2,48,256]{3,2,1,0:T(8,128)(2,1)} %chunk.1), calls=%async_computation | async-start | bytes 1572864 | tf_op jit(solution)/shard_map/all_to_all | solution.py:325
  10.8 0.7 copy-start.6
  11.5 4.5 %collective-permute-start = (bf16[2,4,48,256]{3,2,1,0:T(8,128)(2,1)S(1)}, bf16[2,4,48,256]{3,2,1,0:T(8,128)(2,1)S(1)}, u32[]{:S(2)}, u32[]{:S(2)}) collective-permute-start(bf16[2,4,48,256]{3,2,1,0:T(8,128)(2,1)S(1)} %get-tuple-element.19), channel_id=1, source_target_pairs={{0,2},{2,0},{4,6},{6,4},{8,10},{10,8},{12,14},{14,12},{16,18},{18,... | collective-permute-start | bytes 589832 | tf_op jit(solution)/shard_map/ppermute | solution.py:368
  11.9 11.8 %collective-permute-start.1 = (bf16[2,4,48,256]{3,2,1,0:T(8,128)(2,1)S(1)}, bf16[2,4,48,256]{3,2,1,0:T(8,128)(2,1)S(1)}, u32[]{:S(2)}, u32[]{:S(2)}) collective-permute-start(bf16[2,4,48,256]{3,2,1,0:T(8,128)(2,1)S(1)} %get-tuple-element.20), channel_id=1, source_target_pairs={{0,4},{2,6},{4,0},{6,2},{8,12},{10,14},{12,8},{14,10},{16,20},{18,... | collective-permute-start | bytes 589832 | tf_op jit(solution)/shard_map/ppermute | solution.py:368
  13.6 15.5 %collective-permute-start.2 = (bf16[2,4,48,256]{3,2,1,0:T(8,128)(2,1)S(1)}, bf16[2,4,48,256]{3,2,1,0:T(8,128)(2,1)S(1)}, u32[]{:S(2)}, u32[]{:S(2)}) collective-permute-start(bf16[2,4,48,256]{3,2,1,0:T(8,128)(2,1)S(1)} %get-tuple-element.21), channel_id=1, source_target_pairs={{0,6},{2,4},{4,2},{6,0},{8,14},{10,12},{12,10},{14,8},{16,22},{18,... | collective-permute-start | bytes 589832 | tf_op jit(solution)/shard_map/ppermute | solution.py:368
  15.2 0.8 copy-start.4
  29.1 1.5 %copy-start.2 = (bf16[2,4,48,256]{3,2,1,0:T(8,128)(2,1)}, bf16[2,4,48,256]{3,2,1,0:T(8,128)(2,1)S(1)}, u32[]{:S(2)}) copy-start(bf16[2,4,48,256]{3,2,1,0:T(8,128)(2,1)S(1)} %collective-permute-done.2.refs_2_.refs_3_) | copy-start | bytes 589828
  30.5 28.5 %copy-start.9 = (s32[1,2,128]{2,1,0:T(2,128)S(1)}, s32[1,2,128]{2,1,0:T(2,128)}, u32[]{:S(2)}) copy-start(s32[1,2,128]{2,1,0:T(2,128)} %param.9) | copy-start | bytes 3076
  30.5 23.5 %all-to-all-start.1 = ((bf16[16,2,48,256]{3,2,1,0:T(8,128)(2,1)}), bf16[16,2,48,256]{3,2,1,0:T(8,128)(2,1)}, u32[]{:S(2)}, u32[]{:S(2)}) async-start(bf16[16,2,48,256]{3,2,1,0:T(8,128)(2,1)} %bitcast.30), calls=%async_computation.1 | async-start | bytes 1572864 | tf_op jit(solution)/shard_map/all_to_all | solution.py:325
  35.3 28.9 %copy-start = (bf16[1,2,768,1024]{3,2,1,0:T(8,128)(2,1)S(1)}, bf16[1,2,768,1024]{3,2,1,0:T(8,128)(2,1)}, u32[]{:S(2)}) copy-start(bf16[1,2,768,1024]{3,2,1,0:T(8,128)(2,1)} %param.7) | copy-start | bytes 9437188
  35.3 1.1 copy-start.3
  36.4 0.9 copy-start.7
  37.6 0.9 copy-start.1
  54.1 25.5 %all-to-all-start.3 = ((bf16[4,8,48,256]{3,2,1,0:T(8,128)(2,1)}), bf16[4,8,48,256]{3,2,1,0:T(8,128)(2,1)}, u32[]{:S(2)}, u32[]{:S(2)}) async-start(bf16[4,8,48,256]{3,2,1,0:T(8,128)(2,1)} %copy-done.1), calls=%async_computation.3 | async-start | bytes 1572864 | tf_op jit(solution)/shard_map/all_to_all | solution.py:388
  61.4 8.0 %collective-permute-start.3 = (bf16[2,256,256]{2,1,0:T(8,128)(2,1)}, bf16[2,256,256]{2,1,0:T(8,128)(2,1)S(1)}, u32[]{:S(2)}, u32[]{:S(2)}) collective-permute-start(bf16[2,256,256]{2,1,0:T(8,128)(2,1)} %faces.1), channel_id=1, source_target_pairs={{0,1},{1,0},{2,3},{3,2},{4,5},{5,4},{6,7},{7,6},{8,9},{9,8},{10,11... | collective-permute-start | bytes 786440 | tf_op jit(solution)/shard_map/ppermute | solution.py:402
  70.3 5.0 %collective-permute-start.4 = (bf16[128,512]{1,0:T(8,128)(2,1)S(1)}, bf16[128,512]{1,0:T(8,128)(2,1)S(1)}, u32[]{:S(2)}, u32[]{:S(2)}) collective-permute-start(bf16[128,512]{1,0:T(8,128)(2,1)S(1)} %get-tuple-element.25), channel_id=1, source_target_pairs={{0,1},{1,0},{2,3},{3,2},{4,5},{5,4},{6,7},{7,6},{8,9},{9,8},{10,11... | collective-permute-start | bytes 393224 | tf_op jit(solution)/shard_map/ppermute | solution.py:418
  75.3 26.9 %copy-start.5 = (bf16[512,512]{1,0:T(8,128)(2,1)S(1)}, bf16[512,512]{1,0:T(8,128)(2,1)}, u32[]{:S(2)}) copy-start(bf16[512,512]{1,0:T(8,128)(2,1)} %copy-done.4) | copy-start | bytes 1572868
  79.6 22.6 %all-to-all-start.2 = ((bf16[16,2,48,256]{3,2,1,0:T(8,128)(2,1)}), bf16[16,2,48,256]{3,2,1,0:T(8,128)(2,1)S(1)}, u32[]{:S(2)}, u32[]{:S(2)}) async-start(bf16[16,2,48,256]{3,2,1,0:T(8,128)(2,1)} %finish.1), calls=%async_computation.2 | async-start | bytes 1572864 | tf_op jit(solution)/shard_map/all_to_all | solution.py:325

commit v5 on v4

--- a/solution.py
+++ b/solution.py
@@ -14,6 +14,7 @@
 ANY = pl.BlockSpec(memory_space=pl.ANY)
 HBM = pl.BlockSpec(memory_space=pltpu.HBM)
 TILE = 16
+TOKEN = jax.ShapeDtypeStruct((8, 128), jnp.float32)
 
 
 def tables(assign, sectors):
@@ -41,32 +42,20 @@
     return [slice(start, start + TILE) for start in range(0, rows, TILE)]
 
 
-def transform_kernel(table_ref, x_ref, *refs):
-    out_ref, held_ref, sems = refs[-3:]
+def transform_kernel(table_ref, x_ref, after_ref, out_ref):
     count, rows, width = x_ref.shape
-    copies = []
-    for index, span in enumerate(tiles(rows)):
+    for span in tiles(rows):
         tile = x_ref[:, span, :].reshape(count * TILE, width)
-        held_ref[index] = dot(table_ref[...], tile).astype(BF16).reshape(count, TILE, width)
-        for part in range(2):
-            half = slice(part * count // 2, (part + 1) * count // 2)
-            copies.append(
-                pltpu.make_async_copy(held_ref.at[index, half], out_ref.at[half, span], sems.at[index, part])
-            )
-            copies[-1].start()
-    for copy in copies:
-        copy.wait()
+        out_ref[:, span, :] = dot(table_ref[...], tile).astype(BF16).reshape(count, TILE, width)
 
 
 def transform(table, pieces, after):
-    count, rows, width = pieces.shape
+    rows = pieces.shape[1]
     if rows % TILE:
         return jnp.einsum("ks,sdr->kdr", table, pieces, preferred_element_type=F32).astype(BF16)
-    steps = rows // TILE
     return call(
-        transform_kernel, jax.ShapeDtypeStruct(pieces.shape, BF16), [VMEM, VMEM] + [ANY] * len(after), "transform", 8,
-        table, pieces, *after, out_spaces=[pltpu.HBM],
-        scratch=(pltpu.VMEM((steps, count, TILE, width), BF16), pltpu.SemaphoreType.DMA((steps, 2))),
+        transform_kernel, jax.ShapeDtypeStruct(pieces.shape, BF16), [VMEM, VMEM, ANY], "transform", 8,
+        table, pieces, after,
     )
 
 
@@ -178,7 +167,8 @@
         away_ref[part] = outward.T
 
 
-def chunk_kernel(x_ref, out_ref, sems):
+def chunk_kernel(x_ref, out_ref, token_ref, sems):
+    token_ref[...] = jnp.zeros_like(token_ref)
     local, devices = x_ref.shape[:2]
     count = sems.shape[0]
     step = devices // count
@@ -197,39 +187,12 @@
     rows = cycle // devices
     split = block.reshape(local, devices, rows, width)
     if rows % TILE or devices % 4:
-        return split.transpose(1, 0, 2, 3)
+        return split.transpose(1, 0, 2, 3), None
     out = jax.ShapeDtypeStruct((devices, local, rows, width), block.dtype)
     return call(
-        chunk_kernel, out, [HBM], "chunk", 8, split,
+        chunk_kernel, (out, TOKEN), [HBM], "chunk", 8, split,
         scratch=(pltpu.SemaphoreType.DMA((4, local)),),
     )
-
-
-GROUP = 4
-
-
-def near_kernel(me_ref, x_ref, *refs):
-    *outs, sems = refs
-    copies = []
-    for k in range(GROUP):
-        member = me_ref[0] ^ k
-        copies.append(pltpu.make_async_copy(x_ref.at[:, :, member], outs[k], sems.at[k]))
-        copies[-1].start()
-    for copy in copies:
-        copy.wait()
-
-
-def far_kernel(me_ref, *refs):
-    blocks, out_ref, sems = refs[:GROUP], refs[GROUP], refs[GROUP + 1]
-    local = blocks[0].shape[0]
-    copies = []
-    for j, block in enumerate(blocks):
-        member = me_ref[0] ^ j
-        for i in range(local):
-            copies.append(pltpu.make_async_copy(block.at[i], out_ref.at[:, member * local + i], sems.at[j, i]))
-            copies[-1].start()
-    for copy in copies:
-        copy.wait()
 
 
 def right_sides(real, imag, paired):
@@ -340,7 +303,7 @@
     scattered = scattered.reshape(1, -1)
     edges = gathered.shape[0]
 
-    pieces = exchange(by_chunk(loads, devices)).reshape(sectors, rows, width)
+    pieces = exchange(by_chunk(loads, devices)[0]).reshape(sectors, rows, width)
 
     edge, turned, outward = call(
         prepare_kernel,
@@ -351,31 +314,15 @@
     if aligned:
         wide = shape((sectors * TILE, sectors * TILE), BF16)
         forward, inverse = call(widen_kernel, (wide, wide), [VMEM, VMEM], "widen", 12, forward, inverse)
-    groups = devices // GROUP
-    by_groups = aligned and devices == groups * GROUP and groups > 1
-    place = lax.axis_index("sector")
-    member = (place % GROUP).astype(jnp.int32).reshape(1)
-    group = (place // GROUP).astype(jnp.int32).reshape(1)
-    blocks = []
-    if by_groups:
-        block = shape((local, groups, rows, width), BF16)
-        blocks = call(
-            near_kernel, [block] * GROUP, [SMEM, HBM], "near", 8,
-            member, state.reshape(local, groups, GROUP, rows, width),
-            scratch=(pltpu.SemaphoreType.DMA((GROUP,)),),
+    state, token = by_chunk(state, devices)
+    spectrum = transform(forward, pieces, token)
+    harmonic = exchange(spectrum.reshape(devices, 2, rows, width))
+    state = exchange(state).reshape(sectors, rows, width)
+    if aligned:
+        state = call(
+            stage_kernel, shape(state.shape, BF16), [HBM], "stage", 8, state,
+            scratch=(pltpu.SemaphoreType.DMA((4,)),),
         )
-        blocks = [
-            lax.ppermute(block, "sector", [(i, i ^ k) for i in range(devices)]) if k else block
-            for k, block in enumerate(blocks)
-        ]
-
-    spectrum = transform(forward, pieces, blocks[1:])
-    if by_groups:
-        state = call(
-            far_kernel, shape((groups, GROUP * local, rows, width), BF16), [SMEM] + [ANY] * GROUP, "far", 8,
-            member, *blocks, scratch=(pltpu.SemaphoreType.DMA((GROUP, local)),),
-        )
-    harmonic = exchange(spectrum.reshape(devices, 2, rows, width))
 
     if not aligned:
         harmonic = harmonic.transpose(1, 0, 2, 3).reshape(1, 2, cycle, width)
@@ -383,17 +330,6 @@
         faces_kernel, shape((2, 2 * face, width), BF16), [VMEM, HBM], "faces", 8,
         sent, harmonic, scratch=fetch_scratch(harmonic),
     )
-    if by_groups:
-        members = [[GROUP * z + i for z in range(groups)] for i in range(GROUP)]
-        state = lax.all_to_all(
-            state, "sector", split_axis=0, concat_axis=0, tiled=True, axis_index_groups=members
-        ).reshape(sectors, rows, width)
-        state = call(
-            stage_kernel, shape(state.shape, BF16), [HBM], "stage", 8, state,
-            scratch=(pltpu.SemaphoreType.DMA((4,)),),
-        )
-    else:
-        state = exchange(by_chunk(state, devices)).reshape(sectors, rows, width)
     own = call(
         own_kernel, shape((cycle, 2 * width), F32), [SMEM, VMEM, HBM], "own", 12, paired, weight, harmonic,
         scratch=fetch_scratch(harmonic),

time: 116 us -> 116 us (level)
  blocking collectives: 11.8 us -> 37.7 us
  waiting for transfers between devices: 52.7 us -> 36.8 us
  starting transfers between devices: 26.2 us -> 20 us
  local copies, waits for them, and re-layouts: 5.99 us -> 3.25 us
  Pallas kernels: 17.2 us -> 16 us
    all_to_all x1 -> x2, blocking collectives: 11.8 us -> 37.7 us  [exchange(): lax.all_to_all(pieces, 'sector', split_axis=0, concat_axis=0, tiled=True)]
    ppermute x3 -> x0, waiting for transfers between devices: 13.1 us -> none  [per_device(): lax.ppermute(block, 'sector', [(i, i ^ k) for i in range(devices)])]
    all_to_all x1 -> x0, starting transfers between devices: 4.95 us -> none  [per_device(): lax.all_to_all(state, 'sector', split_axis=0, concat_axis=0, tiled=True,...]
    all_to_all x1 -> x0, waiting for transfers between devices: 3.01 us -> none  [per_device(): lax.all_to_all(state, 'sector', split_axis=0, concat_axis=0, tiled=True,...]
    unnamed x20 -> x12, local copies, waits for them, and re-layouts: 4.42 us -> 1.68 us
    ppermute x3 -> x0, starting transfers between devices: 2.08 us -> none  [per_device(): lax.ppermute(block, 'sector', [(i, i ^ k) for i in range(devices)])]
    all_to_all x3, waiting for transfers between devices: 32.9 us -> 31.6 us  [exchange(): lax.all_to_all(pieces, 'sector', split_axis=0, concat_axis=0, tiled=True)]
    pallas_call x13 -> x12, Pallas kernels: 17.2 us -> 16 us  [call(): pl.pallas_call(kernel, out_shape=[space(out.shape, out.dtype) for out, sp...]
  transfers between devices with their start and end apart: 9 -> 5, of which waited for: 7 -> 4; matrix products, arithmetic and copies ran while one was open for 1% -> 1% of each run, Pallas kernels for 11% -> 11%
where the time goes in v5:
time: 116 us; the launch traced here: 115 us
  blocking collectives  37.7 us (33%)
  waiting for transfers between devices  36.8 us (32%)
  starting transfers between devices  20 us (17%)
  Pallas kernels  16 us (14%)
  local copies, waits for them, and re-layouts  3.25 us (3%)
    all_to_all x2, blocking collectives, exchange(): lax.all_to_all(pieces, 'sector', split_axis=0, concat_axis=0, tiled=True)  37.7 us
    all_to_all x3, waiting for transfers between devices, exchange(): lax.all_to_all(pieces, 'sector', split_axis=0, concat_axis=0, tiled=True)  31.6 us
    all_to_all x3, starting transfers between devices, exchange(): lax.all_to_all(pieces, 'sector', split_axis=0, concat_axis=0, tiled=True)  16.8 us
    pallas_call x12, Pallas kernels, call(): pl.pallas_call(kernel, out_shape=[space(out.shape, out.dtype) for out, sp...  16 us
    ppermute x1, waiting for transfers between devices, per_device(): near = lax.ppermute(faces, 'radial', [(0, 1), (1, 0)])  2.78 us
    ppermute x1, waiting for transfers between devices, per_device(): got = lax.ppermute(leaving, 'radial', [(0, 1), (1, 0)])  2.41 us
  transfers between devices with their start and end apart: 5, of which 4 were waited for; matrix products, arithmetic and copies ran while one was open for 1% of the time, Pallas kernels for 11%

profile of v5, /device:TPU:0, one launch (start us, length us, event | category | flops | bytes accessed | tf_op | source)
XLA Modules:
  0.0 115.4 jit_solution(6577483972002064727)
XLA Ops:
  0.0 2.2 %chunk.2 = (bf16[16,2,48,256]{3,2,1,0:T(8,128)(2,1)}, f32[8,128]{1,0:T(8,128)}) custom-call(bf16[2,16,48,256]{3,2,1,0:T(8,128)(2,1)} %bitcast.30), custom_call_target="tpu_custom_call" | custom-call | tf_op jit(solution)/shard_map/chunk/pallas_call | solution.py:260
  2.2 7.4 %all-to-all-start = ((bf16[16,2,48,256]{3,2,1,0:T(8,128)(2,1)}), bf16[16,2,48,256]{3,2,1,0:T(8,128)(2,1)S(1)}, u32[]{:S(2)}, u32[]{:S(2)}) async-start(bf16[16,2,48,256]{3,2,1,0:T(8,128)(2,1)} %get-tuple-element.18), calls=%async_computation | async-start | bytes 1572864 | tf_op jit(solution)/shard_map/all_to_all | solution.py:288
  10.5 1.3 %chunk.3 = (bf16[16,2,48,256]{3,2,1,0:T(8,128)(2,1)S(1)}, f32[8,128]{1,0:T(8,128)S(1)}) custom-call(bf16[2,16,48,256]{3,2,1,0:T(8,128)(2,1)} %bitcast.31), custom_call_target="tpu_custom_call" | custom-call | tf_op jit(solution)/shard_map/chunk/pallas_call | solution.py:260
  11.8 0.9 copy-done.1
  13.4 0.8 copy-done.2
  14.1 14.2 %all-to-all-done = bf16[16,2,48,256]{3,2,1,0:T(8,128)(2,1)S(1)} async-done(((bf16[16,2,48,256]{3,2,1,0:T(8,128)(2,1)}), bf16[16,2,48,256]{3,2,1,0:T(8,128)(2,1)S(1)}, u32[]{:S(2)}, u32[]{:S(2)}) %all-to-all-start) | async-done | bytes 786464 | tf_op jit(solution)/shard_map/all_to_all | solution.py:288
  28.9 25.9 %all_to_all.25.x_ref = bf16[16,2,48,256]{3,2,1,0:T(8,128)(2,1)} all-to-all(bf16[16,2,48,256]{3,2,1,0:T(8,128)(2,1)S(1)} %bitcast.22), channel_id=1, replica_groups=mesh['sector'=16,'radial'=2] {'sector'}, dimensions={0} | all-to-all | bytes 1572864 | tf_op jit(solution)/shard_map/all_to_all | solution.py:288
  54.8 4.3 %all-to-all-start.3 = ((bf16[16,2,48,256]{3,2,1,0:T(8,128)(2,1)}), bf16[16,2,48,256]{3,2,1,0:T(8,128)(2,1)}, u32[]{:S(2)}, u32[]{:S(2)}) async-start(bf16[16,2,48,256]{3,2,1,0:T(8,128)(2,1)} %copy-done.1), calls=%async_computation.3 | async-start | bytes 1572864 | tf_op jit(solution)/shard_map/all_to_all | solution.py:288
  59.2 2.4 %faces.1 = bf16[2,256,256]{2,1,0:T(8,128)(2,1)} custom-call(s32[1,256]{1,0:T(1,128)S(1)} %bitcast.29, bf16[16,2,48,256]{3,2,1,0:T(8,128)(2,1)} %all_to_all.25.x_ref), custom_call_target="tpu_custom_call" | custom-call | tf_op jit(solution)/shard_map/faces/pallas_call | solution.py:260
  61.5 1.6 %collective-permute-start = (bf16[2,256,256]{2,1,0:T(8,128)(2,1)}, bf16[2,256,256]{2,1,0:T(8,128)(2,1)S(1)}, u32[]{:S(2)}, u32[]{:S(2)}) collective-permute-start(bf16[2,256,256]{2,1,0:T(8,128)(2,1)} %faces.1), channel_id=1, source_target_pairs={{0,1},{1,0},{2,3},{3,2},{4,5},{5,4},{6,7},{7,6},{8,9},{9,8},{10,11... | collective-permute-start | bytes 786440 | tf_op jit(solution)/shard_map/ppermute | solution.py:338
  64.3 0.9 prepare.1
  65.2 2.7 %own.1.own_ref = f32[768,512]{1,0:T(8,128)S(1)} custom-call(s32[1]{0:T(128)S(6)} %convert_element_type.49.paired_ref, bf16[2,768,1024]{2,1,0:T(8,128)(2,1)S(1)} %bitcast.19, bf16[16,2,48,256]{3,2,1,0:T(8,128)(2,1)} %all_to_all.25.x_ref), custom_call_target="tpu_custom_call" | custom-call | tf_op jit(solution)/shard_map/own/pallas_call | solution.py:260
  67.9 2.8 %collective-permute-done.near_ref = bf16[2,256,256]{2,1,0:T(8,128)(2,1)S(1)} collective-permute-done((bf16[2,256,256]{2,1,0:T(8,128)(2,1)}, bf16[2,256,256]{2,1,0:T(8,128)(2,1)S(1)}, u32[]{:S(2)}, u32[]{:S(2)}) %collective-permute-start) | collective-permute-done | bytes 262176 | tf_op jit(solution)/shard_map/ppermute | solution.py:338
  70.7 0.9 middle.1
  71.5 1.6 %collective-permute-start.1 = (bf16[128,512]{1,0:T(8,128)(2,1)S(1)}, bf16[128,512]{1,0:T(8,128)(2,1)S(1)}, u32[]{:S(2)}, u32[]{:S(2)}) collective-permute-start(bf16[128,512]{1,0:T(8,128)(2,1)S(1)} %get-tuple-element.23), channel_id=1, source_target_pairs={{0,1},{1,0},{2,3},{3,2},{4,5},{5,4},{6,7},{7,6},{8,9},{9,8},{10,11... | collective-permute-start | bytes 393224 | tf_op jit(solution)/shard_map/ppermute | solution.py:354
  73.1 1.4 %back.1.back_ref = f32[768,512]{1,0:T(8,128)S(1)} custom-call(s32[1]{0:T(128)S(6)} %convert_element_type.49.paired_ref, bf16[2,768,768]{2,1,0:T(8,128)(2,1)S(1)} %get-tuple-element.16.turned_ref, bf16[768,512]{1,0:T(8,128)(2,1)S(1)} %get-tuple-element.22.middle_ref), custom_call_target="tpu_custom_call" | custom-call | tf_op jit(solution)/shard_map/back/pallas_call | solution.py:260
  74.5 2.4 %collective-permute-done.1.got_ref = bf16[128,512]{1,0:T(8,128)(2,1)S(1)} collective-permute-done((bf16[128,512]{1,0:T(8,128)(2,1)S(1)}, bf16[128,512]{1,0:T(8,128)(2,1)S(1)}, u32[]{:S(2)}, u32[]{:S(2)}) %collective-permute-start.1) | collective-permute-done | bytes 131104 | tf_op jit(solution)/shard_map/ppermute | solution.py:354
  76.9 1.2 %finish.1 = bf16[16,2,48,256]{3,2,1,0:T(8,128)(2,1)} custom-call(s32[1,128]{1,0:T(1,128)S(1)} %bitcast.28, f32[768,512]{1,0:T(8,128)S(1)} %back.1.back_ref, bf16[128,512]{1,0:T(8,128)(2,1)S(1)} %collective-permute-done.1.got_ref), custom_call_target="tpu_custom_call" | custom-call | tf_op jit(solution)/shard_map/finish/pallas_call | solution.py:260
  78.1 5.1 %all-to-all-start.2 = ((bf16[16,2,48,256]{3,2,1,0:T(8,128)(2,1)}), bf16[16,2,48,256]{3,2,1,0:T(8,128)(2,1)S(1)}, u32[]{:S(2)}, u32[]{:S(2)}) async-start(bf16[16,2,48,256]{3,2,1,0:T(8,128)(2,1)} %finish.1), calls=%async_computation.2 | async-start | bytes 1572864 | tf_op jit(solution)/shard_map/all_to_all | solution.py:288
  83.3 1.3 %stage.1.state_ref = bf16[32,48,256]{2,1,0:T(8,128)(2,1)S(1)} custom-call(bf16[32,48,256]{2,1,0:T(8,128)(2,1)} %bitcast.15.x_ref), custom_call_target="tpu_custom_call" | custom-call | tf_op jit(solution)/shard_map/stage/pallas_call | solution.py:260
  84.5 17.4 %all-to-all-done.2 = bf16[16,2,48,256]{3,2,1,0:T(8,128)(2,1)S(1)} async-done(((bf16[16,2,48,256]{3,2,1,0:T(8,128)(2,1)}), bf16[16,2,48,256]{3,2,1,0:T(8,128)(2,1)S(1)}, u32[]{:S(2)}, u32[]{:S(2)}) %all-to-all-start.2) | async-done | bytes 786464 | tf_op jit(solution)/shard_map/all_to_all | solution.py:288
  102.0 0.7 respond.1
  102.9 11.8 %all_to_all.26 = f32[16,2,48]{2,1,0:T(2,128)S(1)} all-to-all(f32[16,2,48]{2,1,0:T(2,128)S(1)} %reshape_reshape.3), channel_id=1, replica_groups=mesh['sector'=16,'radial'=2] {'sector'}, dimensions={0} | all-to-all | bytes 12288 | tf_op jit(solution)/shard_map/all_to_all | solution.py:288
  114.7 0.7 reshape.346
  (27 shorter events, 2.9 us)
Async XLA Ops:
  0.0 9.6 %copy-start.4 = (s32[16]{0:T(128)S(1)}, s32[16]{0:T(128)}, u32[]{:S(2)}) copy-start(s32[16]{0:T(128)} %param.8) | copy-start | bytes 196
  2.2 26.1 %all-to-all-start = ((bf16[16,2,48,256]{3,2,1,0:T(8,128)(2,1)}), bf16[16,2,48,256]{3,2,1,0:T(8,128)(2,1)S(1)}, u32[]{:S(2)}, u32[]{:S(2)}) async-start(bf16[16,2,48,256]{3,2,1,0:T(8,128)(2,1)} %get-tuple-element.18), calls=%async_computation | async-start | bytes 1572864 | tf_op jit(solution)/shard_map/all_to_all | solution.py:288
  11.8 0.9 copy-start.1
  13.3 0.8 copy-start.2
  28.3 30.8 %copy-start.5 = (s32[1,2,128]{2,1,0:T(2,128)S(1)}, s32[1,2,128]{2,1,0:T(2,128)}, u32[]{:S(2)}) copy-start(s32[1,2,128]{2,1,0:T(2,128)} %param.9) | copy-start | bytes 3076
  28.9 35.5 %copy-start = (bf16[1,2,768,1024]{3,2,1,0:T(8,128)(2,1)S(1)}, bf16[1,2,768,1024]{3,2,1,0:T(8,128)(2,1)}, u32[]{:S(2)}) copy-start(bf16[1,2,768,1024]{3,2,1,0:T(8,128)(2,1)} %param.7) | copy-start | bytes 9437188
  54.8 23.3 %all-to-all-start.3 = ((bf16[16,2,48,256]{3,2,1,0:T(8,128)(2,1)}), bf16[16,2,48,256]{3,2,1,0:T(8,128)(2,1)}, u32[]{:S(2)}, u32[]{:S(2)}) async-start(bf16[16,2,48,256]{3,2,1,0:T(8,128)(2,1)} %copy-done.1), calls=%async_computation.3 | async-start | bytes 1572864 | tf_op jit(solution)/shard_map/all_to_all | solution.py:288
  61.5 9.1 %collective-permute-start = (bf16[2,256,256]{2,1,0:T(8,128)(2,1)}, bf16[2,256,256]{2,1,0:T(8,128)(2,1)S(1)}, u32[]{:S(2)}, u32[]{:S(2)}) collective-permute-start(bf16[2,256,256]{2,1,0:T(8,128)(2,1)} %faces.1), channel_id=1, source_target_pairs={{0,1},{1,0},{2,3},{3,2},{4,5},{5,4},{6,7},{7,6},{8,9},{9,8},{10,11... | collective-permute-start | bytes 786440 | tf_op jit(solution)/shard_map/ppermute | solution.py:338
  71.5 5.4 %collective-permute-start.1 = (bf16[128,512]{1,0:T(8,128)(2,1)S(1)}, bf16[128,512]{1,0:T(8,128)(2,1)S(1)}, u32[]{:S(2)}, u32[]{:S(2)}) collective-permute-start(bf16[128,512]{1,0:T(8,128)(2,1)S(1)} %get-tuple-element.23), channel_id=1, source_target_pairs={{0,1},{1,0},{2,3},{3,2},{4,5},{5,4},{6,7},{7,6},{8,9},{9,8},{10,11... | collective-permute-start | bytes 393224 | tf_op jit(solution)/shard_map/ppermute | solution.py:354
  76.9 25.1 %copy-start.3 = (bf16[512,512]{1,0:T(8,128)(2,1)S(1)}, bf16[512,512]{1,0:T(8,128)(2,1)}, u32[]{:S(2)}) copy-start(bf16[512,512]{1,0:T(8,128)(2,1)} %copy-done.2) | copy-start | bytes 1572868
  78.1 23.8 %all-to-all-start.2 = ((bf16[16,2,48,256]{3,2,1,0:T(8,128)(2,1)}), bf16[16,2,48,256]{3,2,1,0:T(8,128)(2,1)S(1)}, u32[]{:S(2)}, u32[]{:S(2)}) async-start(bf16[16,2,48,256]{3,2,1,0:T(8,128)(2,1)} %finish.1), calls=%async_computation.2 | async-start | bytes 1572864 | tf_op jit(solution)/shard_map/all_to_all | solution.py:288

commit v6 on v5

--- a/solution.py
+++ b/solution.py
@@ -191,7 +191,7 @@
     out = jax.ShapeDtypeStruct((devices, local, rows, width), block.dtype)
     return call(
         chunk_kernel, (out, TOKEN), [HBM], "chunk", 8, split,
-        scratch=(pltpu.SemaphoreType.DMA((4, local)),),
+        scratch=(pltpu.SemaphoreType.DMA((1, local)),),
     )
 
 

time: 116 us -> 116 us (level)
  no operation moved by 1% of the time
where the time goes in v6:
time: 116 us; the launch traced here: 115 us
  blocking collectives  37.7 us (33%)
  waiting for transfers between devices  36.9 us (32%)
  starting transfers between devices  19.9 us (17%)
  Pallas kernels  15.7 us (14%)
  local copies, waits for them, and re-layouts  3.25 us (3%)
    all_to_all x2, blocking collectives, exchange(): lax.all_to_all(pieces, 'sector', split_axis=0, concat_axis=0, tiled=True)  37.7 us
    all_to_all x3, waiting for transfers between devices, exchange(): lax.all_to_all(pieces, 'sector', split_axis=0, concat_axis=0, tiled=True)  31.8 us
    all_to_all x3, starting transfers between devices, exchange(): lax.all_to_all(pieces, 'sector', split_axis=0, concat_axis=0, tiled=True)  16.8 us
    pallas_call x12, Pallas kernels, call(): pl.pallas_call(kernel, out_shape=[space(out.shape, out.dtype) for out, sp...  15.7 us
    ppermute x1, waiting for transfers between devices, per_device(): near = lax.ppermute(faces, 'radial', [(0, 1), (1, 0)])  2.78 us
    ppermute x1, waiting for transfers between devices, per_device(): got = lax.ppermute(leaving, 'radial', [(0, 1), (1, 0)])  2.41 us
  transfers between devices with their start and end apart: 5, of which 4 were waited for; matrix products, arithmetic and copies ran while one was open for 1% of the time, Pallas kernels for 11%

profile of v6, /device:TPU:0, one launch (start us, length us, event | category | flops | bytes accessed | tf_op | source)
XLA Modules:
  0.0 115.2 jit_solution(13183348506465574804)
XLA Ops:
  0.0 2.1 %chunk.2 = (bf16[16,2,48,256]{3,2,1,0:T(8,128)(2,1)}, f32[8,128]{1,0:T(8,128)}) custom-call(bf16[2,16,48,256]{3,2,1,0:T(8,128)(2,1)} %bitcast.30), custom_call_target="tpu_custom_call" | custom-call | tf_op jit(solution)/shard_map/chunk/pallas_call | solution.py:260
  2.1 7.4 %all-to-all-start = ((bf16[16,2,48,256]{3,2,1,0:T(8,128)(2,1)}), bf16[16,2,48,256]{3,2,1,0:T(8,128)(2,1)S(1)}, u32[]{:S(2)}, u32[]{:S(2)}) async-start(bf16[16,2,48,256]{3,2,1,0:T(8,128)(2,1)} %get-tuple-element.18), calls=%async_computation | async-start | bytes 1572864 | tf_op jit(solution)/shard_map/all_to_all | solution.py:288
  10.3 1.1 chunk.3
  11.5 0.9 copy-done.1
  13.1 0.8 copy-done.2
  13.8 14.3 %all-to-all-done = bf16[16,2,48,256]{3,2,1,0:T(8,128)(2,1)S(1)} async-done(((bf16[16,2,48,256]{3,2,1,0:T(8,128)(2,1)}), bf16[16,2,48,256]{3,2,1,0:T(8,128)(2,1)S(1)}, u32[]{:S(2)}, u32[]{:S(2)}) %all-to-all-start) | async-done | bytes 786464 | tf_op jit(solution)/shard_map/all_to_all | solution.py:288
  28.7 25.9 %all_to_all.25.x_ref = bf16[16,2,48,256]{3,2,1,0:T(8,128)(2,1)} all-to-all(bf16[16,2,48,256]{3,2,1,0:T(8,128)(2,1)S(1)} %bitcast.22), channel_id=1, replica_groups=mesh['sector'=16,'radial'=2] {'sector'}, dimensions={0} | all-to-all | bytes 1572864 | tf_op jit(solution)/shard_map/all_to_all | solution.py:288
  54.7 4.3 %all-to-all-start.3 = ((bf16[16,2,48,256]{3,2,1,0:T(8,128)(2,1)}), bf16[16,2,48,256]{3,2,1,0:T(8,128)(2,1)}, u32[]{:S(2)}, u32[]{:S(2)}) async-start(bf16[16,2,48,256]{3,2,1,0:T(8,128)(2,1)} %copy-done.1), calls=%async_computation.3 | async-start | bytes 1572864 | tf_op jit(solution)/shard_map/all_to_all | solution.py:288
  59.0 2.4 %faces.1 = bf16[2,256,256]{2,1,0:T(8,128)(2,1)} custom-call(s32[1,256]{1,0:T(1,128)S(1)} %bitcast.29, bf16[16,2,48,256]{3,2,1,0:T(8,128)(2,1)} %all_to_all.25.x_ref), custom_call_target="tpu_custom_call" | custom-call | tf_op jit(solution)/shard_map/faces/pallas_call | solution.py:260
  61.4 1.6 %collective-permute-start = (bf16[2,256,256]{2,1,0:T(8,128)(2,1)}, bf16[2,256,256]{2,1,0:T(8,128)(2,1)S(1)}, u32[]{:S(2)}, u32[]{:S(2)}) collective-permute-start(bf16[2,256,256]{2,1,0:T(8,128)(2,1)} %faces.1), channel_id=1, source_target_pairs={{0,1},{1,0},{2,3},{3,2},{4,5},{5,4},{6,7},{7,6},{8,9},{9,8},{10,11... | collective-permute-start | bytes 786440 | tf_op jit(solution)/shard_map/ppermute | solution.py:338
  64.2 0.9 prepare.1
  65.1 2.7 %own.1.own_ref = f32[768,512]{1,0:T(8,128)S(1)} custom-call(s32[1]{0:T(128)S(6)} %convert_element_type.49.paired_ref, bf16[2,768,1024]{2,1,0:T(8,128)(2,1)S(1)} %bitcast.19, bf16[16,2,48,256]{3,2,1,0:T(8,128)(2,1)} %all_to_all.25.x_ref), custom_call_target="tpu_custom_call" | custom-call | tf_op jit(solution)/shard_map/own/pallas_call | solution.py:260
  67.7 2.8 %collective-permute-done.near_ref = bf16[2,256,256]{2,1,0:T(8,128)(2,1)S(1)} collective-permute-done((bf16[2,256,256]{2,1,0:T(8,128)(2,1)}, bf16[2,256,256]{2,1,0:T(8,128)(2,1)S(1)}, u32[]{:S(2)}, u32[]{:S(2)}) %collective-permute-start) | collective-permute-done | bytes 262176 | tf_op jit(solution)/shard_map/ppermute | solution.py:338
  70.5 0.9 middle.1
  71.4 1.6 %collective-permute-start.1 = (bf16[128,512]{1,0:T(8,128)(2,1)S(1)}, bf16[128,512]{1,0:T(8,128)(2,1)S(1)}, u32[]{:S(2)}, u32[]{:S(2)}) collective-permute-start(bf16[128,512]{1,0:T(8,128)(2,1)S(1)} %get-tuple-element.23), channel_id=1, source_target_pairs={{0,1},{1,0},{2,3},{3,2},{4,5},{5,4},{6,7},{7,6},{8,9},{9,8},{10,11... | collective-permute-start | bytes 393224 | tf_op jit(solution)/shard_map/ppermute | solution.py:354
  73.0 1.4 %back.1.back_ref = f32[768,512]{1,0:T(8,128)S(1)} custom-call(s32[1]{0:T(128)S(6)} %convert_element_type.49.paired_ref, bf16[2,768,768]{2,1,0:T(8,128)(2,1)S(1)} %get-tuple-element.16.turned_ref, bf16[768,512]{1,0:T(8,128)(2,1)S(1)} %get-tuple-element.22.middle_ref), custom_call_target="tpu_custom_call" | custom-call | tf_op jit(solution)/shard_map/back/pallas_call | solution.py:260
  74.3 2.4 %collective-permute-done.1.got_ref = bf16[128,512]{1,0:T(8,128)(2,1)S(1)} collective-permute-done((bf16[128,512]{1,0:T(8,128)(2,1)S(1)}, bf16[128,512]{1,0:T(8,128)(2,1)S(1)}, u32[]{:S(2)}, u32[]{:S(2)}) %collective-permute-start.1) | collective-permute-done | bytes 131104 | tf_op jit(solution)/shard_map/ppermute | solution.py:354
  76.8 1.2 %finish.1 = bf16[16,2,48,256]{3,2,1,0:T(8,128)(2,1)} custom-call(s32[1,128]{1,0:T(1,128)S(1)} %bitcast.28, f32[768,512]{1,0:T(8,128)S(1)} %back.1.back_ref, bf16[128,512]{1,0:T(8,128)(2,1)S(1)} %collective-permute-done.1.got_ref), custom_call_target="tpu_custom_call" | custom-call | tf_op jit(solution)/shard_map/finish/pallas_call | solution.py:260
  78.0 5.1 %all-to-all-start.2 = ((bf16[16,2,48,256]{3,2,1,0:T(8,128)(2,1)}), bf16[16,2,48,256]{3,2,1,0:T(8,128)(2,1)S(1)}, u32[]{:S(2)}, u32[]{:S(2)}) async-start(bf16[16,2,48,256]{3,2,1,0:T(8,128)(2,1)} %finish.1), calls=%async_computation.2 | async-start | bytes 1572864 | tf_op jit(solution)/shard_map/all_to_all | solution.py:288
  83.1 1.3 %stage.1.state_ref = bf16[32,48,256]{2,1,0:T(8,128)(2,1)S(1)} custom-call(bf16[32,48,256]{2,1,0:T(8,128)(2,1)} %bitcast.15.x_ref), custom_call_target="tpu_custom_call" | custom-call | tf_op jit(solution)/shard_map/stage/pallas_call | solution.py:260
  84.4 17.4 %all-to-all-done.2 = bf16[16,2,48,256]{3,2,1,0:T(8,128)(2,1)S(1)} async-done(((bf16[16,2,48,256]{3,2,1,0:T(8,128)(2,1)}), bf16[16,2,48,256]{3,2,1,0:T(8,128)(2,1)S(1)}, u32[]{:S(2)}, u32[]{:S(2)}) %all-to-all-start.2) | async-done | bytes 786464 | tf_op jit(solution)/shard_map/all_to_all | solution.py:288
  101.8 0.7 respond.1
  102.8 11.8 %all_to_all.26 = f32[16,2,48]{2,1,0:T(2,128)S(1)} all-to-all(f32[16,2,48]{2,1,0:T(2,128)S(1)} %reshape_reshape.3), channel_id=1, replica_groups=mesh['sector'=16,'radial'=2] {'sector'}, dimensions={0} | all-to-all | bytes 12288 | tf_op jit(solution)/shard_map/all_to_all | solution.py:288
  114.5 0.7 reshape.346
  (27 shorter events, 2.9 us)
Async XLA Ops:
  0.0 9.5 %copy-start.4 = (s32[16]{0:T(128)S(1)}, s32[16]{0:T(128)}, u32[]{:S(2)}) copy-start(s32[16]{0:T(128)} %param.8) | copy-start | bytes 196
  2.1 26.1 %all-to-all-start = ((bf16[16,2,48,256]{3,2,1,0:T(8,128)(2,1)}), bf16[16,2,48,256]{3,2,1,0:T(8,128)(2,1)S(1)}, u32[]{:S(2)}, u32[]{:S(2)}) async-start(bf16[16,2,48,256]{3,2,1,0:T(8,128)(2,1)} %get-tuple-element.18), calls=%async_computation | async-start | bytes 1572864 | tf_op jit(solution)/shard_map/all_to_all | solution.py:288
  11.5 0.9 copy-start.1
  13.0 0.8 copy-start.2
  28.2 30.8 %copy-start.5 = (s32[1,2,128]{2,1,0:T(2,128)S(1)}, s32[1,2,128]{2,1,0:T(2,128)}, u32[]{:S(2)}) copy-start(s32[1,2,128]{2,1,0:T(2,128)} %param.9) | copy-start | bytes 3076
  28.7 35.5 %copy-start = (bf16[1,2,768,1024]{3,2,1,0:T(8,128)(2,1)S(1)}, bf16[1,2,768,1024]{3,2,1,0:T(8,128)(2,1)}, u32[]{:S(2)}) copy-start(bf16[1,2,768,1024]{3,2,1,0:T(8,128)(2,1)} %param.7) | copy-start | bytes 9437188
  54.7 23.3 %all-to-all-start.3 = ((bf16[16,2,48,256]{3,2,1,0:T(8,128)(2,1)}), bf16[16,2,48,256]{3,2,1,0:T(8,128)(2,1)}, u32[]{:S(2)}, u32[]{:S(2)}) async-start(bf16[16,2,48,256]{3,2,1,0:T(8,128)(2,1)} %copy-done.1), calls=%async_computation.3 | async-start | bytes 1572864 | tf_op jit(solution)/shard_map/all_to_all | solution.py:288
  61.4 9.1 %collective-permute-start = (bf16[2,256,256]{2,1,0:T(8,128)(2,1)}, bf16[2,256,256]{2,1,0:T(8,128)(2,1)S(1)}, u32[]{:S(2)}, u32[]{:S(2)}) collective-permute-start(bf16[2,256,256]{2,1,0:T(8,128)(2,1)} %faces.1), channel_id=1, source_target_pairs={{0,1},{1,0},{2,3},{3,2},{4,5},{5,4},{6,7},{7,6},{8,9},{9,8},{10,11... | collective-permute-start | bytes 786440 | tf_op jit(solution)/shard_map/ppermute | solution.py:338
  71.4 5.4 %collective-permute-start.1 = (bf16[128,512]{1,0:T(8,128)(2,1)S(1)}, bf16[128,512]{1,0:T(8,128)(2,1)S(1)}, u32[]{:S(2)}, u32[]{:S(2)}) collective-permute-start(bf16[128,512]{1,0:T(8,128)(2,1)S(1)} %get-tuple-element.23), channel_id=1, source_target_pairs={{0,1},{1,0},{2,3},{3,2},{4,5},{5,4},{6,7},{7,6},{8,9},{9,8},{10,11... | collective-permute-start | bytes 393224 | tf_op jit(solution)/shard_map/ppermute | solution.py:354
  76.8 25.1 %copy-start.3 = (bf16[512,512]{1,0:T(8,128)(2,1)S(1)}, bf16[512,512]{1,0:T(8,128)(2,1)}, u32[]{:S(2)}) copy-start(bf16[512,512]{1,0:T(8,128)(2,1)} %copy-done.2) | copy-start | bytes 1572868
  78.0 23.8 %all-to-all-start.2 = ((bf16[16,2,48,256]{3,2,1,0:T(8,128)(2,1)}), bf16[16,2,48,256]{3,2,1,0:T(8,128)(2,1)S(1)}, u32[]{:S(2)}, u32[]{:S(2)}) async-start(bf16[16,2,48,256]{3,2,1,0:T(8,128)(2,1)} %finish.1), calls=%async_computation.2 | async-start | bytes 1572864 | tf_op jit(solution)/shard_map/all_to_all | solution.py:288

commit v7 on v6

--- a/solution.py
+++ b/solution.py
@@ -116,8 +116,7 @@
     return pltpu.VMEM(array.shape, array.dtype), pltpu.SemaphoreType.DMA((math.gcd(array.shape[0], 8),))
 
 
-def faces_kernel(index_ref, x_ref, out_ref, held_ref, sems):
-    copies = fetch(x_ref, held_ref, sems)
+def faces_kernel(index_ref, x_ref, out_ref):
     chunks, _, rows, width = x_ref.shape
     count = index_ref.shape[1]
     square = (count, count)
@@ -125,10 +124,8 @@
     column = jnp.sum(jnp.where(diagonal, index_ref[...].astype(F32), 0.0), axis=1, keepdims=True)
     pick = column.astype(jnp.int32) == lax.broadcasted_iota(jnp.int32, (count, chunks * rows), 1)
     pick = jnp.where(pick, 1.0, 0.0).astype(BF16)
-    for copy in copies:
-        copy.wait()
     for part in range(2):
-        out_ref[part] = dot(pick, rows_of(held_ref, part)).astype(BF16)
+        out_ref[part] = dot(pick, rows_of(x_ref, part)).astype(BF16)
 
 
 def widen(table):
@@ -327,8 +324,7 @@
     if not aligned:
         harmonic = harmonic.transpose(1, 0, 2, 3).reshape(1, 2, cycle, width)
     faces = call(
-        faces_kernel, shape((2, 2 * face, width), BF16), [VMEM, HBM], "faces", 8,
-        sent, harmonic, scratch=fetch_scratch(harmonic),
+        faces_kernel, shape((2, 2 * face, width), BF16), [VMEM, VMEM], "faces", 8, sent, harmonic,
     )
     own = call(
         own_kernel, shape((cycle, 2 * width), F32), [SMEM, VMEM, HBM], "own", 12, paired, weight, harmonic,

time: 116 us -> 116 us (level)
  Pallas kernels: 15.7 us -> 14.5 us
    pallas_call x12, Pallas kernels: 15.7 us -> 14.5 us  [call(): pl.pallas_call(kernel, out_shape=[space(out.shape, out.dtype) for out, sp...]
    unnamed x12 -> x14, local copies, waits for them, and re-layouts: 1.68 us -> 2.83 us
  transfers between devices with their start and end apart: 5 -> 5, of which waited for: 4 -> 4; matrix products, arithmetic and copies ran while one was open for 1% -> 1% of each run, Pallas kernels for 11% -> 10%
where the time goes in v7:
time: 116 us; the launch traced here: 115 us
  blocking collectives  37.7 us (33%)
  waiting for transfers between devices  37 us (32%)
  starting transfers between devices  20 us (17%)
  Pallas kernels  14.5 us (12%)
  local copies, waits for them, and re-layouts  4.4 us (4%)
    all_to_all x2, blocking collectives, exchange(): lax.all_to_all(pieces, 'sector', split_axis=0, concat_axis=0, tiled=True)  37.7 us
    all_to_all x3, waiting for transfers between devices, exchange(): lax.all_to_all(pieces, 'sector', split_axis=0, concat_axis=0, tiled=True)  31.7 us
    all_to_all x3, starting transfers between devices, exchange(): lax.all_to_all(pieces, 'sector', split_axis=0, concat_axis=0, tiled=True)  16.9 us
    pallas_call x12, Pallas kernels, call(): pl.pallas_call(kernel, out_shape=[space(out.shape, out.dtype) for out, sp...  14.5 us
    unnamed x14, local copies, waits for them, and re-layouts  2.83 us
    ppermute x1, waiting for transfers between devices, per_device(): near = lax.ppermute(faces, 'radial', [(0, 1), (1, 0)])  2.8 us
    ppermute x1, waiting for transfers between devices, per_device(): got = lax.ppermute(leaving, 'radial', [(0, 1), (1, 0)])  2.43 us
  transfers between devices with their start and end apart: 5, of which 4 were waited for; matrix products, arithmetic and copies ran while one was open for 1% of the time, Pallas kernels for 10%

profile of v7, /device:TPU:0, one launch (start us, length us, event | category | flops | bytes accessed | tf_op | source)
XLA Modules:
  0.0 115.2 jit_solution(13830781016987069346)
XLA Ops:
  0.0 2.1 %chunk.2 = (bf16[16,2,48,256]{3,2,1,0:T(8,128)(2,1)}, f32[8,128]{1,0:T(8,128)}) custom-call(bf16[2,16,48,256]{3,2,1,0:T(8,128)(2,1)} %bitcast.30), custom_call_target="tpu_custom_call" | custom-call | tf_op jit(solution)/shard_map/chunk/pallas_call | solution.py:257
  2.1 7.4 %all-to-all-start = ((bf16[16,2,48,256]{3,2,1,0:T(8,128)(2,1)}), bf16[16,2,48,256]{3,2,1,0:T(8,128)(2,1)S(1)}, u32[]{:S(2)}, u32[]{:S(2)}) async-start(bf16[16,2,48,256]{3,2,1,0:T(8,128)(2,1)} %get-tuple-element.18), calls=%async_computation | async-start | bytes 1572864 | tf_op jit(solution)/shard_map/all_to_all | solution.py:285
  10.3 1.1 chunk.3
  11.5 0.9 copy-done.2
  13.1 0.8 copy-done.3
  13.9 14.3 %all-to-all-done = bf16[16,2,48,256]{3,2,1,0:T(8,128)(2,1)S(1)} async-done(((bf16[16,2,48,256]{3,2,1,0:T(8,128)(2,1)}), bf16[16,2,48,256]{3,2,1,0:T(8,128)(2,1)S(1)}, u32[]{:S(2)}, u32[]{:S(2)}) %all-to-all-start) | async-done | bytes 786464 | tf_op jit(solution)/shard_map/all_to_all | solution.py:285
  28.7 25.9 %all_to_all.25.x_ref = bf16[16,2,48,256]{3,2,1,0:T(8,128)(2,1)} all-to-all(bf16[16,2,48,256]{3,2,1,0:T(8,128)(2,1)S(1)} %bitcast.22), channel_id=1, replica_groups=mesh['sector'=16,'radial'=2] {'sector'}, dimensions={0} | all-to-all | bytes 1572864 | tf_op jit(solution)/shard_map/all_to_all | solution.py:285
  54.7 4.3 %all-to-all-start.3 = ((bf16[16,2,48,256]{3,2,1,0:T(8,128)(2,1)}), bf16[16,2,48,256]{3,2,1,0:T(8,128)(2,1)}, u32[]{:S(2)}, u32[]{:S(2)}) async-start(bf16[16,2,48,256]{3,2,1,0:T(8,128)(2,1)} %copy-done.2), calls=%async_computation.3 | async-start | bytes 1572864 | tf_op jit(solution)/shard_map/all_to_all | solution.py:285
  59.0 1.1 copy-done.1
  60.1 1.2 %faces.1 = bf16[2,256,256]{2,1,0:T(8,128)(2,1)} custom-call(s32[1,256]{1,0:T(1,128)S(1)} %bitcast.29, bf16[16,2,48,256]{3,2,1,0:T(8,128)(2,1)S(1)} %copy-done.1), custom_call_target="tpu_custom_call" | custom-call | tf_op jit(solution)/shard_map/faces/pallas_call | solution.py:257
  61.3 1.5 %collective-permute-start = (bf16[2,256,256]{2,1,0:T(8,128)(2,1)}, bf16[2,256,256]{2,1,0:T(8,128)(2,1)S(1)}, u32[]{:S(2)}, u32[]{:S(2)}) collective-permute-start(bf16[2,256,256]{2,1,0:T(8,128)(2,1)} %faces.1), channel_id=1, source_target_pairs={{0,1},{1,0},{2,3},{3,2},{4,5},{5,4},{6,7},{7,6},{8,9},{9,8},{10,11... | collective-permute-start | bytes 786440 | tf_op jit(solution)/shard_map/ppermute | solution.py:334
  64.1 0.8 prepare.1
  64.9 2.7 %own.1.own_ref = f32[768,512]{1,0:T(8,128)S(1)} custom-call(s32[1]{0:T(128)S(6)} %convert_element_type.49.paired_ref, bf16[2,768,1024]{2,1,0:T(8,128)(2,1)S(1)} %bitcast.19, bf16[16,2,48,256]{3,2,1,0:T(8,128)(2,1)} %all_to_all.25.x_ref), custom_call_target="tpu_custom_call" | custom-call | tf_op jit(solution)/shard_map/own/pallas_call | solution.py:257
  67.6 2.8 %collective-permute-done.near_ref = bf16[2,256,256]{2,1,0:T(8,128)(2,1)S(1)} collective-permute-done((bf16[2,256,256]{2,1,0:T(8,128)(2,1)}, bf16[2,256,256]{2,1,0:T(8,128)(2,1)S(1)}, u32[]{:S(2)}, u32[]{:S(2)}) %collective-permute-start) | collective-permute-done | bytes 262176 | tf_op jit(solution)/shard_map/ppermute | solution.py:334
  70.4 0.9 middle.1
  71.3 1.6 %collective-permute-start.1 = (bf16[128,512]{1,0:T(8,128)(2,1)S(1)}, bf16[128,512]{1,0:T(8,128)(2,1)S(1)}, u32[]{:S(2)}, u32[]{:S(2)}) collective-permute-start(bf16[128,512]{1,0:T(8,128)(2,1)S(1)} %get-tuple-element.23), channel_id=1, source_target_pairs={{0,1},{1,0},{2,3},{3,2},{4,5},{5,4},{6,7},{7,6},{8,9},{9,8},{10,11... | collective-permute-start | bytes 393224 | tf_op jit(solution)/shard_map/ppermute | solution.py:350
  72.8 1.4 %back.1.back_ref = f32[768,512]{1,0:T(8,128)S(1)} custom-call(s32[1]{0:T(128)S(6)} %convert_element_type.49.paired_ref, bf16[2,768,768]{2,1,0:T(8,128)(2,1)S(1)} %get-tuple-element.16.turned_ref, bf16[768,512]{1,0:T(8,128)(2,1)S(1)} %get-tuple-element.22.middle_ref), custom_call_target="tpu_custom_call" | custom-call | tf_op jit(solution)/shard_map/back/pallas_call | solution.py:257
  74.2 2.4 %collective-permute-done.1.got_ref = bf16[128,512]{1,0:T(8,128)(2,1)S(1)} collective-permute-done((bf16[128,512]{1,0:T(8,128)(2,1)S(1)}, bf16[128,512]{1,0:T(8,128)(2,1)S(1)}, u32[]{:S(2)}, u32[]{:S(2)}) %collective-permute-start.1) | collective-permute-done | bytes 131104 | tf_op jit(solution)/shard_map/ppermute | solution.py:350
  76.6 1.2 %finish.1 = bf16[16,2,48,256]{3,2,1,0:T(8,128)(2,1)} custom-call(s32[1,128]{1,0:T(1,128)S(1)} %bitcast.28, f32[768,512]{1,0:T(8,128)S(1)} %back.1.back_ref, bf16[128,512]{1,0:T(8,128)(2,1)S(1)} %collective-permute-done.1.got_ref), custom_call_target="tpu_custom_call" | custom-call | tf_op jit(solution)/shard_map/finish/pallas_call | solution.py:257
  77.9 5.2 %all-to-all-start.2 = ((bf16[16,2,48,256]{3,2,1,0:T(8,128)(2,1)}), bf16[16,2,48,256]{3,2,1,0:T(8,128)(2,1)S(1)}, u32[]{:S(2)}, u32[]{:S(2)}) async-start(bf16[16,2,48,256]{3,2,1,0:T(8,128)(2,1)} %finish.1), calls=%async_computation.2 | async-start | bytes 1572864 | tf_op jit(solution)/shard_map/all_to_all | solution.py:285
  83.1 1.3 %stage.1.state_ref = bf16[32,48,256]{2,1,0:T(8,128)(2,1)S(1)} custom-call(bf16[32,48,256]{2,1,0:T(8,128)(2,1)} %bitcast.15.x_ref), custom_call_target="tpu_custom_call" | custom-call | tf_op jit(solution)/shard_map/stage/pallas_call | solution.py:257
  84.4 17.4 %all-to-all-done.2 = bf16[16,2,48,256]{3,2,1,0:T(8,128)(2,1)S(1)} async-done(((bf16[16,2,48,256]{3,2,1,0:T(8,128)(2,1)}), bf16[16,2,48,256]{3,2,1,0:T(8,128)(2,1)S(1)}, u32[]{:S(2)}, u32[]{:S(2)}) %all-to-all-start.2) | async-done | bytes 786464 | tf_op jit(solution)/shard_map/all_to_all | solution.py:285
  101.8 0.7 respond.1
  102.7 11.8 %all_to_all.26 = f32[16,2,48]{2,1,0:T(2,128)S(1)} all-to-all(f32[16,2,48]{2,1,0:T(2,128)S(1)} %reshape_reshape.3), channel_id=1, replica_groups=mesh['sector'=16,'radial'=2] {'sector'}, dimensions={0} | all-to-all | bytes 12288 | tf_op jit(solution)/shard_map/all_to_all | solution.py:285
  (29 shorter events, 3.6 us)
Async XLA Ops:
  0.0 9.5 %copy-start.5 = (s32[16]{0:T(128)S(1)}, s32[16]{0:T(128)}, u32[]{:S(2)}) copy-start(s32[16]{0:T(128)} %param.8) | copy-start | bytes 196
  2.1 26.1 %all-to-all-start = ((bf16[16,2,48,256]{3,2,1,0:T(8,128)(2,1)}), bf16[16,2,48,256]{3,2,1,0:T(8,128)(2,1)S(1)}, u32[]{:S(2)}, u32[]{:S(2)}) async-start(bf16[16,2,48,256]{3,2,1,0:T(8,128)(2,1)} %get-tuple-element.18), calls=%async_computation | async-start | bytes 1572864 | tf_op jit(solution)/shard_map/all_to_all | solution.py:285
  11.5 0.9 copy-start.2
  13.0 0.8 copy-start.3
  28.2 30.8 %copy-start.6 = (s32[1,2,128]{2,1,0:T(2,128)S(1)}, s32[1,2,128]{2,1,0:T(2,128)}, u32[]{:S(2)}) copy-start(s32[1,2,128]{2,1,0:T(2,128)} %param.9) | copy-start | bytes 3076
  28.7 35.3 %copy-start = (bf16[1,2,768,1024]{3,2,1,0:T(8,128)(2,1)S(1)}, bf16[1,2,768,1024]{3,2,1,0:T(8,128)(2,1)}, u32[]{:S(2)}) copy-start(bf16[1,2,768,1024]{3,2,1,0:T(8,128)(2,1)} %param.7) | copy-start | bytes 9437188
  54.7 23.2 %all-to-all-start.3 = ((bf16[16,2,48,256]{3,2,1,0:T(8,128)(2,1)}), bf16[16,2,48,256]{3,2,1,0:T(8,128)(2,1)}, u32[]{:S(2)}, u32[]{:S(2)}) async-start(bf16[16,2,48,256]{3,2,1,0:T(8,128)(2,1)} %copy-done.2), calls=%async_computation.3 | async-start | bytes 1572864 | tf_op jit(solution)/shard_map/all_to_all | solution.py:285
  59.0 1.1 copy-start.1
  61.3 9.1 %collective-permute-start = (bf16[2,256,256]{2,1,0:T(8,128)(2,1)}, bf16[2,256,256]{2,1,0:T(8,128)(2,1)S(1)}, u32[]{:S(2)}, u32[]{:S(2)}) collective-permute-start(bf16[2,256,256]{2,1,0:T(8,128)(2,1)} %faces.1), channel_id=1, source_target_pairs={{0,1},{1,0},{2,3},{3,2},{4,5},{5,4},{6,7},{7,6},{8,9},{9,8},{10,11... | collective-permute-start | bytes 786440 | tf_op jit(solution)/shard_map/ppermute | solution.py:334
  71.3 5.4 %collective-permute-start.1 = (bf16[128,512]{1,0:T(8,128)(2,1)S(1)}, bf16[128,512]{1,0:T(8,128)(2,1)S(1)}, u32[]{:S(2)}, u32[]{:S(2)}) collective-permute-start(bf16[128,512]{1,0:T(8,128)(2,1)S(1)} %get-tuple-element.23), channel_id=1, source_target_pairs={{0,1},{1,0},{2,3},{3,2},{4,5},{5,4},{6,7},{7,6},{8,9},{9,8},{10,11... | collective-permute-start | bytes 393224 | tf_op jit(solution)/shard_map/ppermute | solution.py:350
  76.6 25.2 %copy-start.4 = (bf16[512,512]{1,0:T(8,128)(2,1)S(1)}, bf16[512,512]{1,0:T(8,128)(2,1)}, u32[]{:S(2)}) copy-start(bf16[512,512]{1,0:T(8,128)(2,1)} %copy-done.3) | copy-start | bytes 1572868
  77.9 23.9 %all-to-all-start.2 = ((bf16[16,2,48,256]{3,2,1,0:T(8,128)(2,1)}), bf16[16,2,48,256]{3,2,1,0:T(8,128)(2,1)S(1)}, u32[]{:S(2)}, u32[]{:S(2)}) async-start(bf16[16,2,48,256]{3,2,1,0:T(8,128)(2,1)} %finish.1), calls=%async_computation.2 | async-start | bytes 1572864 | tf_op jit(solution)/shard_map/all_to_all | solution.py:285
